TPU v7x, 32 devices: a whole 2x2x4 slice. The times are simulated.
32 devices in a mesh: dp: 2 (over y), row: 4 (over x, core), col: 4 (over z).
Axes of the slice: x: 2, y: 2, z: 4, core: 2. Of those that a mesh axis runs over, the one named last changes fastest.
Arguments:
- tokens: bfloat16 [8192, 768], P(('dp', 'col', 'row')), may hold values from -6 to 6
- cotangent: bfloat16 [8192, 768], P(('dp', 'col', 'row')), may hold values from -6 to 6
- lengths: int32 [2], P('dp'), may hold values from 1024 to 4096, as said below
- query_weight: float32 [768, 768], P(('row', 'col')), may hold values from -0.21875 to 0.21875
- key_weight: float32 [768, 768], P(('row', 'col')), may hold values from -0.21875 to 0.21875
- value_weight: float32 [768, 768], P(('row', 'col')), may hold values from -0.21875 to 0.21875
- query_bias: float32 [768], P('col'), may hold values from -3 to 3
- value_bias: float32 [768], P('col'), may hold values from -0.1875 to 0.1875
- out_weight: float32 [768, 768], P(('col', 'row')), may hold values from -6 to 6
- out_bias: float32 [768], P('row'), may hold values from -1.75 to 1.75
- norm1_gain: float32 [768], P('row'), may hold values from 0.5 to 1.5
- norm1_shift: float32 [768], P('row'), may hold values from -1.75 to 1.75
- up_weight: float32 [768, 3072], P('row', 'col'), may hold values from -0.21875 to 0.21875
- up_bias: float32 [3072], P('col'), may hold values from -3 to 3
- down_weight: float32 [3072, 768], P(('col', 'row')), may hold values from -0.109375 to 0.109375
- down_bias: float32 [768], P('row'), may hold values from -1.75 to 1.75
- norm2_gain: float32 [768], P('row'), may hold values from 0.5 to 1.5
- norm2_shift: float32 [768], P('row'), may hold values from -1.75 to 1.75
Outputs:
- output: bfloat16 [8192, 768], P(('dp', 'col', 'row'))
- grad_tokens: float32 [8192, 768], P(('dp', 'col', 'row'))
- grad_query_weight: float32 [768, 768], P(('row', 'col'))
- grad_key_weight: float32 [768, 768], P(('row', 'col'))
- grad_value_weight: float32 [768, 768], P(('row', 'col'))
- grad_query_bias: float32 [768], P('col')
- grad_value_bias: float32 [768], P('col')
- grad_out_weight: float32 [768, 768], P(('col', 'row'))
- grad_out_bias: float32 [768], P('row')
- grad_norm1_gain: float32 [768], P('row')
- grad_norm1_shift: float32 [768], P('row')
- grad_up_weight: float32 [768, 3072], P('row', 'col')
- grad_up_bias: float32 [3072], P('col')
- grad_down_weight: float32 [3072, 768], P(('col', 'row'))
- grad_down_bias: float32 [768], P('row')
- grad_norm2_gain: float32 [768], P('row')
- grad_norm2_shift: float32 [768], P('row')
Inputs may be any that keep to these rules, and one draw needn't show every extreme that they name: `lengths`: one sequence is exactly 4096 long.
All inputs are finite; a program needn't handle non-finite values.
Results may differ from a plain program's by a relative error of at most 0.024.
Values may be sent and summed in bfloat16 or wider, within the bound.
No kernel may reach another device: no remote copies, remote signals or barrier semaphores. Data moves between devices by JAX's collectives and lax.ppermute only.
A program may use at most 256 MiB of HBM per device.

v0:
```python
import functools
import math

import jax
import jax.numpy as jnp
from jax import lax
from jax.experimental import pallas as pl
from jax.experimental.pallas import tpu as pltpu
from jax.sharding import PartitionSpec as P

HD = 64
LANES = 256
EPS = 1e-05
BF = jnp.bfloat16
F32 = jnp.float32
VMEM_BYTES = 60 * 1024 * 1024
TURNED = HD + 16
SMALL_BYTES = 24 * 1024 * 1024
ATTN_BYTES = 36 * 1024 * 1024
NEAR_COST = 4
C4 = 6


def nn(a, b):
    return jnp.dot(a, b, preferred_element_type=F32)


def tn(a, b):
    return lax.dot_general(a, b, (((0,), (0,)), ((), ())), preferred_element_type=F32)


def nt(a, b):
    return lax.dot_general(a, b, (((1,), (1,)), ((), ())), preferred_element_type=F32)


def cost(us):
    return pl.CostEstimate(flops=int(us * 0.6e9), bytes_accessed=1000, transcendentals=0)


def head_lanes(shape, head, width):
    lane = lax.broadcasted_iota(jnp.int32, shape, 1)
    mine = (lane >= head * HD) & (lane < (head + 1) * HD)
    return mine | (lane == width) | ((lane >= width + 1 + 3 * head) & (lane < width + 4 + 3 * head))


def three_parts(x):
    hi = x.astype(BF).astype(F32)
    mid = (x - hi).astype(BF).astype(F32)
    return hi, mid, x - hi - mid


def tail_rows(parts, ones, n):
    row = lax.broadcasted_iota(jnp.int32, (n, parts[0].shape[1]), 0)
    out = jnp.where(row == 0, ones, 0.0)
    for head, value in enumerate(parts):
        for i, piece in enumerate(three_parts(value)):
            out = jnp.where(row == 1 + 3 * head + i, piece, out)
    return out


def widen_keys(kv, owner, base, meta, keys_out, values_out, turned, at, width, shift, sizes):
    n = kv.shape[0]
    rows_n, cols_n = sizes
    keys_out[at : at + n, :width] = kv[:, :width]
    values_out[at : at + n, :width] = kv[:, width:]
    shape = (n, LANES - width)
    t = lax.broadcasted_iota(jnp.int32, shape, 0) + base
    lane = lax.broadcasted_iota(jnp.int32, shape, 1)
    source = meta[3] - (t >> shift)
    source = jnp.where(source < 0, source + cols_n, source)
    position = ((source * rows_n + owner) << shift) + (t & ((1 << shift) - 1))
    mask = jnp.where(lane == 0, jnp.where(position >= meta[0], -1e30, 0.0), 1.0)
    keys_out[at : at + n, width:] = mask.astype(BF)
    values_out[at : at + n, width:] = jnp.ones(shape, BF)
    flat = values_out[at : at + n, :].T
    for head in range(width // HD):
        first = head * TURNED
        turned[first : first + HD, at : at + n] = flat[head * HD : (head + 1) * HD, :]
        turned[first + HD : first + TURNED, at : at + n] = jnp.ones((TURNED - HD, n), BF)


def attn_fwd_kernel(*refs, heads, first, pair, shift, sizes, chunk, blocks, parts):
    meta, *refs = refs
    q_refs, refs = refs[:parts], refs[parts:]
    kvs, refs = refs[: 2 * parts], refs[2 * parts :]
    if first:
        acc_out, stat_out, k_out, v_out, turned = refs
    else:
        acc_in, stat_in = refs[:2]
        outs = refs[2 : 2 + blocks]
        qb_ref, k_out, v_out, turned = refs[2 + blocks :]
    width = heads * HD
    keys = k_out.shape[0]
    at = 0
    for i, ref in enumerate(kvs):
        base = at % (keys // 2)
        owner = meta[1] ^ pair[i // parts]
        widen_keys(ref[...], owner, base, meta, k_out, v_out, turned, at, width, shift, sizes)
        at += ref.shape[0]
    q = jnp.concatenate([ref[...] for ref in q_refs], axis=0)
    rows = q.shape[0]
    slot = lax.broadcasted_iota(jnp.int32, (16, rows), 0)
    stat = jnp.zeros((16, rows), F32)
    logs = []
    for head in range(heads):
        qh = jnp.where(head_lanes(q.shape, head, width), q, jnp.zeros_like(q))
        scores = [nt(k_out[i : i + chunk, :], qh) for i in range(0, keys, chunk)]
        peak = functools.reduce(
            jnp.maximum, [jnp.max(s, axis=0, keepdims=True) for s in scores]
        )
        if not first:
            old = stat_in[head : head + 1, :]
            peak = jnp.maximum(peak, old)
        acc = None
        for i, s in enumerate(scores):
            p = jnp.exp(s - peak).astype(BF)
            at = head * TURNED
            part = nn(turned[at : at + TURNED, i * chunk : (i + 1) * chunk], p)
            acc = part if acc is None else acc + part
        total = acc[HD : HD + 1]
        mine = slice(head * HD, (head + 1) * HD)
        if first:
            acc_out[mine, :] = acc[:HD]
            stat = jnp.where(slot == head, peak, stat)
            stat = jnp.where(slot == head + 8, total, stat)
        else:
            keep = jnp.exp(old - peak)
            total = total + stat_in[head + 8 : head + 9, :] * keep
            out = ((acc[:HD] + acc_in[mine, :] * keep) * (1.0 / total)).astype(BF)
            each = rows // blocks
            for b in range(blocks):
                outs[b][mine, :] = out[:, b * each : (b + 1) * each]
            logs.append(-(peak + jnp.log(total)))
    if first:
        stat_out[...] = stat
    else:
        qb_ref[:, :width] = q[:, :width]
        qb_ref[:, width:] = tail_rows(logs, 1.0, LANES - width).T.astype(BF)


def attn_fwd(meta, q, kvs, pair, heads, local, sizes, us, state=None, chunk=512):
    rows = sum(part.shape[0] for part in q)
    half = sum(kv.shape[0] for kv in kvs) // 2
    width = kvs[0].shape[1] // 2
    first = state is None
    blocks = rows // local
    vmem = pl.BlockSpec(memory_space=pltpu.VMEM)
    args = [meta, *q, *kvs]
    if first:
        out_shape = [jax.ShapeDtypeStruct((width, rows), F32), jax.ShapeDtypeStruct((16, rows), F32)]
    else:
        args += list(state)
        out_shape = [jax.ShapeDtypeStruct((width, local), BF)] * blocks
        out_shape += [jax.ShapeDtypeStruct((rows, LANES), BF)]
    out_shape += [jax.ShapeDtypeStruct((2 * half, LANES), BF)] * 2
    return pl.pallas_call(
        functools.partial(
            attn_fwd_kernel,
            heads=heads,
            first=first,
            pair=pair,
            shift=local.bit_length() - 1,
            sizes=sizes,
            chunk=chunk,
            blocks=blocks,
            parts=len(q),
        ),
        in_specs=[pl.BlockSpec(memory_space=pltpu.SMEM)] + [vmem] * (len(args) - 1),
        out_specs=[vmem] * len(out_shape),
        out_shape=out_shape,
        scratch_shapes=[pltpu.VMEM((heads * TURNED, 2 * half), BF)],
        compiler_params=pltpu.CompilerParams(vmem_limit_bytes=ATTN_BYTES),
        cost_estimate=cost(us),
        name="attn_fwd_near" if first else "attn_fwd_far",
    )(*args)


def grad_rows_kernel(*refs, heads, blocks):
    outs, grads, wide = refs[:blocks], refs[blocks : 2 * blocks], refs[2 * blocks]
    width = heads * HD
    for b in range(blocks):
        g = grads[b][...].astype(F32)
        prod = g * outs[b][...].astype(F32)
        each = g.shape[1]
        parts = [
            -jnp.sum(prod[head * HD : (head + 1) * HD], axis=0, keepdims=True) for head in range(heads)
        ]
        tall = jnp.concatenate([g, tail_rows(parts, 0.0, LANES - width)], axis=0)
        wide[b * each : (b + 1) * each, :] = tall.T.astype(BF)


def grad_rows(outs, grads, heads):
    each = outs[0].shape[1]
    return small_call(
        functools.partial(grad_rows_kernel, heads=heads, blocks=len(outs)),
        jax.ShapeDtypeStruct((each * len(outs), LANES), BF),
        "grad_rows",
    )(*outs, *grads)


def attn_bwd_kernel(at_ref, q_ref, g_ref, k_ref, v_ref, dq_in, *refs, heads, block, pieces):
    outs, (dq_out, dk, dv) = refs[:pieces], refs[pieces:]
    width = heads * HD
    half = dk.shape[0]
    keys = pl.ds(pl.multiple_of(at_ref[0] * half, half), half)
    dk[...] = jnp.zeros_like(dk)
    dv[...] = jnp.zeros_like(dv)

    def step(i, carry):
        at = pl.ds(pl.multiple_of(i * block, block), block)
        q_all = q_ref[at, :]
        g_all = g_ref[at, :]
        k = k_ref[keys, :]
        dq = jnp.zeros((block, LANES), F32)
        for head in range(heads):
            mine = head_lanes((block, LANES), head, width)
            q = jnp.where(mine, q_all, jnp.zeros_like(q_all))
            g = jnp.where(mine, g_all, jnp.zeros_like(g_all))
            p = jnp.exp(nt(k, q))
            ds = (p * nt(v_ref[keys, :], g)).astype(BF)
            dv[...] += nn(p.astype(BF), g)
            dk[...] += nn(ds, q)
            dq = jnp.where(mine, tn(ds, k), dq)
        dq_out[at, :] = dq_in[at, :] + dq
        return carry

    lax.fori_loop(0, q_ref.shape[0] // block, step, 0)
    each = outs[0].shape[0]
    for i, out in enumerate(outs):
        at = slice(i * each, (i + 1) * each)
        out[:, :width] = dk[at, :width].astype(out.dtype)
        out[:, width:] = dv[at, :width].astype(out.dtype)


def attn_bwd(at, q, g, k, v, dq, heads, us, pieces=2, block=512):
    rows = q.shape[0]
    half = k.shape[0] // 2
    width = heads * HD
    vmem = pl.BlockSpec(memory_space=pltpu.VMEM)
    out_shape = [jax.ShapeDtypeStruct((half // pieces, 2 * width), BF)] * pieces
    return pl.pallas_call(
        functools.partial(attn_bwd_kernel, heads=heads, block=block, pieces=pieces),
        in_specs=[pl.BlockSpec(memory_space=pltpu.SMEM)] + [vmem] * 5,
        out_specs=[vmem] * (pieces + 1),
        out_shape=out_shape + [jax.ShapeDtypeStruct((rows, LANES), F32)],
        scratch_shapes=[pltpu.VMEM((half, LANES), F32)] * 2,
        compiler_params=pltpu.CompilerParams(vmem_limit_bytes=ATTN_BYTES),
        cost_estimate=cost(us),
        name="attn_bwd",
    )(jnp.full((1,), at, jnp.int32), q, g, k, v, dq)


def small_call(kernel, out_shape, name, scratch=(), us=1.4):
    return pl.pallas_call(
        kernel,
        out_shape=out_shape,
        scratch_shapes=scratch,
        compiler_params=pltpu.CompilerParams(vmem_limit_bytes=SMALL_BYTES),
        cost_estimate=cost(us),
        name=name,
    )


def meta_call(kernel, args, out_shape, name, scratch=(), us=1.2):
    vmem = pl.BlockSpec(memory_space=pltpu.VMEM)
    return pl.pallas_call(
        kernel,
        in_specs=[pl.BlockSpec(memory_space=pltpu.SMEM)] + [vmem] * (len(args) - 1),
        out_specs=[vmem] * len(out_shape),
        out_shape=out_shape,
        scratch_shapes=scratch,
        compiler_params=pltpu.CompilerParams(vmem_limit_bytes=SMALL_BYTES),
        cost_estimate=cost(us),
        name=name,
    )(*args)


def row_mean(x):
    return jnp.mean(x, axis=1, keepdims=True)


def col_sum(x):
    return jnp.sum(x, axis=0, keepdims=True)


def norm_forward(resid, gain, shift):
    centered = resid - row_mean(resid)
    inv = lax.rsqrt(row_mean(centered * centered) + EPS)
    normal = centered * inv
    return normal * gain + shift, normal, inv


def norm_backward(grad_out, normal, inv, gain):
    scaled = grad_out * gain
    return inv * (scaled - row_mean(scaled) - normal * row_mean(scaled * normal))


def project_qkv_kernel(meta, *refs, n, blocks, last, rows_n, cols_n, feat, hw, scale):
    x, ws, bias_ref = refs[:n], refs[n : n + rows_n], refs[n + rows_n]
    if last:
        vec_ref, q_ref, kv_ref, w_out, pack_ref, w_all = refs[n + rows_n + 1 :]
    else:
        q_ref, kv_ref, w_all = refs[n + rows_n + 1 :]
    each = feat // cols_n
    for k in range(rows_n):
        for m in range(cols_n):
            source = meta[3] - m
            source = jnp.where(source < 0, source + cols_n, source)
            at = pl.multiple_of((meta[1] ^ k) * feat + source * each, each)
            w_all[pl.ds(at, each), :] = ws[k][m * each : (m + 1) * each, :]
    w = w_all[...]
    each = q_ref.shape[0] // len(blocks)
    for i, k in enumerate(blocks):
        at = slice(i * each, (i + 1) * each)
        out = nn(x[k][:each, :], w) + bias_ref[0:1, :]
        q_ref[at, :hw] = (out[:, :hw].astype(BF).astype(F32) * scale).astype(BF)
        lane = lax.broadcasted_iota(jnp.int32, (each, LANES - hw), 1)
        q_ref[at, hw:] = jnp.where(lane == 0, 1.0, 0.0).astype(BF)
        kv_ref[at, :] = out[:, hw:].astype(BF)
    if last:
        w_out[...] = w.T
        more = x[0].shape[0] - each
        for k in range(n):
            pack_ref[k * more : (k + 1) * more, :] = x[k][each:, :]
        pack_ref[n * more :, :] = vec_ref[...]


def project_qkv(meta, x, blocks, cols_n, ws, bias, local, scale, vecs=None):
    feat, wide = ws[0].shape
    hw = wide // 3
    rows = local * len(blocks)
    shapes = [
        jax.ShapeDtypeStruct((rows, LANES), BF),
        jax.ShapeDtypeStruct((rows, 2 * hw), BF),
    ]
    args = [meta, *x, *ws, bias]
    if vecs is not None:
        args.append(vecs)
        more = (x[0].shape[0] - local) * len(x) + vecs.shape[0]
        shapes.append(jax.ShapeDtypeStruct((wide, feat * len(ws)), BF))
        shapes.append(jax.ShapeDtypeStruct((more, vecs.shape[1]), BF))
    return meta_call(
        functools.partial(
            project_qkv_kernel,
            n=len(x),
            blocks=blocks,
            last=vecs is not None,
            rows_n=len(ws),
            cols_n=cols_n,
            feat=feat,
            hw=hw,
            scale=scale,
        ),
        args,
        shapes,
        "project_qkv",
        scratch=[pltpu.VMEM((feat * len(ws), wide), BF)],
    )


def project_kernel(meta, *refs, n, rows_n, sub, feat):
    mixed, packs = refs[:n], refs[n : n + rows_n]
    x_ref, hid_ref, low_ref, normal_ref, inv_ref, w_ref, vec_ref = refs[n + rows_n :]
    r = meta[1]
    for k in range(rows_n):
        at = pl.multiple_of((r ^ k) * sub, sub)
        for i in range(n):
            w_ref[i, pl.ds(at, sub), :] = packs[k][((n - i) % n) * sub : ((n - i) % n + 1) * sub, :]
    values = []
    for k in range(rows_n):
        part = packs[k][n * sub : n * sub + 32, :feat].astype(F32)
        values.append(part[0:8] + part[8:16] + part[16:24])
    pieces = []
    for owner in range(rows_n):
        value = values[0]
        for k in range(1, rows_n):
            value = jnp.where((r ^ k) == owner, values[k], value)
        pieces.append(value)
    vecs = jnp.concatenate(pieces, axis=1)
    vec_ref[...] = vecs
    total = x_ref[...].astype(F32) + vecs[0:1, :]
    for j in range(n):
        total = total + tn(mixed[j][...], w_ref[j])
    hidden, normal, inv = norm_forward(total, vecs[1:2, :], vecs[2:3, :])
    hid_ref[...] = hidden
    low_ref[...] = hidden.astype(BF)
    normal_ref[...] = normal
    inv_ref[...] = jnp.broadcast_to(inv, inv_ref.shape)


def project(meta, mixed, packs, x, sub):
    rows, width = x.shape
    feat = width // len(packs)
    return meta_call(
        functools.partial(
            project_kernel, n=len(mixed), rows_n=len(packs), sub=sub, feat=feat
        ),
        [meta, *mixed, *packs, x],
        [
            jax.ShapeDtypeStruct((rows, width), F32),
            jax.ShapeDtypeStruct((rows, width), BF),
            jax.ShapeDtypeStruct((rows, width), F32),
            jax.ShapeDtypeStruct((rows, 128), F32),
            jax.ShapeDtypeStruct((len(mixed), sub * len(packs), width), BF),
            jax.ShapeDtypeStruct((8, width), F32),
        ],
        "project_norm1",
    )


def weight_rows(meta, packs, units, down):
    size = packs[0].shape[0] // 2
    at = size if down else 0
    values = [packs[0][at : at + units, :]]
    rest = packs[1:]
    if rest[0].shape[0] > size:
        return values + [ref[at : at + units, :] for ref in rest]
    mine = (meta[4] == 0) != down
    for own, other in zip(rest[::2], rest[1::2]):
        values.append(jnp.where(mine, own[:units, :].astype(F32), other[:units, :].astype(F32)).astype(BF))
    return values


def bias_rows(meta, packs, units):
    size = packs[0].shape[0] // 2
    at = slice(units, units + 16)
    values = [packs[0][at, :].astype(F32)]
    rest = packs[1:]
    if rest[0].shape[0] > size:
        values += [ref[at, :].astype(F32) for ref in rest]
    else:
        for own, other in zip(rest[::2], rest[1::2]):
            values.append(jnp.where(meta[4] == 0, own[at, :].astype(F32), other[at, :].astype(F32)))
    return jnp.concatenate([v[0:1, :units] + v[1:2, :units] + v[2:3, :units] for v in values], axis=1)


def ffn_fwd_kernel(meta, *refs, n, units):
    h0, h1 = refs[:2]
    packs = refs[2 : 2 + n]
    keep_ref, send_ref, act_ref, slope_ref = refs[2 + n :]
    rows = h0.shape[0]
    h = jnp.concatenate([h0[...], h1[...]], axis=0)
    up = jnp.concatenate(weight_rows(meta, packs, units, False), axis=0)
    x = nt(h, up) + bias_rows(meta, packs, units)
    cdf = 0.5 * (1.0 + lax.erf(x * math.sqrt(0.5)))
    act = (x * cdf).astype(BF)
    act_ref[...] = act
    slope = cdf + x * (math.sqrt(0.5 / math.pi) * jnp.exp(-0.5 * x * x))
    slope_ref[...] = slope.astype(BF)
    out = nn(act, jnp.concatenate(weight_rows(meta, packs, units, True), axis=0))
    keep_ref[...] = out[:rows]
    send_ref[...] = out[rows:].astype(BF)


def ffn_fwd(meta, h0, h1, packs, units, wide):
    rows, width = h0.shape
    return meta_call(
        functools.partial(ffn_fwd_kernel, n=len(packs), units=units),
        [meta, h0, h1, *packs],
        [
            jax.ShapeDtypeStruct((rows, width), F32),
            jax.ShapeDtypeStruct((rows, width), BF),
            jax.ShapeDtypeStruct((2 * rows, wide), BF),
            jax.ShapeDtypeStruct((2 * rows, wide), BF),
        ],
        "ffn_fwd",
        us=1.4,
    )


def ffn_bwd_kernel(meta, *refs, n, units):
    g0, g1 = refs[:2]
    packs = refs[2 : 2 + n]
    slope_ref, keep_ref, send_ref, pre_ref = refs[2 + n :]
    rows = g0.shape[0]
    g = jnp.concatenate([g0[...], g1[...]], axis=0)
    down = jnp.concatenate(weight_rows(meta, packs, units, True), axis=0)
    pre = (nt(g, down) * slope_ref[...].astype(F32)).astype(BF)
    pre_ref[...] = pre
    out = nn(pre, jnp.concatenate(weight_rows(meta, packs, units, False), axis=0))
    keep_ref[...] = out[:rows]
    send_ref[...] = out[rows:].astype(BF)


def ffn_bwd(meta, g0, g1, packs, slope, units):
    rows, width = g0.shape
    return meta_call(
        functools.partial(ffn_bwd_kernel, n=len(packs), units=units),
        [meta, g0, g1, *packs, slope],
        [
            jax.ShapeDtypeStruct((rows, width), F32),
            jax.ShapeDtypeStruct((rows, width), BF),
            jax.ShapeDtypeStruct(slope.shape, BF),
        ],
        "ffn_bwd",
        us=1.4,
    )


def ffn_grads_kernel(meta, *refs):
    act0, act1, pre0, pre1 = refs[:4]
    h = jnp.concatenate([ref[...] for ref in refs[4:8]], axis=0)
    g = jnp.concatenate([ref[...] for ref in refs[8:12]], axis=0)
    keep_ref, send_ref, bias_ref = refs[12:]
    pre = jnp.concatenate([pre0[...], pre1[...]], axis=0)
    act = jnp.concatenate([act0[...], act1[...]], axis=0)
    g_up = tn(pre, h).astype(BF)
    g_down = tn(act, g).astype(BF)
    first = meta[4] == 0

    @pl.when(first)
    def _():
        keep_ref[...] = g_up
        send_ref[...] = g_down

    @pl.when(jnp.logical_not(first))
    def _():
        keep_ref[...] = g_down
        send_ref[...] = g_up

    bias_ref[...] = jnp.broadcast_to(col_sum(pre.astype(F32)), bias_ref.shape)


def ffn_grads(meta, acts, pres, hiddens, grads):
    width = hiddens[0].shape[1]
    wide = acts[0].shape[1]
    return meta_call(
        ffn_grads_kernel,
        [meta, *acts, *pres, *hiddens, *grads],
        [
            jax.ShapeDtypeStruct((wide, width), BF),
            jax.ShapeDtypeStruct((wide, width), BF),
            jax.ShapeDtypeStruct((8, wide), F32),
        ],
        "ffn_grads",
    )


def norm2_kernel(
    meta, hid_ref, keep_ref, near_ref, far_ref, cot_ref, vec_ref, out_ref, grad_ref, low_ref, sum_ref
):
    branch = keep_ref[...] + near_ref[...].astype(F32) + far_ref[...].astype(F32) + vec_ref[3:4, :]
    gain = vec_ref[4:5, :]
    normed, normal, inv = norm_forward(hid_ref[...] + branch, gain, vec_ref[5:6, :])
    row = lax.broadcasted_iota(jnp.int32, (out_ref.shape[0], 1), 0)
    valid = (meta[2] + row < meta[0]).astype(F32)
    out_ref[...] = (normed * valid).astype(BF)
    grad_y = cot_ref[...].astype(F32) * valid
    grad = norm_backward(grad_y, normal, inv, gain)
    grad_ref[...] = grad
    low = grad.astype(BF)
    low_ref[...] = low
    sum_ref[...] = jnp.zeros_like(sum_ref)
    sum_ref[0:1, :] = col_sum(grad_y * normal)
    sum_ref[1:2, :] = col_sum(grad_y)
    sum_ref[2:3, :] = col_sum(low.astype(F32))


def norm2(meta, hidden, keep, near, far, cot, vecs):
    rows, width = hidden.shape
    shapes = [
        jax.ShapeDtypeStruct((rows, width), BF),
        jax.ShapeDtypeStruct((rows, width), F32),
        jax.ShapeDtypeStruct((rows, width), BF),
        jax.ShapeDtypeStruct((8, width), F32),
    ]
    return meta_call(norm2_kernel, [meta, hidden, keep, near, far, cot, vecs], shapes, "norm2_both")


def norm1_back_kernel(
    keep_ref, near_ref, far_ref, add_ref, normal_ref, inv_ref, vec_ref, w_ref, out_ref, low_ref, sum_ref, *mixed
):
    grad = keep_ref[...] + near_ref[...].astype(F32) + far_ref[...].astype(F32) + add_ref[...]
    normal = normal_ref[...]
    resid = norm_backward(grad, normal, inv_ref[:, 0:1], vec_ref[1:2, :])
    out_ref[...] = resid
    low = resid.astype(BF)
    low_ref[...] = low
    for j, ref in enumerate(mixed):
        ref[...] = nt(w_ref[j], low).astype(BF)
    sum_ref[...] = jnp.zeros_like(sum_ref)
    sum_ref[0:1, :] = col_sum(grad * normal)
    sum_ref[1:2, :] = col_sum(grad)
    sum_ref[2:3, :] = col_sum(low.astype(F32))


def norm1_back(keep, near, far, add, normal, inv, vecs, w):
    rows, width = add.shape
    out = small_call(
        norm1_back_kernel,
        [
            jax.ShapeDtypeStruct((rows, width), F32),
            jax.ShapeDtypeStruct((rows, width), BF),
            jax.ShapeDtypeStruct((8, width), F32),
        ]
        + [jax.ShapeDtypeStruct((w.shape[1], rows), BF)] * w.shape[0],
        "norm1_back",
    )(keep, near, far, add, normal, inv, vecs, w)
    return out[0], out[1], out[2], out[3:]


def two_parts(x):
    hi = x.astype(BF).astype(F32)
    return jnp.concatenate([hi, x - hi], axis=0).astype(BF)


def both_parts(rows):
    n = rows.shape[0] // 2
    return rows[:n].astype(F32) + rows[n:].astype(F32)


def out_grads_kernel(meta, *refs, n, rows_n, sub):
    mixed, grad, s1, s2, bias = refs[:n], *refs[n : n + 4]
    keep, far, send, sums, total = refs[n + 4 :]
    g = grad[...]
    for j in range(n):
        total[j] = nn(mixed[j][...], g)
    count = n * sub
    for j in range(n):
        at = slice(j * sub, (j + 1) * sub)

        def rows(k):
            return total[j, pl.ds(pl.multiple_of((meta[1] ^ k) * sub, sub), sub), :]

        keep[at, :] = rows(0)
        far[at, :] = rows(2)
        send[at, :] = rows(1).astype(BF)
        send[count + j * sub : count + (j + 1) * sub, :] = rows(3).astype(BF)
    sums[...] = jnp.zeros_like(sums)
    sums[0:3, :] = s1[0:3, :]
    sums[3:6, :] = s2[0:3, :]
    units = bias.shape[1] // n
    for j in range(n):
        away = meta[3] - j
        away = jnp.where(away < 0, away + n, away)
        value = bias[0:1, :units]
        for k in range(1, n):
            value = jnp.where(away == k, bias[0:1, k * units : (k + 1) * units], value)
        zero = jnp.zeros_like(value)
        row = [jnp.where(meta[1] == owner, value, zero) for owner in range(rows_n)]
        sums[8 + j : 9 + j, :] = jnp.concatenate(row, axis=1)
    send[2 * count :, :] = two_parts(sums[...])


def out_grads(meta, mixed, grad, s1, s2, bias, sub, rows_n):
    n, heads, width = len(mixed), mixed[0].shape[0], grad.shape[1]
    shapes = [
        jax.ShapeDtypeStruct((n * sub, width), F32),
        jax.ShapeDtypeStruct((n * sub, width), F32),
        jax.ShapeDtypeStruct((2 * n * sub + 32, width), BF),
        jax.ShapeDtypeStruct((16, width), F32),
    ]
    return meta_call(
        functools.partial(out_grads_kernel, n=n, sub=sub, rows_n=rows_n),
        [meta, *mixed, grad, s1, s2, bias],
        shapes,
        "out_grads",
        scratch=[pltpu.VMEM((n, heads, width), F32)],
    )


def far_message_kernel(far, sums, got, out):
    n = far.shape[0]
    out[:n, :] = (far[...] + got[n : 2 * n, :].astype(F32)).astype(BF)
    out[n:, :] = two_parts(sums[...] + both_parts(got[2 * n :, :]))


def far_message(far, sums, got):
    n, width = far.shape
    shape = jax.ShapeDtypeStruct((n + 32, width), BF)
    return small_call(far_message_kernel, shape, "far_message", us=0.7)(far, sums, got)


def col_messages_kernel(*refs, n, sub, added):
    (one, two, keep, sums, near, far), outs = refs[:6], refs[6:]
    count = n * sub
    both = sums[...] + both_parts(near[2 * count :, :]) + both_parts(far[count:, :])
    parts = two_parts(both)
    own = keep[...] + near[:count, :].astype(F32) + far[:count, :].astype(F32)
    units = one.shape[0] // n
    size = units if added else 2 * units
    for k in range(n):
        j = (n - k) % n
        at = slice(k * units, (k + 1) * units)
        if added:
            outs[k][:units, :] = (one[at, :].astype(F32) + two[at, :].astype(F32)).astype(BF)
        else:
            outs[k][:units, :] = one[at, :]
            outs[k][units:size, :] = two[at, :]
        outs[k][size : size + sub, :] = own[j * sub : (j + 1) * sub].astype(BF)
        outs[k][size + sub :, :] = parts


def col_messages(one, two, keep, sums, near, far, sub, n, added):
    rows, width = one.shape
    size = rows // n * (1 if added else 2)
    shapes = [jax.ShapeDtypeStruct((size + sub + 32, width), BF)] * n
    return small_call(
        functools.partial(col_messages_kernel, n=n, sub=sub, added=added), shapes, "col_messages"
    )(one, two, keep, sums, near, far)


def sum_messages_kernel(*refs):
    refs, out = refs[:-1], refs[-1]
    n = out.shape[0] - 32
    total = refs[0][:n, :].astype(F32)
    sums = both_parts(refs[0][n:, :])
    for ref in refs[1:]:
        total = total + ref[:n, :].astype(F32)
        sums = sums + both_parts(ref[n:, :])
    out[:n, :] = total.astype(BF)
    out[n:, :] = two_parts(sums)


def sum_messages(messages):
    shape = jax.ShapeDtypeStruct(messages[0].shape, BF)
    return small_call(sum_messages_kernel, shape, "sum_messages", us=0.7)(*messages)


def finish_kernel(meta, own, other, *refs, rows_n, units, sub, paired):
    ups, (down, out, sums) = refs[:rows_n], refs[rows_n:]
    size = own.shape[0] - sub - 32
    a = own[:size, :].astype(F32)
    b = other[:size, :].astype(F32)
    if paired:
        first = meta[4] == 0
        up = jnp.where(first, a, b)
        down[...] = jnp.where(first, b, a)
    else:
        up = a[:units] + b[:units]
        down[...] = a[units:] + b[units:]
    feat = up.shape[1] // rows_n
    pieces = [up[:, k * feat : (k + 1) * feat] for k in range(rows_n)]
    for k in range(rows_n):
        value = pieces[0]
        for owner in range(1, rows_n):
            value = jnp.where((meta[1] ^ k) == owner, pieces[owner], value)
        ups[k][...] = value.T.astype(BF)
    at = size + sub
    out[...] = own[size:at, :].astype(F32) + other[size:at, :].astype(F32)
    sums[...] = both_parts(own[at:, :]) + both_parts(other[at:, :])


def finish(meta, own, other, rows_n, units, sub, paired):
    width = own.shape[1]
    shapes = [jax.ShapeDtypeStruct((width // rows_n, units), BF)] * rows_n
    shapes += [jax.ShapeDtypeStruct((n, width), F32) for n in (units, sub, 16)]
    return meta_call(
        functools.partial(finish_kernel, rows_n=rows_n, units=units, sub=sub, paired=paired),
        [meta, own, other],
        shapes,
        "finish_grads",
    )


def up_grads_kernel(meta, *refs, n):
    pieces, out = refs[:n], refs[n]
    units = pieces[0].shape[1]
    values = [ref[...].astype(F32) for ref in pieces]
    for owner in range(n):
        value = values[0]
        for k in range(1, n):
            value = jnp.where((meta[1] ^ k) == owner, values[k], value)
        out[:, owner * units : (owner + 1) * units] = value


def up_grads(meta, pieces):
    feat, units = pieces[0].shape
    return meta_call(
        functools.partial(up_grads_kernel, n=len(pieces)),
        [meta, *pieces],
        [jax.ShapeDtypeStruct((feat, units * len(pieces)), F32)],
        "up_grads",
    )[0]


def join_kernel(keep0, keep1, near0, near1, far, dq, w_ref, *outs, scale, hw):
    n = len(outs) // 2
    each = outs[0].shape[0]
    half = keep0.shape[0]
    for k in range(n):
        at = slice(k * each, (k + 1) * each)
        inside = slice(at.start % half, at.start % half + each)
        keep, near = ((keep0, near0), (keep1, near1))[at.start // half]
        kv = keep[inside, :].astype(F32) + near[inside, :].astype(F32) + far[at, :].astype(F32)
        d = jnp.concatenate([(dq[at, :hw] * scale).astype(BF), kv.astype(BF)], axis=1)
        outs[k][...] = d
        outs[n + k][...] = nn(d, w_ref[...]).astype(outs[n + k].dtype)


def join_grads(keep, near, far, dq, w, n, scale):
    rows = dq.shape[0]
    wide, width = w.shape
    shapes = [jax.ShapeDtypeStruct((rows // n, wide), BF)] * n
    shapes += [jax.ShapeDtypeStruct((rows // n, width), BF if k == 1 else F32) for k in range(n)]
    kernel = functools.partial(join_kernel, scale=scale, hw=wide // 3)
    out = small_call(kernel, shapes, "join_grads")(*keep, *near, far, dq, w)
    return out[:n], out[n:]


def qkv_grads_kernel(meta, *refs, n, feat):
    x, grads, keep, far, send, send_far, total = refs[:n], refs[n : 2 * n], *refs[2 * n :]
    each = grads[0].shape[0]
    rows_of_x = jnp.concatenate([ref[:each, :] for ref in x], axis=0)
    g = jnp.concatenate([ref[...] for ref in grads], axis=0)
    total[...] = tn(rows_of_x, g)

    def rows(k):
        return total[pl.ds(pl.multiple_of((meta[1] ^ k) * feat, feat), feat), :]

    bias = col_sum(g.astype(F32))
    hi = bias.astype(BF).astype(F32)
    row = lax.broadcasted_iota(jnp.int32, (16, bias.shape[1]), 0)
    tail = jnp.where(row == 0, hi, jnp.where(row == 1, bias - hi, 0.0))
    keep[:feat, :] = rows(0)
    keep[feat:, :] = tail
    far[...] = rows(2)
    send[:feat, :] = rows(1).astype(BF)
    send[feat:, :] = tail.astype(BF)
    send_far[...] = rows(3).astype(BF)


def qkv_grads(meta, x, grads, feat):
    wide = grads[0].shape[1]
    width = x[0].shape[1]
    return meta_call(
        functools.partial(qkv_grads_kernel, n=len(x), feat=feat),
        [meta, *x, *grads],
        [
            jax.ShapeDtypeStruct((feat + 16, wide), F32),
            jax.ShapeDtypeStruct((feat, wide), F32),
            jax.ShapeDtypeStruct((feat + 16, wide), BF),
            jax.ShapeDtypeStruct((feat, wide), BF),
        ],
        "qkv_grads",
        scratch=[pltpu.VMEM((width, wide), F32)],
    )


def spread_kernel(meta, *refs, n):
    pieces, outs = refs[:n], refs[n:]
    hw = pieces[0].shape[1] // 3
    values = [ref[...].astype(F32) for ref in pieces]
    for j in range(n):
        away = meta[3] - j
        away = jnp.where(away < 0, away + n, away)
        value = values[0]
        for k in range(1, n):
            value = jnp.where(away == k, values[k], value)
        for i, out in enumerate(outs):
            out[:, j * hw : (j + 1) * hw] = value[:, i * hw : (i + 1) * hw]


def spread(meta, pieces):
    sub, wide = pieces[0].shape
    width = wide // 3 * len(pieces)
    return meta_call(
        functools.partial(spread_kernel, n=len(pieces)),
        [meta, *pieces],
        [jax.ShapeDtypeStruct((sub, width), F32)] * 3,
        "spread",
    )


def pack_kernel(meta, *refs, n):
    blocks, (down, bias, out, half) = refs[:n], refs[n:]
    units, feat = blocks[0].shape
    size = out.shape[0] // 2
    values = [ref[...].astype(F32) for ref in blocks]
    for owner in range(n):
        value = values[0]
        for k in range(1, n):
            value = jnp.where((meta[1] ^ k) == owner, values[k], value)
        out[:units, owner * feat : (owner + 1) * feat] = value.astype(BF)
    out[units:size, :] = bias[...]
    out[size : size + units, :] = down[...].astype(BF)
    out[size + units :, :] = jnp.zeros((size - units, out.shape[1]), BF)

    @pl.when(meta[4] == 0)
    def _():
        half[...] = out[:size, :]

    @pl.when(meta[4] != 0)
    def _():
        half[...] = out[size:, :]


def pack_weights(meta, blocks, down, bias):
    rows, width = down.shape
    size = rows + bias.shape[0]
    return meta_call(
        functools.partial(pack_kernel, n=len(blocks)),
        [meta, *blocks, down, bias],
        [jax.ShapeDtypeStruct((2 * size, width), BF), jax.ShapeDtypeStruct((size, width), BF)],
        "pack_weights",
    )


CORE = [(0, 1), (1, 0), (2, 3), (3, 2)]
CROSS = [(0, 2), (2, 0), (1, 3), (3, 1)]


def core_swap(x):
    return lax.ppermute(x, "row", CORE)


def cross_swap(x):
    return lax.ppermute(x, "row", CROSS)


def shift_col(x, step):
    n = lax.axis_size("col")
    return lax.ppermute(x, "col", [(i, (i + step) % n) for i in range(n)])


def after(x, *others):
    return lax.optimization_barrier((x,) + others)[0]


def natural_row(blocks):
    r = lax.axis_index("row")
    low = (r & 1) == 0
    b0, b1, b2, b3 = blocks
    left = jnp.where(low, jnp.stack([b0, b1]), jnp.stack([b1, b0]))
    right = jnp.where(low, jnp.stack([b2, b3]), jnp.stack([b3, b2]))
    return jnp.where(r < 2, jnp.concatenate([left, right]), jnp.concatenate([right, left]))


def gather_row_rel(x):
    far = cross_swap(x)
    near = core_swap(x)
    return [x, near, far, core_swap(far)]


def sum_dp(x):
    n = lax.axis_size("dp")
    if n == 2:
        return x + lax.ppermute(x, "dp", [(0, 1), (1, 0)])
    return lax.psum(x, "dp")


def split3(x):
    hi = lax.reduce_precision(x, 8, 7)
    mid = lax.reduce_precision(x - hi, 8, 7)
    low = x - hi - mid
    return hi.astype(BF), mid.astype(BF), low.astype(BF)


def per_device(
    tokens,
    cotangent,
    lengths,
    query_weight,
    key_weight,
    value_weight,
    query_bias,
    value_bias,
    out_weight,
    out_bias,
    norm1_gain,
    norm1_shift,
    up_weight,
    up_bias,
    down_weight,
    down_bias,
    norm2_gain,
    norm2_shift,
):
    rows_n = lax.axis_size("row")
    cols_n = lax.axis_size("col")
    r = lax.axis_index("row")
    z = lax.axis_index("col")
    local, width = tokens.shape
    block_len = local * cols_n
    hw = width // cols_n
    heads = hw // HD
    feat = width // rows_n
    scale = 1.0 / math.sqrt(HD)
    paired = lax.axis_size("dp") == 2
    pair = lax.axis_index("dp") if paired else jnp.zeros((), jnp.int32)
    meta = jnp.stack([lengths[0], r, z * (local * rows_n) + r * local, z, pair]).astype(jnp.int32)

    sub_out = out_weight.shape[0]
    x_blocks = [jnp.concatenate([tokens, out_weight.astype(BF)])]
    x_blocks.append(shift_col(x_blocks[0], 1))

    up_t = up_weight.astype(BF).T
    units = up_t.shape[0] // rows_n
    up_t = up_t.reshape(rows_n, units, feat)
    pieces = [lax.dynamic_index_in_dim(up_t, r ^ k, 0, keepdims=False) for k in range(4)]
    up_blocks = [
        pieces[0],
        core_swap(pieces[1]),
        cross_swap(pieces[2]),
        lax.ppermute(pieces[3], "row", [(i, i ^ 3) for i in range(rows_n)]),
    ]

    qkv = jnp.stack([query_weight, key_weight, value_weight], axis=1).astype(BF)
    sub = qkv.shape[0]
    qkv = qkv.reshape(sub, 3, cols_n, hw).transpose(2, 0, 1, 3).reshape(cols_n, sub, 3 * hw)
    pieces = []
    for k in range(cols_n):
        piece = lax.dynamic_index_in_dim(qkv, (z + k) % cols_n, 0, keepdims=False)
        pieces.append(shift_col(piece, k) if k else piece)
    second, *pieces = lax.optimization_barrier((x_blocks[1], *pieces))
    x_blocks.append(shift_col(second, 1))
    w_blocks = gather_row_rel(jnp.concatenate(pieces))
    for _ in range(3, cols_n):
        x_blocks.append(shift_col(x_blocks[-1], 1))

    bias_mine = lax.dynamic_slice_in_dim(up_bias, r * units, units, 0)
    bias_rows = jnp.pad(jnp.stack(split3(bias_mine)), ((0, 13), (0, width - units)))
    def cross_dp(x):
        return lax.ppermute(x, "dp", [(0, 1), (1, 0)]) if paired else x[:1]

    pack, half = pack_weights(meta, up_blocks, down_weight, bias_rows)
    hops = [shift_col(after(half if paired else pack, x_blocks[-1]), 1)]

    qkv_bias = jnp.concatenate([query_bias, jnp.zeros_like(value_bias), value_bias])
    qkv_bias = jnp.broadcast_to(qkv_bias[None], (8, 3 * hw))
    vecs = jnp.stack([out_bias, norm1_gain, norm1_shift, down_bias, norm2_gain, norm2_shift])
    vecs = jnp.pad(jnp.stack(split3(vecs)), ((0, 1), (0, 2), (0, width - feat))).reshape(32, width)
    early, late = (0, 1), tuple(range(2, cols_n))
    q_a, kv_a = project_qkv(meta, x_blocks[:2], early, cols_n, w_blocks, qkv_bias, local, scale)
    far_a, near_a = cross_swap(kv_a), core_swap(kv_a)
    x_blocks[-1], near_a, pack = lax.optimization_barrier((x_blocks[-1], near_a, pack))
    q_b, kv_b, w_qkv, out_pack = project_qkv(
        meta, x_blocks, late, cols_n, w_blocks, qkv_bias, local, scale, vecs
    )
    far_b, near_b = cross_swap(kv_b), core_swap(kv_b)
    near_b, far_a = lax.optimization_barrier((near_b, far_a))
    sizes = (rows_n, cols_n)
    q_parts = [q_a, q_b]
    acc, stat, k_near, v_near = attn_fwd(
        meta, q_parts, [kv_a, kv_b, near_a, near_b], (0, 1), heads, local, sizes, NEAR_COST
    )
    stat, hops[0] = lax.optimization_barrier((stat, hops[0]))
    hops.append(shift_col(hops[0], 1))
    crossed = [cross_dp(hops[0])]
    stat, far_a, far_b, out_pack = lax.optimization_barrier((stat, far_a, far_b, out_pack))
    out_far, out_near = cross_swap(out_pack), core_swap(out_pack)
    state = (acc, stat)
    far = [far_a, far_b, core_swap(far_a), core_swap(far_b)]
    *mixed_part, qb_rows, k_far, v_far = attn_fwd(
        meta, q_parts, far, (2, 3), heads, local, sizes, 4, state=state
    )
    *mixed_part, second, third, out_far, qb_rows = lax.optimization_barrier(
        (*mixed_part, hops[1], crossed[0], out_far, qb_rows)
    )
    hops[1], crossed[0] = second, third
    crossed.append(cross_dp(hops[1]))
    mixed = [mixed_part[0]] + [shift_col(mixed_part[k], -k) for k in range(1, cols_n)]

    out_packs = [out_pack, out_near, out_far, core_swap(out_far)]
    *mixed, third, crossed[1] = lax.optimization_barrier((*mixed, hops[1], crossed[1]))
    hops.append(shift_col(third, 1))
    crossed.append(cross_dp(hops[2]))
    packs = [pack]
    for hop, other in zip(hops, crossed):
        packs += [hop, other] if paired else [hop]
    hidden, hidden_low, normal1, inv1, out_full, vecs = project(meta, mixed, out_packs, tokens, sub_out)

    h_own, h_far, h_near = hidden_low, cross_swap(hidden_low), core_swap(hidden_low)
    h_near, h_far, packs[-1] = lax.optimization_barrier((h_near, h_far, packs[-1]))
    h_diag = core_swap(h_far)
    keep0, send0, act0, slope0 = ffn_fwd(meta, h_own, h_near, packs, units, units * cols_n)
    keep1, send1, act1, slope1 = ffn_fwd(meta, h_far, h_diag, packs, units, units * cols_n)
    far = (keep1 + core_swap(send1).astype(F32)).astype(BF)
    got_far = cross_swap(far)
    got_near = core_swap(send0)
    output, grad_resid2, grad_branch, sums2 = norm2(
        meta, hidden, keep0, got_near, got_far, cotangent, vecs
    )

    g_own, g_far, g_near = grad_branch, cross_swap(grad_branch), core_swap(grad_branch)
    keep0, send0, pre0 = ffn_bwd(meta, g_own, g_near, packs, slope0, units)
    g_far = after(g_far, send0)
    g_diag = core_swap(g_far)
    keep1, send1, pre1 = ffn_bwd(meta, g_far, g_diag, packs, slope1, units)
    far = (keep1 + core_swap(send1).astype(F32)).astype(BF)
    got_far = cross_swap(far)
    got_near = core_swap(send0)
    g_one, g_two, g_up_bias = ffn_grads(
        meta,
        (act0, act1),
        (pre0, pre1),
        (h_own, h_near, h_far, h_diag),
        (g_own, g_near, g_far, g_diag),
    )
    if paired:
        g_two = lax.ppermute(g_two, "dp", [(0, 1), (1, 0)])
    keep0 = after(keep0, g_one)
    grad_resid1, grad_attended, sums1, grad_mixed = norm1_back(
        keep0, got_near, got_far, grad_resid2, normal1, inv1, vecs, out_full
    )
    grad_mixed = [grad_mixed[0]] + [shift_col(grad_mixed[k], k) for k in range(1, cols_n)]

    out_keep, out_far, out_send, sums = out_grads(
        meta, mixed, grad_attended, sums1, sums2, g_up_bias, sub_out, rows_n
    )
    out_got = core_swap(out_send)
    out_got = after(out_got, grad_mixed[1])
    out_message = far_message(out_far, sums, out_got)
    out_got_far = cross_swap(out_message)
    messages = col_messages(
        g_one, g_two, out_keep, sums, out_got, out_got_far, sub_out, cols_n, paired
    )

    grads = after(grad_rows(mixed_part, grad_mixed, heads), out_message)
    dq = jnp.zeros((block_len, LANES), F32)
    *part3, dq = attn_bwd(1, qb_rows, grads, k_far, v_far, dq, heads, 4)
    got3 = [core_swap(part) for part in part3]
    dq = after(dq, messages[1])
    packed = shift_col(after(messages[1], dq), 1)
    *part2, dq = attn_bwd(0, qb_rows, grads, k_far, v_far, dq, heads, 4)
    far_sum = [(a.astype(F32) + b.astype(F32)).astype(BF) for a, b in zip(part2, got3)]
    far_sum = jnp.concatenate(far_sum)
    far_got = cross_swap(far_sum)
    packed = sum_messages([messages[2], packed])
    dq = after(dq, far_sum, packed)
    packed = shift_col(after(packed, dq), 1)
    *part1, dq = attn_bwd(1, qb_rows, grads, k_near, v_near, dq, heads, 4)
    got1 = [core_swap(part) for part in part1]
    packed = sum_messages([messages[3], packed])
    dq = after(dq, packed)
    packed = shift_col(after(packed, dq), 1)
    *part0, dq = attn_bwd(0, qb_rows, grads, k_near, v_near, dq, heads, C4)

    d_blocks, back = join_grads(part0, got1, far_got, dq, w_qkv, cols_n, scale)
    ring = [shift_col(back[1], 1)]

    d_blocks = [after(d_blocks[0], packed), *d_blocks[1:]]
    own, far, send, send_far = qkv_grads(meta, x_blocks, d_blocks, feat)
    packed = sum_messages([after(messages[0], back[1]), packed])
    got, got_far = core_swap(send), core_swap(send_far)
    ring[0], got, got_far, packed = lax.optimization_barrier((ring[0], got, got_far, packed))
    for step in range(2, cols_n + 1):
        total = back[step % cols_n] + ring[-1].astype(F32)
        if step < cols_n:
            ring.append(shift_col(total.astype(BF), 1))
    grad_tokens = grad_resid1 + total
    if paired:
        other = lax.ppermute(packed, "dp", [(0, 1), (1, 0)])
    else:
        other = lax.psum(packed.astype(F32), "dp") - packed.astype(F32)
    g_bias = own[feat] + own[feat + 1]

    def with_bias(block, bias):
        hi = lax.reduce_precision(bias, 8, 7)
        rows = jnp.pad(jnp.stack([hi, bias - hi]), ((0, 14), (0, 0)))
        return jnp.concatenate([block, rows]).astype(BF)

    def bias_of(got):
        return got[-16].astype(F32) + got[-15].astype(F32)

    g_bias = g_bias + bias_of(got)
    mine = own[:feat] + got[:feat].astype(F32)
    got_x = got = cross_swap(with_bias(far + got_far.astype(F32), g_bias))
    g_bias = g_bias + bias_of(got)
    mine = mine + got[:feat].astype(F32)
    if paired:
        got = lax.ppermute(after(with_bias(mine, g_bias), ring[0]), "dp", [(0, 1), (1, 0)])
        g_bias = g_bias + bias_of(got)
        g_qkv = mine + got[:feat].astype(F32)
    else:
        g_bias, g_qkv = lax.psum((g_bias, mine), "dp")
    g_qkv = g_qkv.astype(BF).reshape(cols_n, sub, 3 * hw)
    pieces = []
    for k in range(cols_n):
        piece = lax.dynamic_index_in_dim(g_qkv, (z + k) % cols_n, 0, keepdims=False)
        pieces.append(shift_col(piece, k) if k else piece)
    g_qkv = spread(meta, pieces)
    other = after(other, ring[1], got_x)
    *g_up, g_down_weight, g_out_weight, sums = finish(
        meta, packed, other, rows_n, units, sub_out, paired
    )
    g_up[1] = core_swap(g_up[1])
    g_up[2] = cross_swap(g_up[2])
    g_up[3] = lax.ppermute(g_up[3], "row", [(i, i ^ 3) for i in range(rows_n)])
    g_up_weight = up_grads(meta, g_up)
    vec_out = lax.dynamic_slice_in_dim(sums[:6], r * feat, feat, 1)
    g_up_bias = lax.dynamic_index_in_dim(sums[8 : 8 + cols_n], z, 0, keepdims=False)

    return (
        output,
        grad_tokens,
        g_qkv[0],
        g_qkv[1],
        g_qkv[2],
        g_bias[:hw],
        g_bias[2 * hw :],
        g_out_weight,
        vec_out[2],
        vec_out[0],
        vec_out[1],
        g_up_weight,
        g_up_bias,
        g_down_weight,
        vec_out[5],
        vec_out[3],
        vec_out[4],
    )


def solution(mesh):
    token_spec = P(("dp", "col", "row"), None)
    placed = (
        token_spec,
        token_spec,
        P("dp"),
        P(("row", "col"), None),
        P(("row", "col"), None),
        P(("row", "col"), None),
        P("col"),
        P("col"),
        P(("col", "row"), None),
        P("row"),
        P("row"),
        P("row"),
        P("row", "col"),
        P("col"),
        P(("col", "row"), None),
        P("row"),
        P("row"),
        P("row"),
    )
    return jax.shard_map(
        per_device,
        mesh=mesh,
        in_specs=placed,
        out_specs=(token_spec, token_spec) + placed[3:],
        check_vma=False,
    )
```

profile of v0, /device:TPU:0, one launch (start us, length us, event | category | flops | bytes accessed | tf_op | source)
XLA Modules:
  0.0 268.1 jit_solution(7706956583116873765)
XLA Ops:
  2.7 3.1 %collective-permute-start = (bf16[304,768]{1,0:T(8,128)(2,1)S(1)}, bf16[304,768]{1,0:T(8,128)(2,1)S(1)}, u32[]{:S(2)}, u32[]{:S(2)}) collective-permute-start(bf16[304,768]{1,0:T(8,128)(2,1)S(1)} %pad_maximum_fusion.1.refs_0_), channel_id=1, source_target_pairs={{0,1},{1,2},{2,3},{3,0},{4,5},{5,6},{6,7},{7,4},{8,9},{9,10},{10,1... | collective-permute-start | bytes 1400840 | tf_op jit(solution)/shard_map/ppermute | solution.py:913
  7.9 1.6 collective-permute-start.1
  10.6 2.8 %collective-permute-start.3 = (bf16[48,576]{1,0:T(8,128)(2,1)S(1)}, bf16[48,576]{1,0:T(8,128)(2,1)S(1)}, u32[]{:S(2)}, u32[]{:S(2)}) collective-permute-start(bf16[48,576]{1,0:T(8,128)(2,1)S(1)} %get-tuple-element.323), channel_id=1, source_target_pairs={{0,3},{1,0},{2,1},{3,2},{4,7},{5,4},{6,5},{7,6},{8,11},{9,8},{10,9... | collective-permute-start | bytes 165896 | tf_op jit(solution)/shard_map/ppermute | solution.py:913
  13.8 7.0 %collective-permute-done.1 = bf16[48,576]{1,0:T(8,128)(2,1)S(1)} collective-permute-done((bf16[48,576]{1,0:T(8,128)(2,1)S(1)}, bf16[48,576]{1,0:T(8,128)(2,1)S(1)}, u32[]{:S(2)}, u32[]{:S(2)}) %collective-permute-start.1) | collective-permute-done | bytes 55328 | tf_op jit(solution)/shard_map/ppermute | solution.py:913
  20.8 1.8 collective-permute-done.2
  22.6 1.8 collective-permute-start.7
  24.5 1.6 collective-permute-start.5
  27.9 5.4 %collective-permute-done.5.refs_4_.refs_6_ = bf16[192,576]{1,0:T(8,128)(2,1)S(1)} collective-permute-done((bf16[192,576]{1,0:T(8,128)(2,1)S(1)}, bf16[192,576]{1,0:T(8,128)(2,1)S(1)}, u32[]{:S(2)}, u32[]{:S(2)}) %collective-permute-start.5) | collective-permute-done | bytes 221216 | tf_op jit(solution)/shard_map/ppermute | solution.py:908
  33.2 1.7 collective-permute-start.12
  34.9 2.1 collective-permute-done.7.refs_2_
  40.3 1.6 collective-permute-start.14
  41.9 8.6 %collective-permute-done.8.refs_3_ = bf16[304,768]{1,0:T(8,128)(2,1)S(1)} collective-permute-done((bf16[304,768]{1,0:T(8,128)(2,1)S(1)}, bf16[304,768]{1,0:T(8,128)(2,1)S(1)}, u32[]{:S(2)}, u32[]{:S(2)}) %collective-permute-start.8) | collective-permute-done | bytes 466976 | tf_op jit(solution)/shard_map/ppermute | solution.py:913
  50.5 1.5 project_qkv.3
  52.1 1.6 collective-permute-start.16
  53.9 10.0 %attn_fwd_near.1 = (f32[192,1024]{1,0:T(8,128)S(1)}, f32[16,1024]{1,0:T(8,128)S(1)}, bf16[2048,256]{1,0:T(8,128)(2,1)S(1)}, bf16[2048,256]{1,0:T(8,128)(2,1)S(1)}) custom-call(s32[5]{0:T(128)S(1)} %stack.82.meta.refs_0_, bf16[512,256]{1,0:T(8,128)(2,1)S(1)} %get-tuple-element.168.refs_1_, bf16[512,256]{1,0:T(8,128)(2,1)S(1)} %get-tuple-element.173.refs_2_, ...), custom_call_target="tpu_custom_call" | custom-call | flops 2400000000 | bytes 1000 | tf_op jit(solution)/shard_map/attn_fwd_near/pallas_call | solution.py:156
  66.9 1.6 collective-permute-start.20
  68.5 10.5 %attn_fwd_far.1 = (bf16[192,256]{1,0:T(8,128)(2,1)S(1)}, bf16[192,256]{1,0:T(8,128)(2,1)S(1)}, bf16[192,256]{1,0:T(8,128)(2,1)S(1)}, bf16[192,256]{1,0:T(8,128)(...) custom-call(s32[5]{0:T(128)S(1)} %stack.82.meta.refs_0_, ...), custom_call_target="tpu_custom_call" | custom-call | flops 2400000000 | bytes 1000 | tf_op jit(solution)/shard_map/attn_fwd_far/pallas_call | solution.py:156
  79.7 3.6 %collective-permute-start.22 = (bf16[192,256]{1,0:T(8,128)(2,1)S(1)}, bf16[192,256]{1,0:T(8,128)(2,1)S(1)}, u32[]{:S(2)}, u32[]{:S(2)}) collective-permute-start(bf16[192,256]{1,0:T(8,128)(2,1)S(1)} %get-tuple-element.195.refs_1_), channel_id=1, source_target_pairs={{0,3},{1,0},{2,1},{3,2},{4,7},{5,4},{6,5},{7,6},{8,11},{9,8},{10,9... | collective-permute-start | bytes 294920 | tf_op jit(solution)/shard_map/ppermute | solution.py:913
  83.8 2.7 %collective-permute-done.22.refs_1_ = bf16[192,256]{1,0:T(8,128)(2,1)S(1)} collective-permute-done((bf16[192,256]{1,0:T(8,128)(2,1)S(1)}, bf16[192,256]{1,0:T(8,128)(2,1)S(1)}, u32[]{:S(2)}, u32[]{:S(2)}) %collective-permute-start.22) | collective-permute-done | bytes 98336 | tf_op jit(solution)/shard_map/ppermute | solution.py:913
  86.5 5.0 %collective-permute-done.23.refs_2_ = bf16[192,256]{1,0:T(8,128)(2,1)S(1)} collective-permute-done((bf16[192,256]{1,0:T(8,128)(2,1)S(1)}, bf16[192,256]{1,0:T(8,128)(2,1)S(1)}, u32[]{:S(2)}, u32[]{:S(2)}) %collective-permute-start.23) | collective-permute-done | bytes 98336 | tf_op jit(solution)/shard_map/ppermute | solution.py:913
  91.5 2.0 collective-permute-done.24.refs_3_
  95.2 1.6 collective-permute-start.29
  96.8 6.0 %collective-permute-done.30.refs_7_ = bf16[208,768]{1,0:T(8,128)(2,1)S(1)} collective-permute-done((bf16[208,768]{1,0:T(8,128)(2,1)S(1)}, bf16[208,768]{1,0:T(8,128)(2,1)S(1)}, u32[]{:S(2)}, u32[]{:S(2)}) %collective-permute-start.30) | collective-permute-done | bytes 319520 | tf_op jit(solution)/shard_map/ppermute | solution.py:913
  102.8 1.5 collective-permute-start.31
  104.3 2.5 collective-permute-done.29.refs_0_.refs_6_
  106.8 3.0 %collective-permute-done.31.refs_8_ = bf16[208,768]{1,0:T(8,128)(2,1)S(1)} collective-permute-done((bf16[208,768]{1,0:T(8,128)(2,1)S(1)}, bf16[208,768]{1,0:T(8,128)(2,1)S(1)}, u32[]{:S(2)}, u32[]{:S(2)}) %collective-permute-start.31) | collective-permute-done | bytes 319520 | tf_op jit(solution)/shard_map/ppermute | solution.py:1014
  109.7 1.7 collective-permute-done.33.refs_1_.refs_7_
  111.5 2.6 ffn_fwd.3
  114.2 2.6 ffn_fwd.2
  117.4 1.6 collective-permute-start.35
  118.9 9.7 %collective-permute-done.35.far_ref = bf16[256,768]{1,0:T(8,128)(2,1)S(1)} collective-permute-done((bf16[256,768]{1,0:T(8,128)(2,1)S(1)}, bf16[256,768]{1,0:T(8,128)(2,1)S(1)}, u32[]{:S(2)}, u32[]{:S(2)}) %collective-permute-start.35) | collective-permute-done | bytes 393248 | tf_op jit(solution)/shard_map/ppermute | solution.py:908
  128.6 2.0 norm2_both.1
  132.3 2.2 ffn_bwd.2
  134.5 7.6 %collective-permute-done.37.refs_0_.refs_10_ = bf16[256,768]{1,0:T(8,128)(2,1)S(1)} collective-permute-done((bf16[256,768]{1,0:T(8,128)(2,1)S(1)}, bf16[256,768]{1,0:T(8,128)(2,1)S(1)}, u32[]{:S(2)}, u32[]{:S(2)}) %collective-permute-start.37) | collective-permute-done | bytes 393248 | tf_op jit(solution)/shard_map/ppermute | solution.py:908
  142.1 1.7 collective-permute-done.38.refs_1_.refs_11_
  143.8 2.1 ffn_bwd.3
  147.9 1.6 collective-permute-start.41
  149.4 3.9 %ffn_grads.1 = (bf16[768,768]{1,0:T(8,128)(2,1)S(1)}, bf16[768,768]{1,0:T(8,128)(2,1)S(1)}, f32[8,768]{1,0:T(8,128)S(1)}) custom-call(s32[5]{0:T(128)S(1)} %stack.82.meta.refs_0_, bf16[512,768]{1,0:T(8,128)(2,1)S(1)} %get-tuple-element.222.refs_0_, bf16[512,768]{1,0:T(8,128)(2,1)S(1)} %get-tuple-element.223.refs_1_, ...), custom_call_target="tpu_custom_call" | custom-call | flops 720000000 | bytes 1000 | tf_op jit(solution)/shard_map/ffn_grads/pallas_call | solution.py:266
  153.3 1.6 collective-permute-start.46
  154.9 4.2 %collective-permute-done.41.far_ref = bf16[256,768]{1,0:T(8,128)(2,1)S(1)} collective-permute-done((bf16[256,768]{1,0:T(8,128)(2,1)S(1)}, bf16[256,768]{1,0:T(8,128)(2,1)S(1)}, u32[]{:S(2)}, u32[]{:S(2)}) %collective-permute-start.41) | collective-permute-done | bytes 393248 | tf_op jit(solution)/shard_map/ppermute | solution.py:908
  161.7 1.9 collective-permute-start.43
  163.6 2.8 %collective-permute-start.44 = (bf16[192,256]{1,0:T(8,128)(2,1)S(1)}, bf16[192,256]{1,0:T(8,128)(2,1)S(1)}, u32[]{:S(2)}, u32[]{:S(2)}) collective-permute-start(bf16[192,256]{1,0:T(8,128)(2,1)S(1)} %get-tuple-element.242), channel_id=1, source_target_pairs={{0,3},{1,0},{2,1},{3,2},{4,7},{5,4},{6,5},{7,6},{8,11},{9,8},{10,9... | collective-permute-start | bytes 294920 | tf_op jit(solution)/shard_map/ppermute | solution.py:913
  166.4 2.7 %collective-permute-done.42.refs_5_ = bf16[192,256]{1,0:T(8,128)(2,1)S(1)} collective-permute-done((bf16[192,256]{1,0:T(8,128)(2,1)S(1)}, bf16[192,256]{1,0:T(8,128)(2,1)S(1)}, u32[]{:S(2)}, u32[]{:S(2)}) %collective-permute-start.42) | collective-permute-done | bytes 98336 | tf_op jit(solution)/shard_map/ppermute | solution.py:913
  169.2 1.6 collective-permute-start.47
  170.8 1.7 collective-permute-done.43.refs_6_
  172.8 9.1 %attn_bwd.4 = (bf16[512,384]{1,0:T(8,128)(2,1)S(1)}, bf16[512,384]{1,0:T(8,128)(2,1)S(1)}, f32[1024,256]{1,0:T(8,128)S(1)}) custom-call(s32[1]{0:T(128)} %constant.102.clone.1.at_ref, bf16[1024,256]{1,0:T(8,128)(2,1)S(1)} %get-tuple-element.238.q_ref, bf16[1024,256]{1,0:T(8,128)(2,1)S(1)} %grad_rows.1.g_ref, bf16[2048,256]{1,0:T(8,128)(2,1)S(1)} %get-tuple-element.254.k_ref, ...), custom_call_target="tpu_custom_call" | custom-call | flops 2400000000 | bytes 1000 | tf_op jit(solution)/shard_map/attn_bwd/pallas_call | solution.py:241
  182.9 2.2 collective-permute-start.50
  185.0 9.1 %attn_bwd.5 = (bf16[512,384]{1,0:T(8,128)(2,1)S(1)}, bf16[512,384]{1,0:T(8,128)(2,1)S(1)}, f32[1024,256]{1,0:T(8,128)S(1)}) custom-call(s32[1]{0:T(128)} %constant.101.clone.1.at_ref, bf16[1024,256]{1,0:T(8,128)(2,1)S(1)} %get-tuple-element.238.q_ref, bf16[1024,256]{1,0:T(8,128)(2,1)S(1)} %grad_rows.1.g_ref, bf16[2048,256]{1,0:T(8,128)(2,1)S(1)} %get-tuple-element.254.k_ref, ...), custom_call_target="tpu_custom_call" | custom-call | flops 2400000000 | bytes 1000 | tf_op jit(solution)/shard_map/attn_bwd/pallas_call | solution.py:241
  194.5 1.8 collective-permute-done.50.refs_1_
  198.7 9.1 %attn_bwd.6 = (bf16[512,384]{1,0:T(8,128)(2,1)S(1)}, bf16[512,384]{1,0:T(8,128)(2,1)S(1)}, f32[1024,256]{1,0:T(8,128)S(1)}) custom-call(s32[1]{0:T(128)} %constant.102.clone.1.at_ref, bf16[1024,256]{1,0:T(8,128)(2,1)S(1)} %get-tuple-element.238.q_ref, bf16[1024,256]{1,0:T(8,128)(2,1)S(1)} %grad_rows.1.g_ref, bf16[2048,256]{1,0:T(8,128)(2,1)S(1)} %get-tuple-element.252.k_ref, ...), custom_call_target="tpu_custom_call" | custom-call | flops 2400000000 | bytes 1000 | tf_op jit(solution)/shard_map/attn_bwd/pallas_call | solution.py:241
  209.7 9.1 %attn_bwd.7 = (bf16[512,384]{1,0:T(8,128)(2,1)S(1)}, bf16[512,384]{1,0:T(8,128)(2,1)S(1)}, f32[1024,256]{1,0:T(8,128)S(1)}) custom-call(s32[1]{0:T(128)} %constant.101.clone.1.at_ref, bf16[1024,256]{1,0:T(8,128)(2,1)S(1)} %get-tuple-element.238.q_ref, bf16[1024,256]{1,0:T(8,128)(2,1)S(1)} %grad_rows.1.g_ref, bf16[2048,256]{1,0:T(8,128)(2,1)S(1)} %get-tuple-element.252.k_ref, ...), custom_call_target="tpu_custom_call" | custom-call | flops 3600000000 | bytes 1000 | tf_op jit(solution)/shard_map/attn_bwd/pallas_call | solution.py:241
  218.8 2.0 join_grads.1
  223.1 2.9 %qkv_grads.1 = (f32[208,576]{1,0:T(8,128)S(1)}, f32[192,576]{1,0:T(8,128)S(1)}, bf16[208,576]{1,0:T(8,128)(2,1)}, bf16[192,576]{1,0:T(8,128)(2,1)}) custom-call(s32[5]{0:T(128)S(1)} %stack.82.meta.refs_0_, bf16[304,768]{1,0:T(8,128)(2,1)S(1)} %pad_maximum_fusion.1.refs_0_, bf16[304,768]{1,0:T(8,128)(2,1)S(1)} %collective-permute-done.refs_1_, ...), custom_call_target="tpu_custom_call" | custom-call | flops 720000000 | bytes 1000 | tf_op jit(solution)/shard_map/qkv_grads/pallas_call | solution.py:266
  229.4 4.5 %collective-permute-done.55 = bf16[256,768]{1,0:T(8,128)(2,1)} collective-permute-done((bf16[256,768]{1,0:T(8,128)(2,1)}, bf16[256,768]{1,0:T(8,128)(2,1)}, u32[]{:S(2)}, u32[]{:S(2)}) %collective-permute-start.55) | collective-permute-done | bytes 393248 | tf_op jit(solution)/shard_map/ppermute | solution.py:913
  238.2 1.6 collective-permute-start.66
  239.8 2.4 collective-permute-done.61
  242.3 1.6 collective-permute-start.62
  243.9 4.5 %collective-permute-done.59 = bf16[256,768]{1,0:T(8,128)(2,1)S(1)} collective-permute-done((bf16[256,768]{1,0:T(8,128)(2,1)S(1)}, bf16[256,768]{1,0:T(8,128)(2,1)S(1)}, u32[]{:S(2)}, u32[]{:S(2)}) %collective-permute-start.59) | collective-permute-done | bytes 393248 | tf_op jit(solution)/shard_map/ppermute | solution.py:913
  248.6 2.0 collective-permute-done.66.other
  250.6 2.2 finish_grads.1
  256.1 2.1 collective-permute-start.63
  258.8 1.5 collective-permute-start.64
  261.7 1.5 up_grads.1
  263.2 2.0 collective-permute-done.64.refs_2_
  (219 shorter events, 46.8 us)
Async XLA Ops:
  2.7 19.9 %collective-permute-start = (bf16[304,768]{1,0:T(8,128)(2,1)S(1)}, bf16[304,768]{1,0:T(8,128)(2,1)S(1)}, u32[]{:S(2)}, u32[]{:S(2)}) collective-permute-start(bf16[304,768]{1,0:T(8,128)(2,1)S(1)} %pad_maximum_fusion.1.refs_0_), channel_id=1, source_target_pairs={{0,1},{1,2},{2,3},{3,0},{4,5},{5,6},{6,7},{7,4},{8,9},{9,10},{10,1... | collective-permute-start | bytes 1400840 | tf_op jit(solution)/shard_map/ppermute | solution.py:913
  7.9 12.9 %collective-permute-start.1 = (bf16[48,576]{1,0:T(8,128)(2,1)S(1)}, bf16[48,576]{1,0:T(8,128)(2,1)S(1)}, u32[]{:S(2)}, u32[]{:S(2)}) collective-permute-start(bf16[48,576]{1,0:T(8,128)(2,1)S(1)} %get-tuple-element.325), channel_id=1, source_target_pairs={{0,1},{1,2},{2,3},{3,0},{4,5},{5,6},{6,7},{7,4},{8,9},{9,10},{10,1... | collective-permute-start | bytes 165896 | tf_op jit(solution)/shard_map/ppermute | solution.py:913
  9.5 13.1 %collective-permute-start.2 = (bf16[48,576]{1,0:T(8,128)(2,1)S(1)}, bf16[48,576]{1,0:T(8,128)(2,1)S(1)}, u32[]{:S(2)}, u32[]{:S(2)}) collective-permute-start(bf16[48,576]{1,0:T(8,128)(2,1)S(1)} %get-tuple-element.324), channel_id=1, source_target_pairs={{0,2},{1,3},{2,0},{3,1},{4,6},{5,7},{6,4},{7,5},{8,10},{9,11},{10,... | collective-permute-start | bytes 165896 | tf_op jit(solution)/shard_map/ppermute | solution.py:913
  10.6 12.0 %collective-permute-start.3 = (bf16[48,576]{1,0:T(8,128)(2,1)S(1)}, bf16[48,576]{1,0:T(8,128)(2,1)S(1)}, u32[]{:S(2)}, u32[]{:S(2)}) collective-permute-start(bf16[48,576]{1,0:T(8,128)(2,1)S(1)} %get-tuple-element.323), channel_id=1, source_target_pairs={{0,3},{1,0},{2,1},{3,2},{4,7},{5,4},{6,5},{7,6},{8,11},{9,8},{10,9... | collective-permute-start | bytes 165896 | tf_op jit(solution)/shard_map/ppermute | solution.py:913
  22.6 14.4 %collective-permute-start.7 = (bf16[304,768]{1,0:T(8,128)(2,1)S(1)}, bf16[304,768]{1,0:T(8,128)(2,1)S(1)}, u32[]{:S(2)}, u32[]{:S(2)}) collective-permute-start(bf16[304,768]{1,0:T(8,128)(2,1)S(1)} %collective-permute-done.refs_1_), channel_id=1, source_target_pairs={{0,1},{1,2},{2,3},{3,0},{4,5},{5,6},{6,7},{7,4},{8,9},{9,10},{10,1... | collective-permute-start | bytes 1400840 | tf_op jit(solution)/shard_map/ppermute | solution.py:913
  24.5 8.7 %collective-permute-start.5 = (bf16[192,576]{1,0:T(8,128)(2,1)S(1)}, bf16[192,576]{1,0:T(8,128)(2,1)S(1)}, u32[]{:S(2)}, u32[]{:S(2)}) collective-permute-start(bf16[192,576]{1,0:T(8,128)(2,1)S(1)} %constant_dynamic-update-slice_fusion.refs_2_.refs_4_), channel_id=1, source_target_pairs={{0,8},{8,0},{4,12},{12,4},{1,9},{9,1},{5,13},{13,5},{2,10},{10,2},... | collective-permute-start | bytes 663560 | tf_op jit(solution)/shard_map/ppermute | solution.py:908
  26.1 13.4 %collective-permute-start.10 = (bf16[192,192]{1,0:T(8,128)(2,1)S(1)}, bf16[192,192]{1,0:T(8,128)(2,1)S(1)}, u32[]{:S(2)}, u32[]{:S(2)}) collective-permute-start(bf16[192,192]{1,0:T(8,128)(2,1)S(1)} %get-tuple-element.317), channel_id=1, source_target_pairs={{0,4},{4,0},{8,12},{12,8},{1,5},{5,1},{9,13},{13,9},{2,6},{6,2},{1... | collective-permute-start | bytes 221192 | tf_op jit(solution)/shard_map/ppermute | solution.py:904
  26.2 13.3 %collective-permute-start.11 = (bf16[192,192]{1,0:T(8,128)(2,1)S(1)}, bf16[192,192]{1,0:T(8,128)(2,1)S(1)}, u32[]{:S(2)}, u32[]{:S(2)}) collective-permute-start(bf16[192,192]{1,0:T(8,128)(2,1)S(1)} %get-tuple-element.316), channel_id=1, source_target_pairs={{0,8},{8,0},{4,12},{12,4},{1,9},{9,1},{5,13},{13,5},{2,10},{10,2},... | collective-permute-start | bytes 221192 | tf_op jit(solution)/shard_map/ppermute | solution.py:908
  27.7 5.5 %collective-permute-start.4 = (bf16[192,576]{1,0:T(8,128)(2,1)S(1)}, bf16[192,576]{1,0:T(8,128)(2,1)S(1)}, u32[]{:S(2)}, u32[]{:S(2)}) collective-permute-start(bf16[192,576]{1,0:T(8,128)(2,1)S(1)} %constant_dynamic-update-slice_fusion.refs_2_.refs_4_), channel_id=1, source_target_pairs={{0,4},{4,0},{8,12},{12,8},{1,5},{5,1},{9,13},{13,9},{2,6},{6,2},{1... | collective-permute-start | bytes 663560 | tf_op jit(solution)/shard_map/ppermute | solution.py:904
  33.2 3.9 %collective-permute-start.6 = (bf16[192,576]{1,0:T(8,128)(2,1)S(1)}, bf16[192,576]{1,0:T(8,128)(2,1)S(1)}, u32[]{:S(2)}, u32[]{:S(2)}) collective-permute-start(bf16[192,576]{1,0:T(8,128)(2,1)S(1)} %collective-permute-done.5.refs_4_.refs_6_), channel_id=1, source_target_pairs={{0,4},{4,0},{8,12},{12,8},{1,5},{5,1},{9,13},{13,9},{2,6},{6,2},{1... | collective-permute-start | bytes 663560 | tf_op jit(solution)/shard_map/ppermute | solution.py:904
  33.2 6.3 %collective-permute-start.12 = (bf16[192,192]{1,0:T(8,128)(2,1)S(1)}, bf16[192,192]{1,0:T(8,128)(2,1)S(1)}, u32[]{:S(2)}, u32[]{:S(2)}) collective-permute-start(bf16[192,192]{1,0:T(8,128)(2,1)S(1)} %get-tuple-element.315), channel_id=1, source_target_pairs={{0,12},{4,8},{8,4},{12,0},{1,13},{5,9},{9,5},{13,1},{2,14},{6,10},... | collective-permute-start | bytes 221192 | tf_op jit(solution)/shard_map/ppermute | solution.py:995
  37.0 13.5 %collective-permute-start.8 = (bf16[304,768]{1,0:T(8,128)(2,1)S(1)}, bf16[304,768]{1,0:T(8,128)(2,1)S(1)}, u32[]{:S(2)}, u32[]{:S(2)}) collective-permute-start(bf16[304,768]{1,0:T(8,128)(2,1)S(1)} %collective-permute-done.7.refs_2_), channel_id=1, source_target_pairs={{0,1},{1,2},{2,3},{3,0},{4,5},{5,6},{6,7},{7,4},{8,9},{9,10},{10,1... | collective-permute-start | bytes 1400840 | tf_op jit(solution)/shard_map/ppermute | solution.py:913
  38.6 3.3 %collective-permute-start.9 = (bf16[512,384]{1,0:T(8,128)(2,1)S(1)}, bf16[512,384]{1,0:T(8,128)(2,1)S(1)}, u32[]{:S(2)}, u32[]{:S(2)}) collective-permute-start(bf16[512,384]{1,0:T(8,128)(2,1)S(1)} %get-tuple-element.170.refs_3_), channel_id=1, source_target_pairs={{0,4},{4,0},{8,12},{12,8},{1,5},{5,1},{9,13},{13,9},{2,6},{6,2},{1... | collective-permute-start | bytes 1179656 | tf_op jit(solution)/shard_map/ppermute | solution.py:904
  40.3 13.6 %collective-permute-start.14 = (bf16[512,384]{1,0:T(8,128)(2,1)S(1)}, bf16[512,384]{1,0:T(8,128)(2,1)S(1)}, u32[]{:S(2)}, u32[]{:S(2)}) collective-permute-start(bf16[512,384]{1,0:T(8,128)(2,1)S(1)} %get-tuple-element.170.refs_3_), channel_id=1, source_target_pairs={{0,8},{8,0},{4,12},{12,4},{1,9},{9,1},{5,13},{13,5},{2,10},{10,2},... | collective-permute-start | bytes 1179656 | tf_op jit(solution)/shard_map/ppermute | solution.py:908
  52.1 13.2 %collective-permute-start.16 = (bf16[512,384]{1,0:T(8,128)(2,1)S(1)}, bf16[512,384]{1,0:T(8,128)(2,1)S(1)}, u32[]{:S(2)}, u32[]{:S(2)}) collective-permute-start(bf16[512,384]{1,0:T(8,128)(2,1)S(1)} %get-tuple-element.174.refs_4_), channel_id=1, source_target_pairs={{0,8},{8,0},{4,12},{12,4},{1,9},{9,1},{5,13},{13,5},{2,10},{10,2},... | collective-permute-start | bytes 1179656 | tf_op jit(solution)/shard_map/ppermute | solution.py:908
  53.6 11.7 %collective-permute-start.15 = (bf16[208,768]{1,0:T(8,128)(2,1)S(1)}, bf16[208,768]{1,0:T(8,128)(2,1)S(1)}, u32[]{:S(2)}, u32[]{:S(2)}) collective-permute-start(bf16[208,768]{1,0:T(8,128)(2,1)S(1)} %get-tuple-element.179), channel_id=1, source_target_pairs={{0,1},{1,2},{2,3},{3,0},{4,5},{5,6},{6,7},{7,4},{8,9},{9,10},{10,1... | collective-permute-start | bytes 958472 | tf_op jit(solution)/shard_map/ppermute | solution.py:913
  65.3 3.2 %collective-permute-start.17 = (bf16[512,384]{1,0:T(8,128)(2,1)S(1)}, bf16[512,384]{1,0:T(8,128)(2,1)S(1)}, u32[]{:S(2)}, u32[]{:S(2)}) collective-permute-start(bf16[512,384]{1,0:T(8,128)(2,1)S(1)} %collective-permute-done.14.refs_3_), channel_id=1, source_target_pairs={{0,4},{4,0},{8,12},{12,8},{1,5},{5,1},{9,13},{13,9},{2,6},{6,2},{1... | collective-permute-start | bytes 1179656 | tf_op jit(solution)/shard_map/ppermute | solution.py:904
  65.3 3.2 %collective-permute-start.18 = (bf16[512,384]{1,0:T(8,128)(2,1)S(1)}, bf16[512,384]{1,0:T(8,128)(2,1)S(1)}, u32[]{:S(2)}, u32[]{:S(2)}) collective-permute-start(bf16[512,384]{1,0:T(8,128)(2,1)S(1)} %collective-permute-done.16.refs_4_), channel_id=1, source_target_pairs={{0,4},{4,0},{8,12},{12,8},{1,5},{5,1},{9,13},{13,9},{2,6},{6,2},{1... | collective-permute-start | bytes 1179656 | tf_op jit(solution)/shard_map/ppermute | solution.py:904
  65.8 13.1 %collective-permute-start.21 = (bf16[224,768]{1,0:T(8,128)(2,1)S(1)}, bf16[224,768]{1,0:T(8,128)(2,1)S(1)}, u32[]{:S(2)}, u32[]{:S(2)}) collective-permute-start(bf16[224,768]{1,0:T(8,128)(2,1)S(1)} %get-tuple-element.192.refs_4_), channel_id=1, source_target_pairs={{0,8},{8,0},{4,12},{12,4},{1,9},{9,1},{5,13},{13,5},{2,10},{10,2},... | collective-permute-start | bytes 1032200 | tf_op jit(solution)/shard_map/ppermute | solution.py:908
  66.3 12.6 %collective-permute-start.19 = (bf16[208,768]{1,0:T(8,128)(2,1)S(1)}, bf16[208,768]{1,0:T(8,128)(2,1)S(1)}, u32[]{:S(2)}, u32[]{:S(2)}) collective-permute-start(bf16[208,768]{1,0:T(8,128)(2,1)S(1)} %collective-permute-done.15.refs_3_), channel_id=1, source_target_pairs={{0,1},{1,2},{2,3},{3,0},{4,5},{5,6},{6,7},{7,4},{8,9},{9,10},{10,1... | collective-permute-start | bytes 958472 | tf_op jit(solution)/shard_map/ppermute | solution.py:913
  66.9 12.1 %collective-permute-start.20 = (bf16[208,768]{1,0:T(8,128)(2,1)S(1)}, bf16[208,768]{1,0:T(8,128)(2,1)S(1)}, u32[]{:S(2)}, u32[]{:S(2)}) collective-permute-start(bf16[208,768]{1,0:T(8,128)(2,1)S(1)} %collective-permute-done.15.refs_3_), channel_id=1, source_target_pairs={{0,16},{16,0},{1,17},{17,1},{2,18},{18,2},{3,19},{19,3},{4,20},{20... | collective-permute-start | bytes 958472 | tf_op jit(solution)/shard_map/ppermute | solution.py:1014
  79.0 14.5 %collective-permute-start.25 = (bf16[208,768]{1,0:T(8,128)(2,1)S(1)}, bf16[208,768]{1,0:T(8,128)(2,1)S(1)}, u32[]{:S(2)}, u32[]{:S(2)}) collective-permute-start(bf16[208,768]{1,0:T(8,128)(2,1)S(1)} %collective-permute-done.19.refs_5_), channel_id=1, source_target_pairs={{0,16},{16,0},{1,17},{17,1},{2,18},{18,2},{3,19},{19,3},{4,20},{20... | collective-permute-start | bytes 958472 | tf_op jit(solution)/shard_map/ppermute | solution.py:1014
  79.7 6.8 %collective-permute-start.22 = (bf16[192,256]{1,0:T(8,128)(2,1)S(1)}, bf16[192,256]{1,0:T(8,128)(2,1)S(1)}, u32[]{:S(2)}, u32[]{:S(2)}) collective-permute-start(bf16[192,256]{1,0:T(8,128)(2,1)S(1)} %get-tuple-element.195.refs_1_), channel_id=1, source_target_pairs={{0,3},{1,0},{2,1},{3,2},{4,7},{5,4},{6,5},{7,6},{8,11},{9,8},{10,9... | collective-permute-start | bytes 294920 | tf_op jit(solution)/shard_map/ppermute | solution.py:913
  83.3 10.4 %collective-permute-start.26 = (bf16[224,768]{1,0:T(8,128)(2,1)S(1)}, bf16[224,768]{1,0:T(8,128)(2,1)S(1)}, u32[]{:S(2)}, u32[]{:S(2)}) collective-permute-start(bf16[224,768]{1,0:T(8,128)(2,1)S(1)} %get-tuple-element.192.refs_4_), channel_id=1, source_target_pairs={{0,4},{4,0},{8,12},{12,8},{1,5},{5,1},{9,13},{13,9},{2,6},{6,2},{1... | collective-permute-start | bytes 1032200 | tf_op jit(solution)/shard_map/ppermute | solution.py:904
  83.3 10.4 %collective-permute-start.27 = (bf16[224,768]{1,0:T(8,128)(2,1)S(1)}, bf16[224,768]{1,0:T(8,128)(2,1)S(1)}, u32[]{:S(2)}, u32[]{:S(2)}) collective-permute-start(bf16[224,768]{1,0:T(8,128)(2,1)S(1)} %collective-permute-done.21.refs_6_), channel_id=1, source_target_pairs={{0,4},{4,0},{8,12},{12,8},{1,5},{5,1},{9,13},{13,9},{2,6},{6,2},{1... | collective-permute-start | bytes 1032200 | tf_op jit(solution)/shard_map/ppermute | solution.py:904
  83.8 7.7 %collective-permute-start.23 = (bf16[192,256]{1,0:T(8,128)(2,1)S(1)}, bf16[192,256]{1,0:T(8,128)(2,1)S(1)}, u32[]{:S(2)}, u32[]{:S(2)}) collective-permute-start(bf16[192,256]{1,0:T(8,128)(2,1)S(1)} %get-tuple-element.196.refs_2_), channel_id=1, source_target_pairs={{0,2},{1,3},{2,0},{3,1},{4,6},{5,7},{6,4},{7,5},{8,10},{9,11},{10,... | collective-permute-start | bytes 294920 | tf_op jit(solution)/shard_map/ppermute | solution.py:913
  86.5 7.0 %collective-permute-start.24 = (bf16[192,256]{1,0:T(8,128)(2,1)S(1)}, bf16[192,256]{1,0:T(8,128)(2,1)S(1)}, u32[]{:S(2)}, u32[]{:S(2)}) collective-permute-start(bf16[192,256]{1,0:T(8,128)(2,1)S(1)} %get-tuple-element.197.refs_3_), channel_id=1, source_target_pairs={{0,1},{1,2},{2,3},{3,0},{4,5},{5,6},{6,7},{7,4},{8,9},{9,10},{10,1... | collective-permute-start | bytes 294920 | tf_op jit(solution)/shard_map/ppermute | solution.py:913
  93.5 9.3 %collective-permute-start.30 = (bf16[208,768]{1,0:T(8,128)(2,1)S(1)}, bf16[208,768]{1,0:T(8,128)(2,1)S(1)}, u32[]{:S(2)}, u32[]{:S(2)}) collective-permute-start(bf16[208,768]{1,0:T(8,128)(2,1)S(1)} %collective-permute-done.19.refs_5_), channel_id=1, source_target_pairs={{0,1},{1,2},{2,3},{3,0},{4,5},{5,6},{6,7},{7,4},{8,9},{9,10},{10,1... | collective-permute-start | bytes 958472 | tf_op jit(solution)/shard_map/ppermute | solution.py:913
  95.2 9.1 %collective-permute-start.28 = (bf16[256,768]{1,0:T(8,128)(2,1)S(1)}, bf16[256,768]{1,0:T(8,128)(2,1)S(1)}, u32[]{:S(2)}, u32[]{:S(2)}) collective-permute-start(bf16[256,768]{1,0:T(8,128)(2,1)S(1)} %get-tuple-element.205.refs_0_.refs_4_), channel_id=1, source_target_pairs={{0,4},{4,0},{8,12},{12,8},{1,5},{5,1},{9,13},{13,9},{2,6},{6,2},{1... | collective-permute-start | bytes 1179656 | tf_op jit(solution)/shard_map/ppermute | solution.py:904
  95.2 11.5 %collective-permute-start.29 = (bf16[256,768]{1,0:T(8,128)(2,1)S(1)}, bf16[256,768]{1,0:T(8,128)(2,1)S(1)}, u32[]{:S(2)}, u32[]{:S(2)}) collective-permute-start(bf16[256,768]{1,0:T(8,128)(2,1)S(1)} %get-tuple-element.205.refs_0_.refs_4_), channel_id=1, source_target_pairs={{0,8},{8,0},{4,12},{12,4},{1,9},{9,1},{5,13},{13,5},{2,10},{10,2},... | collective-permute-start | bytes 1179656 | tf_op jit(solution)/shard_map/ppermute | solution.py:908
  102.8 7.0 %collective-permute-start.31 = (bf16[208,768]{1,0:T(8,128)(2,1)S(1)}, bf16[208,768]{1,0:T(8,128)(2,1)S(1)}, u32[]{:S(2)}, u32[]{:S(2)}) collective-permute-start(bf16[208,768]{1,0:T(8,128)(2,1)S(1)} %collective-permute-done.30.refs_7_), channel_id=1, source_target_pairs={{0,16},{16,0},{1,17},{17,1},{2,18},{18,2},{3,19},{19,3},{4,20},{20... | collective-permute-start | bytes 958472 | tf_op jit(solution)/shard_map/ppermute | solution.py:1014
  114.0 3.2 %collective-permute-start.34 = (bf16[256,768]{1,0:T(8,128)(2,1)S(1)}, bf16[256,768]{1,0:T(8,128)(2,1)S(1)}, u32[]{:S(2)}, u32[]{:S(2)}) collective-permute-start(bf16[256,768]{1,0:T(8,128)(2,1)S(1)} %get-tuple-element.216), channel_id=1, source_target_pairs={{0,4},{4,0},{8,12},{12,8},{1,5},{5,1},{9,13},{13,9},{2,6},{6,2},{1... | collective-permute-start | bytes 1179656 | tf_op jit(solution)/shard_map/ppermute | solution.py:904
  117.4 11.2 %collective-permute-start.35 = (bf16[256,768]{1,0:T(8,128)(2,1)S(1)}, bf16[256,768]{1,0:T(8,128)(2,1)S(1)}, u32[]{:S(2)}, u32[]{:S(2)}) collective-permute-start(bf16[256,768]{1,0:T(8,128)(2,1)S(1)} %add_convert_fusion.5), channel_id=1, source_target_pairs={{0,8},{8,0},{4,12},{12,4},{1,9},{9,1},{5,13},{13,5},{2,10},{10,2},... | collective-permute-start | bytes 1179656 | tf_op jit(solution)/shard_map/ppermute | solution.py:908
  130.6 11.5 %collective-permute-start.37 = (bf16[256,768]{1,0:T(8,128)(2,1)S(1)}, bf16[256,768]{1,0:T(8,128)(2,1)S(1)}, u32[]{:S(2)}, u32[]{:S(2)}) collective-permute-start(bf16[256,768]{1,0:T(8,128)(2,1)S(1)} %get-tuple-element.219.refs_0_.refs_8_), channel_id=1, source_target_pairs={{0,8},{8,0},{4,12},{12,4},{1,9},{9,1},{5,13},{13,5},{2,10},{10,2},... | collective-permute-start | bytes 1179656 | tf_op jit(solution)/shard_map/ppermute | solution.py:908
  146.2 8.7 %collective-permute-start.39 = (bf16[256,768]{1,0:T(8,128)(2,1)S(1)}, bf16[256,768]{1,0:T(8,128)(2,1)S(1)}, u32[]{:S(2)}, u32[]{:S(2)}) collective-permute-start(bf16[256,768]{1,0:T(8,128)(2,1)S(1)} %get-tuple-element.225), channel_id=1, source_target_pairs={{0,4},{4,0},{8,12},{12,8},{1,5},{5,1},{9,13},{13,9},{2,6},{6,2},{1... | collective-permute-start | bytes 1179656 | tf_op jit(solution)/shard_map/ppermute | solution.py:904
  147.9 11.2 %collective-permute-start.41 = (bf16[256,768]{1,0:T(8,128)(2,1)S(1)}, bf16[256,768]{1,0:T(8,128)(2,1)S(1)}, u32[]{:S(2)}, u32[]{:S(2)}) collective-permute-start(bf16[256,768]{1,0:T(8,128)(2,1)S(1)} %add_convert_fusion.4), channel_id=1, source_target_pairs={{0,8},{8,0},{4,12},{12,4},{1,9},{9,1},{5,13},{13,5},{2,10},{10,2},... | collective-permute-start | bytes 1179656 | tf_op jit(solution)/shard_map/ppermute | solution.py:908
  153.3 29.1 %collective-permute-start.46 = (bf16[768,768]{1,0:T(8,128)(2,1)S(1)}, bf16[768,768]{1,0:T(8,128)(2,1)S(1)}, u32[]{:S(2)}, u32[]{:S(2)}) collective-permute-start(bf16[768,768]{1,0:T(8,128)(2,1)S(1)} %get-tuple-element.257), channel_id=1, source_target_pairs={{0,16},{16,0},{1,17},{17,1},{2,18},{18,2},{3,19},{19,3},{4,20},{20... | collective-permute-start | bytes 3538952 | tf_op jit(solution)/shard_map/ppermute | solution.py:1091
  161.5 7.6 %collective-permute-start.45 = (bf16[416,768]{1,0:T(8,128)(2,1)S(1)}, bf16[416,768]{1,0:T(8,128)(2,1)S(1)}, u32[]{:S(2)}, u32[]{:S(2)}) collective-permute-start(bf16[416,768]{1,0:T(8,128)(2,1)S(1)} %get-tuple-element.249), channel_id=1, source_target_pairs={{0,4},{4,0},{8,12},{12,8},{1,5},{5,1},{9,13},{13,9},{2,6},{6,2},{1... | collective-permute-start | bytes 1916936 | tf_op jit(solution)/shard_map/ppermute | solution.py:904
  161.6 7.5 %collective-permute-start.42 = (bf16[192,256]{1,0:T(8,128)(2,1)S(1)}, bf16[192,256]{1,0:T(8,128)(2,1)S(1)}, u32[]{:S(2)}, u32[]{:S(2)}) collective-permute-start(bf16[192,256]{1,0:T(8,128)(2,1)S(1)} %get-tuple-element.240), channel_id=1, source_target_pairs={{0,1},{1,2},{2,3},{3,0},{4,5},{5,6},{6,7},{7,4},{8,9},{9,10},{10,1... | collective-permute-start | bytes 294920 | tf_op jit(solution)/shard_map/ppermute | solution.py:913
  161.7 10.8 %collective-permute-start.43 = (bf16[192,256]{1,0:T(8,128)(2,1)S(1)}, bf16[192,256]{1,0:T(8,128)(2,1)S(1)}, u32[]{:S(2)}, u32[]{:S(2)}) collective-permute-start(bf16[192,256]{1,0:T(8,128)(2,1)S(1)} %get-tuple-element.241), channel_id=1, source_target_pairs={{0,2},{1,3},{2,0},{3,1},{4,6},{5,7},{6,4},{7,5},{8,10},{9,11},{10,... | collective-permute-start | bytes 294920 | tf_op jit(solution)/shard_map/ppermute | solution.py:913
  163.6 8.9 %collective-permute-start.44 = (bf16[192,256]{1,0:T(8,128)(2,1)S(1)}, bf16[192,256]{1,0:T(8,128)(2,1)S(1)}, u32[]{:S(2)}, u32[]{:S(2)}) collective-permute-start(bf16[192,256]{1,0:T(8,128)(2,1)S(1)} %get-tuple-element.242), channel_id=1, source_target_pairs={{0,3},{1,0},{2,1},{3,2},{4,7},{5,4},{6,5},{7,6},{8,11},{9,8},{10,9... | collective-permute-start | bytes 294920 | tf_op jit(solution)/shard_map/ppermute | solution.py:913
  169.2 13.3 %collective-permute-start.47 = (bf16[224,768]{1,0:T(8,128)(2,1)S(1)}, bf16[224,768]{1,0:T(8,128)(2,1)S(1)}, u32[]{:S(2)}, u32[]{:S(2)}) collective-permute-start(bf16[224,768]{1,0:T(8,128)(2,1)S(1)} %far_message.1), channel_id=1, source_target_pairs={{0,8},{8,0},{4,12},{12,4},{1,9},{9,1},{5,13},{13,5},{2,10},{10,2},... | collective-permute-start | bytes 1032200 | tf_op jit(solution)/shard_map/ppermute | solution.py:908
  181.9 12.3 %collective-permute-start.49 = (bf16[512,384]{1,0:T(8,128)(2,1)S(1)}, bf16[512,384]{1,0:T(8,128)(2,1)S(1)}, u32[]{:S(2)}, u32[]{:S(2)}) collective-permute-start(bf16[512,384]{1,0:T(8,128)(2,1)S(1)} %get-tuple-element.265), channel_id=1, source_target_pairs={{0,4},{4,0},{8,12},{12,8},{1,5},{5,1},{9,13},{13,9},{2,6},{6,2},{1... | collective-permute-start | bytes 1179656 | tf_op jit(solution)/shard_map/ppermute | solution.py:904
  182.0 12.3 %collective-permute-start.48 = (bf16[512,384]{1,0:T(8,128)(2,1)S(1)}, bf16[512,384]{1,0:T(8,128)(2,1)S(1)}, u32[]{:S(2)}, u32[]{:S(2)}) collective-permute-start(bf16[512,384]{1,0:T(8,128)(2,1)S(1)} %get-tuple-element.263), channel_id=1, source_target_pairs={{0,4},{4,0},{8,12},{12,8},{1,5},{5,1},{9,13},{13,9},{2,6},{6,2},{1... | collective-permute-start | bytes 1179656 | tf_op jit(solution)/shard_map/ppermute | solution.py:904
  182.9 13.5 %collective-permute-start.50 = (bf16[272,768]{1,0:T(8,128)(2,1)S(1)}, bf16[272,768]{1,0:T(8,128)(2,1)S(1)}, u32[]{:S(2)}, u32[]{:S(2)}) collective-permute-start(bf16[272,768]{1,0:T(8,128)(2,1)S(1)} %get-tuple-element.267), channel_id=1, source_target_pairs={{0,1},{1,2},{2,3},{3,0},{4,5},{5,6},{6,7},{7,4},{8,9},{9,10},{10,1... | collective-permute-start | bytes 1253384 | tf_op jit(solution)/shard_map/ppermute | solution.py:913
  196.4 13.0 %collective-permute-start.51 = (bf16[272,768]{1,0:T(8,128)(2,1)S(1)}, bf16[272,768]{1,0:T(8,128)(2,1)S(1)}, u32[]{:S(2)}, u32[]{:S(2)}) collective-permute-start(bf16[272,768]{1,0:T(8,128)(2,1)S(1)} %sum_messages.3), channel_id=1, source_target_pairs={{0,1},{1,2},{2,3},{3,0},{4,5},{5,6},{6,7},{7,4},{8,9},{9,10},{10,1... | collective-permute-start | bytes 1253384 | tf_op jit(solution)/shard_map/ppermute | solution.py:913
  197.2 21.6 %collective-permute-start.54 = (bf16[1024,384]{1,0:T(8,128)(2,1)S(1)}, bf16[1024,384]{1,0:T(8,128)(2,1)S(1)}, u32[]{:S(2)}, u32[]{:S(2)}) collective-permute-start(bf16[1024,384]{1,0:T(8,128)(2,1)S(1)} %pad_maximum_fusion), channel_id=1, source_target_pairs={{0,8},{8,0},{4,12},{12,4},{1,9},{9,1},{5,13},{13,5},{2,10},{10,2},... | collective-permute-start | bytes 2359304 | tf_op jit(solution)/shard_map/ppermute | solution.py:908
  207.8 10.9 %collective-permute-start.52 = (bf16[512,384]{1,0:T(8,128)(2,1)S(1)}, bf16[512,384]{1,0:T(8,128)(2,1)S(1)}, u32[]{:S(2)}, u32[]{:S(2)}) collective-permute-start(bf16[512,384]{1,0:T(8,128)(2,1)S(1)} %get-tuple-element.275), channel_id=1, source_target_pairs={{0,4},{4,0},{8,12},{12,8},{1,5},{5,1},{9,13},{13,9},{2,6},{6,2},{1... | collective-permute-start | bytes 1179656 | tf_op jit(solution)/shard_map/ppermute | solution.py:904
  207.9 10.9 %collective-permute-start.53 = (bf16[512,384]{1,0:T(8,128)(2,1)S(1)}, bf16[512,384]{1,0:T(8,128)(2,1)S(1)}, u32[]{:S(2)}, u32[]{:S(2)}) collective-permute-start(bf16[512,384]{1,0:T(8,128)(2,1)S(1)} %get-tuple-element.276), channel_id=1, source_target_pairs={{0,4},{4,0},{8,12},{12,8},{1,5},{5,1},{9,13},{13,9},{2,6},{6,2},{1... | collective-permute-start | bytes 1179656 | tf_op jit(solution)/shard_map/ppermute | solution.py:904
  209.6 13.5 %collective-permute-start.56 = (bf16[272,768]{1,0:T(8,128)(2,1)S(1)}, bf16[272,768]{1,0:T(8,128)(2,1)S(1)}, u32[]{:S(2)}, u32[]{:S(2)}) collective-permute-start(bf16[272,768]{1,0:T(8,128)(2,1)S(1)} %sum_messages.4), channel_id=1, source_target_pairs={{0,1},{1,2},{2,3},{3,0},{4,5},{5,6},{6,7},{7,4},{8,9},{9,10},{10,1... | collective-permute-start | bytes 1253384 | tf_op jit(solution)/shard_map/ppermute | solution.py:913
  221.7 12.2 %collective-permute-start.55 = (bf16[256,768]{1,0:T(8,128)(2,1)}, bf16[256,768]{1,0:T(8,128)(2,1)}, u32[]{:S(2)}, u32[]{:S(2)}) collective-permute-start(bf16[256,768]{1,0:T(8,128)(2,1)} %get-tuple-element.282), channel_id=1, source_target_pairs={{0,1},{1,2},{2,3},{3,0},{4,5},{5,6},{6,7},{7,4},{8,9},{9,10},{10,1... | collective-permute-start | bytes 1179656 | tf_op jit(solution)/shard_map/ppermute | solution.py:913
  226.7 7.2 %collective-permute-start.57 = (bf16[208,576]{1,0:T(8,128)(2,1)}, bf16[208,576]{1,0:T(8,128)(2,1)S(1)}, u32[]{:S(2)}, u32[]{:S(2)}) collective-permute-start(bf16[208,576]{1,0:T(8,128)(2,1)} %get-tuple-element.289), channel_id=1, source_target_pairs={{0,4},{4,0},{8,12},{12,8},{1,5},{5,1},{9,13},{13,9},{2,6},{6,2},{1... | collective-permute-start | bytes 718856 | tf_op jit(solution)/shard_map/ppermute | solution.py:904
  226.7 7.2 %collective-permute-start.58 = (bf16[192,576]{1,0:T(8,128)(2,1)}, bf16[192,576]{1,0:T(8,128)(2,1)}, u32[]{:S(2)}, u32[]{:S(2)}) collective-permute-start(bf16[192,576]{1,0:T(8,128)(2,1)} %get-tuple-element.290), channel_id=1, source_target_pairs={{0,4},{4,0},{8,12},{12,8},{1,5},{5,1},{9,13},{13,9},{2,6},{6,2},{1... | collective-permute-start | bytes 663560 | tf_op jit(solution)/shard_map/ppermute | solution.py:904
  235.6 6.5 %collective-permute-start.61 = (bf16[208,576]{1,0:T(8,128)(2,1)S(1)}, bf16[208,576]{1,0:T(8,128)(2,1)S(1)}, u32[]{:S(2)}, u32[]{:S(2)}) collective-permute-start(bf16[208,576]{1,0:T(8,128)(2,1)S(1)} %pad_maximum_fusion.2), channel_id=1, source_target_pairs={{0,8},{8,0},{4,12},{12,4},{1,9},{9,1},{5,13},{13,5},{2,10},{10,2},... | collective-permute-start | bytes 718856 | tf_op jit(solution)/shard_map/ppermute | solution.py:908
  237.9 10.5 %collective-permute-start.59 = (bf16[256,768]{1,0:T(8,128)(2,1)S(1)}, bf16[256,768]{1,0:T(8,128)(2,1)S(1)}, u32[]{:S(2)}, u32[]{:S(2)}) collective-permute-start(bf16[256,768]{1,0:T(8,128)(2,1)S(1)} %add_convert_fusion.1), channel_id=1, source_target_pairs={{0,1},{1,2},{2,3},{3,0},{4,5},{5,6},{6,7},{7,4},{8,9},{9,10},{10,1... | collective-permute-start | bytes 1179656 | tf_op jit(solution)/shard_map/ppermute | solution.py:913
  238.2 12.5 %collective-permute-start.66 = (bf16[272,768]{1,0:T(8,128)(2,1)S(1)}, bf16[272,768]{1,0:T(8,128)(2,1)S(1)}, u32[]{:S(2)}, u32[]{:S(2)}) collective-permute-start(bf16[272,768]{1,0:T(8,128)(2,1)S(1)} %sum_messages.5.own), channel_id=1, source_target_pairs={{0,16},{16,0},{1,17},{17,1},{2,18},{18,2},{3,19},{19,3},{4,20},{20... | collective-permute-start | bytes 1253384 | tf_op jit(solution)/shard_map/ppermute | solution.py:1143
  242.3 13.6 %collective-permute-start.62 = (bf16[208,576]{1,0:T(8,128)(2,1)S(1)}, bf16[208,576]{1,0:T(8,128)(2,1)S(1)}, u32[]{:S(2)}, u32[]{:S(2)}) collective-permute-start(bf16[208,576]{1,0:T(8,128)(2,1)S(1)} %pad_maximum_fusion.3), channel_id=1, source_target_pairs={{0,16},{16,0},{1,17},{17,1},{2,18},{18,2},{3,19},{19,3},{4,20},{20... | collective-permute-start | bytes 718856 | tf_op jit(solution)/shard_map/ppermute | solution.py:1162
  248.5 18.3 %collective-permute-start.60 = (bf16[256,768]{1,0:T(8,128)(2,1)S(1)}, bf16[256,768]{1,0:T(8,128)(2,1)S(1)}, u32[]{:S(2)}, u32[]{:S(2)}) collective-permute-start(bf16[256,768]{1,0:T(8,128)(2,1)S(1)} %add_convert_fusion), channel_id=1, source_target_pairs={{0,1},{1,2},{2,3},{3,0},{4,5},{5,6},{6,7},{7,4},{8,9},{9,10},{10,1... | collective-permute-start | bytes 1179656 | tf_op jit(solution)/shard_map/ppermute | solution.py:913
  252.8 6.0 %collective-permute-start.67 = (bf16[192,192]{1,0:T(8,128)(2,1)S(1)}, bf16[192,192]{1,0:T(8,128)(2,1)S(1)}, u32[]{:S(2)}, u32[]{:S(2)}) collective-permute-start(bf16[192,192]{1,0:T(8,128)(2,1)S(1)} %get-tuple-element.307), channel_id=1, source_target_pairs={{0,4},{4,0},{8,12},{12,8},{1,5},{5,1},{9,13},{13,9},{2,6},{6,2},{1... | collective-permute-start | bytes 221192 | tf_op jit(solution)/shard_map/ppermute | solution.py:904
  252.8 7.5 %collective-permute-start.68 = (bf16[192,192]{1,0:T(8,128)(2,1)S(1)}, bf16[192,192]{1,0:T(8,128)(2,1)S(1)}, u32[]{:S(2)}, u32[]{:S(2)}) collective-permute-start(bf16[192,192]{1,0:T(8,128)(2,1)S(1)} %get-tuple-element.308), channel_id=1, source_target_pairs={{0,8},{8,0},{4,12},{12,4},{1,9},{9,1},{5,13},{13,5},{2,10},{10,2},... | collective-permute-start | bytes 221192 | tf_op jit(solution)/shard_map/ppermute | solution.py:908
  254.2 7.5 %collective-permute-start.69 = (bf16[192,192]{1,0:T(8,128)(2,1)S(1)}, bf16[192,192]{1,0:T(8,128)(2,1)S(1)}, u32[]{:S(2)}, u32[]{:S(2)}) collective-permute-start(bf16[192,192]{1,0:T(8,128)(2,1)S(1)} %get-tuple-element.309), channel_id=1, source_target_pairs={{0,12},{4,8},{8,4},{12,0},{1,13},{5,9},{9,5},{13,1},{2,14},{6,10},... | collective-permute-start | bytes 221192 | tf_op jit(solution)/shard_map/ppermute | solution.py:1179
  256.1 7.1 %collective-permute-start.63 = (bf16[48,576]{1,0:T(8,128)(2,1)S(1)}, bf16[48,576]{1,0:T(8,128)(2,1)S(1)}, u32[]{:S(2)}, u32[]{:S(2)}) collective-permute-start(bf16[48,576]{1,0:T(8,128)(2,1)S(1)} %get-tuple-element.321), channel_id=1, source_target_pairs={{0,1},{1,2},{2,3},{3,0},{4,5},{5,6},{6,7},{7,4},{8,9},{9,10},{10,1... | collective-permute-start | bytes 165896 | tf_op jit(solution)/shard_map/ppermute | solution.py:913
  258.8 6.4 %collective-permute-start.64 = (bf16[48,576]{1,0:T(8,128)(2,1)S(1)}, bf16[48,576]{1,0:T(8,128)(2,1)S(1)}, u32[]{:S(2)}, u32[]{:S(2)}) collective-permute-start(bf16[48,576]{1,0:T(8,128)(2,1)S(1)} %get-tuple-element.320), channel_id=1, source_target_pairs={{0,2},{1,3},{2,0},{3,1},{4,6},{5,7},{6,4},{7,5},{8,10},{9,11},{10,... | collective-permute-start | bytes 165896 | tf_op jit(solution)/shard_map/ppermute | solution.py:913
  260.3 5.1 %collective-permute-start.65 = (bf16[48,576]{1,0:T(8,128)(2,1)S(1)}, bf16[48,576]{1,0:T(8,128)(2,1)S(1)}, u32[]{:S(2)}, u32[]{:S(2)}) collective-permute-start(bf16[48,576]{1,0:T(8,128)(2,1)S(1)} %get-tuple-element.319), channel_id=1, source_target_pairs={{0,3},{1,0},{2,1},{3,2},{4,7},{5,4},{6,5},{7,6},{8,11},{9,8},{10,9... | collective-permute-start | bytes 165896 | tf_op jit(solution)/shard_map/ppermute | solution.py:913
  (33 other events, 221.7 us)
where the time goes:
time: 273 us; the launch traced here: 268 us
  waiting for transfers between devices  96.7 us (35%)
  Pallas kernels  90.9 us (33%)
  starting transfers between devices  62.4 us (23%)
  local copies, waits for them, and re-layouts  7.98 us (3%)
  other arithmetic  7.69 us (3%)
    ppermute x24, waiting for transfers between devices, shift_col(): return lax.ppermute(x, 'col', [(i, (i + step) % n) for i in range(n)])  55.1 us
    pallas_call x4, Pallas kernels, attn_bwd(): pl.pallas_call(functools.partial(attn_bwd_kernel, heads=heads, block=bloc...  36.4 us
    ppermute x13, waiting for transfers between devices, cross_swap(): return lax.ppermute(x, 'row', CROSS)  31.7 us
    pallas_call x15, Pallas kernels, meta_call(): pl.pallas_call(kernel, in_specs=[pl.BlockSpec(memory_space=pltpu.SMEM)] +...  29.7 us
    ppermute x24, starting transfers between devices, shift_col(): return lax.ppermute(x, 'col', [(i, (i + step) % n) for i in range(n)])  29.6 us
    pallas_call x2, Pallas kernels, attn_fwd(): pl.pallas_call(functools.partial(attn_fwd_kernel, heads=heads, first=firs...  20.4 us
    ppermute x13, starting transfers between devices, cross_swap(): return lax.ppermute(x, 'row', CROSS)  17.6 us
  transfers between devices with their start and end apart: 70, of which 29 were waited for; matrix products, arithmetic and copies ran while one was open for 3% of the time, Pallas kernels for 31%

commit v1 on v0

--- a/solution.py
+++ b/solution.py
@@ -232,7 +232,7 @@
         out[:, width:] = dv[at, :width].astype(out.dtype)
 
 
-def attn_bwd(at, q, g, k, v, dq, heads, us, pieces=2, block=512):
+def attn_bwd(at, q, g, k, v, dq, heads, us, pieces=2, block=1024):
     rows = q.shape[0]
     half = k.shape[0] // 2
     width = heads * HD
@@ -792,7 +792,7 @@
     rows = dq.shape[0]
     wide, width = w.shape
     shapes = [jax.ShapeDtypeStruct((rows // n, wide), BF)] * n
-    shapes += [jax.ShapeDtypeStruct((rows // n, width), BF if k == 1 else F32) for k in range(n)]
+    shapes += [jax.ShapeDtypeStruct((rows // n, width), BF)] * n
     kernel = functools.partial(join_kernel, scale=scale, hw=wide // 3)
     out = small_call(kernel, shapes, "join_grads")(*keep, *near, far, dq, w)
     return out[:n], out[n:]
@@ -981,7 +981,7 @@
     meta = jnp.stack([lengths[0], r, z * (local * rows_n) + r * local, z, pair]).astype(jnp.int32)
 
     sub_out = out_weight.shape[0]
-    x_blocks = [jnp.concatenate([tokens, out_weight.astype(BF)])]
+    x_blocks = [jnp.concatenate([tokens.astype(F32), out_weight]).astype(BF)]
     x_blocks.append(shift_col(x_blocks[0], 1))
 
     up_t = up_weight.astype(BF).T
@@ -1014,7 +1014,8 @@
         return lax.ppermute(x, "dp", [(0, 1), (1, 0)]) if paired else x[:1]
 
     pack, half = pack_weights(meta, up_blocks, down_weight, bias_rows)
-    hops = [shift_col(after(half if paired else pack, x_blocks[-1]), 1)]
+    half = after(half if paired else pack, x_blocks[-1])
+    hops = [shift_col(half, 1)]
 
     qkv_bias = jnp.concatenate([query_bias, jnp.zeros_like(value_bias), value_bias])
     qkv_bias = jnp.broadcast_to(qkv_bias[None], (8, 3 * hw))
@@ -1034,8 +1035,8 @@
     acc, stat, k_near, v_near = attn_fwd(
         meta, q_parts, [kv_a, kv_b, near_a, near_b], (0, 1), heads, local, sizes, NEAR_COST
     )
-    stat, hops[0] = lax.optimization_barrier((stat, hops[0]))
-    hops.append(shift_col(hops[0], 1))
+    stat, hops[0], half = lax.optimization_barrier((stat, hops[0], half))
+    hops += [shift_col(hops[0], 1), shift_col(half, -1)]
     crossed = [cross_dp(hops[0])]
     stat, far_a, far_b, out_pack = lax.optimization_barrier((stat, far_a, far_b, out_pack))
     out_far, out_near = cross_swap(out_pack), core_swap(out_pack)
@@ -1044,17 +1045,15 @@
     *mixed_part, qb_rows, k_far, v_far = attn_fwd(
         meta, q_parts, far, (2, 3), heads, local, sizes, 4, state=state
     )
-    *mixed_part, second, third, out_far, qb_rows = lax.optimization_barrier(
-        (*mixed_part, hops[1], crossed[0], out_far, qb_rows)
-    )
-    hops[1], crossed[0] = second, third
-    crossed.append(cross_dp(hops[1]))
+    *mixed_part, second, third, first, out_far, qb_rows = lax.optimization_barrier(
+        (*mixed_part, hops[1], hops[2], crossed[0], out_far, qb_rows)
+    )
+    hops[1:] = [second, third]
+    crossed = [first, cross_dp(second), cross_dp(third)]
     mixed = [mixed_part[0]] + [shift_col(mixed_part[k], -k) for k in range(1, cols_n)]
 
     out_packs = [out_pack, out_near, out_far, core_swap(out_far)]
-    *mixed, third, crossed[1] = lax.optimization_barrier((*mixed, hops[1], crossed[1]))
-    hops.append(shift_col(third, 1))
-    crossed.append(cross_dp(hops[2]))
+    *mixed, crossed[1] = lax.optimization_barrier((*mixed, crossed[1]))
     packs = [pack]
     for hop, other in zip(hops, crossed):
         packs += [hop, other] if paired else [hop]
@@ -1135,7 +1134,7 @@
     got, got_far = core_swap(send), core_swap(send_far)
     ring[0], got, got_far, packed = lax.optimization_barrier((ring[0], got, got_far, packed))
     for step in range(2, cols_n + 1):
-        total = back[step % cols_n] + ring[-1].astype(F32)
+        total = back[step % cols_n].astype(F32) + ring[-1].astype(F32)
         if step < cols_n:
             ring.append(shift_col(total.astype(BF), 1))
     grad_tokens = grad_resid1 + total

time: 273 us -> 270 us (0.989)
    ppermute x3, waiting for transfers between devices: 2.97 us -> 9.1 us  [cross_dp(): return lax.ppermute(x, 'dp', [(0, 1), (1, 0)]) if paired else x[:1]]
    ppermute x24, waiting for transfers between devices: 55.1 us -> 49.7 us  [shift_col(): return lax.ppermute(x, 'col', [(i, (i + step) % n) for i in range(n)])]
    ppermute x24, starting transfers between devices: 29.6 us -> 33.6 us  [shift_col(): return lax.ppermute(x, 'col', [(i, (i + step) % n) for i in range(n)])]
  transfers between devices with their start and end apart: 70 -> 70, of which waited for: 29 -> 30; matrix products, arithmetic and copies ran while one was open for 3% -> 3% of each run, Pallas kernels for 31% -> 31%
where the time goes in v1:
time: 270 us; the launch traced here: 265 us
  waiting for transfers between devices  97.1 us (36%)
  Pallas kernels  89.1 us (33%)
  starting transfers between devices  62.8 us (23%)
  other arithmetic  6.81 us (3%)
  local copies, waits for them, and re-layouts  6.41 us (2%)
    ppermute x24, waiting for transfers between devices, shift_col(): return lax.ppermute(x, 'col', [(i, (i + step) % n) for i in range(n)])  49.7 us
    pallas_call x4, Pallas kernels, attn_bwd(): pl.pallas_call(functools.partial(attn_bwd_kernel, heads=heads, block=bloc...  34.4 us
    ppermute x24, starting transfers between devices, shift_col(): return lax.ppermute(x, 'col', [(i, (i + step) % n) for i in range(n)])  33.6 us
    ppermute x13, waiting for transfers between devices, cross_swap(): return lax.ppermute(x, 'row', CROSS)  31.4 us
    pallas_call x15, Pallas kernels, meta_call(): pl.pallas_call(kernel, in_specs=[pl.BlockSpec(memory_space=pltpu.SMEM)] +...  29.9 us
    pallas_call x2, Pallas kernels, attn_fwd(): pl.pallas_call(functools.partial(attn_fwd_kernel, heads=heads, first=firs...  20.4 us
    ppermute x13, starting transfers between devices, cross_swap(): return lax.ppermute(x, 'row', CROSS)  18 us
    ppermute x3, waiting for transfers between devices, cross_dp(): return lax.ppermute(x, 'dp', [(0, 1), (1, 0)]) if paired else x[:1]  9.1 us
  transfers between devices with their start and end apart: 70, of which 30 were waited for; matrix products, arithmetic and copies ran while one was open for 3% of the time, Pallas kernels for 31%

profile of v1, /device:TPU:0, one launch (start us, length us, event | category | flops | bytes accessed | tf_op | source)
XLA Modules:
  0.0 264.7 jit_solution(11022867072182650164)
XLA Ops:
  2.7 3.1 %collective-permute-start = (bf16[304,768]{1,0:T(8,128)(2,1)S(1)}, bf16[304,768]{1,0:T(8,128)(2,1)S(1)}, u32[]{:S(2)}, u32[]{:S(2)}) collective-permute-start(bf16[304,768]{1,0:T(8,128)(2,1)S(1)} %pad_maximum_fusion.1.refs_0_), channel_id=1, source_target_pairs={{0,1},{1,2},{2,3},{3,0},{4,5},{5,6},{6,7},{7,4},{8,9},{9,10},{10,1... | collective-permute-start | bytes 1400840 | tf_op jit(solution)/shard_map/ppermute | solution.py:913
  7.9 1.6 collective-permute-start.1
  10.6 2.8 %collective-permute-start.3 = (bf16[48,576]{1,0:T(8,128)(2,1)S(1)}, bf16[48,576]{1,0:T(8,128)(2,1)S(1)}, u32[]{:S(2)}, u32[]{:S(2)}) collective-permute-start(bf16[48,576]{1,0:T(8,128)(2,1)S(1)} %get-tuple-element.325), channel_id=1, source_target_pairs={{0,3},{1,0},{2,1},{3,2},{4,7},{5,4},{6,5},{7,6},{8,11},{9,8},{10,9... | collective-permute-start | bytes 165896 | tf_op jit(solution)/shard_map/ppermute | solution.py:913
  13.8 7.0 %collective-permute-done.1 = bf16[48,576]{1,0:T(8,128)(2,1)S(1)} collective-permute-done((bf16[48,576]{1,0:T(8,128)(2,1)S(1)}, bf16[48,576]{1,0:T(8,128)(2,1)S(1)}, u32[]{:S(2)}, u32[]{:S(2)}) %collective-permute-start.1) | collective-permute-done | bytes 55328 | tf_op jit(solution)/shard_map/ppermute | solution.py:913
  20.8 1.8 collective-permute-done.2
  22.6 1.8 collective-permute-start.7
  24.5 1.6 collective-permute-start.5
  27.9 5.4 %collective-permute-done.5.refs_4_.refs_6_ = bf16[192,576]{1,0:T(8,128)(2,1)S(1)} collective-permute-done((bf16[192,576]{1,0:T(8,128)(2,1)S(1)}, bf16[192,576]{1,0:T(8,128)(2,1)S(1)}, u32[]{:S(2)}, u32[]{:S(2)}) %collective-permute-start.5) | collective-permute-done | bytes 221216 | tf_op jit(solution)/shard_map/ppermute | solution.py:908
  33.2 1.7 collective-permute-start.12
  34.9 2.1 collective-permute-done.7.refs_2_
  37.1 1.5 project_qkv.2
  40.3 1.6 collective-permute-start.14
  41.9 8.6 %collective-permute-done.8.refs_3_ = bf16[304,768]{1,0:T(8,128)(2,1)S(1)} collective-permute-done((bf16[304,768]{1,0:T(8,128)(2,1)S(1)}, bf16[304,768]{1,0:T(8,128)(2,1)S(1)}, u32[]{:S(2)}, u32[]{:S(2)}) %collective-permute-start.8) | collective-permute-done | bytes 466976 | tf_op jit(solution)/shard_map/ppermute | solution.py:913
  50.5 1.5 project_qkv.3
  52.1 1.6 collective-permute-start.16
  54.1 9.9 %attn_fwd_near.1 = (f32[192,1024]{1,0:T(8,128)S(1)}, f32[16,1024]{1,0:T(8,128)S(1)}, bf16[2048,256]{1,0:T(8,128)(2,1)S(1)}, bf16[2048,256]{1,0:T(8,128)(2,1)S(1)}) custom-call(s32[5]{0:T(128)S(1)} %stack.82.meta.refs_0_, bf16[512,256]{1,0:T(8,128)(2,1)S(1)} %get-tuple-element.169.refs_1_, bf16[512,256]{1,0:T(8,128)(2,1)S(1)} %get-tuple-element.174.refs_2_, ...), custom_call_target="tpu_custom_call" | custom-call | flops 2400000000 | bytes 1000 | tf_op jit(solution)/shard_map/attn_fwd_near/pallas_call | solution.py:156
  66.5 4.0 %collective-permute-start.20 = (bf16[208,768]{1,0:T(8,128)(2,1)S(1)}, bf16[208,768]{1,0:T(8,128)(2,1)S(1)}, u32[]{:S(2)}, u32[]{:S(2)}) collective-permute-start(bf16[208,768]{1,0:T(8,128)(2,1)S(1)} %get-tuple-element.193), channel_id=1, source_target_pairs={{0,3},{1,0},{2,1},{3,2},{4,7},{5,4},{6,5},{7,6},{8,11},{9,8},{10,9... | collective-permute-start | bytes 958472 | tf_op jit(solution)/shard_map/ppermute | solution.py:913
  70.5 1.5 collective-permute-start.21
  72.0 10.5 %attn_fwd_far.1 = (bf16[192,256]{1,0:T(8,128)(2,1)S(1)}, bf16[192,256]{1,0:T(8,128)(2,1)S(1)}, bf16[192,256]{1,0:T(8,128)(2,1)S(1)}, bf16[192,256]{1,0:T(8,128)(...) custom-call(s32[5]{0:T(128)S(1)} %stack.82.meta.refs_0_, ...), custom_call_target="tpu_custom_call" | custom-call | flops 2400000000 | bytes 1000 | tf_op jit(solution)/shard_map/attn_fwd_far/pallas_call | solution.py:156
  84.3 2.4 collective-permute-start.23
  87.4 2.6 collective-permute-done.23.refs_1_
  91.3 4.2 %collective-permute-done.24.refs_2_ = bf16[192,256]{1,0:T(8,128)(2,1)S(1)} collective-permute-done((bf16[192,256]{1,0:T(8,128)(2,1)S(1)}, bf16[192,256]{1,0:T(8,128)(2,1)S(1)}, u32[]{:S(2)}, u32[]{:S(2)}) %collective-permute-start.24) | collective-permute-done | bytes 98336 | tf_op jit(solution)/shard_map/ppermute | solution.py:913
  95.5 1.6 collective-permute-done.25.refs_3_
  98.6 1.6 collective-permute-start.30
  100.7 9.1 %collective-permute-done.31.refs_8_ = bf16[208,768]{1,0:T(8,128)(2,1)S(1)} collective-permute-done((bf16[208,768]{1,0:T(8,128)(2,1)S(1)}, bf16[208,768]{1,0:T(8,128)(2,1)S(1)}, u32[]{:S(2)}, u32[]{:S(2)}) %collective-permute-start.31) | collective-permute-done | bytes 319520 | tf_op jit(solution)/shard_map/ppermute | solution.py:1014
  110.2 1.7 collective-permute-done.33.refs_1_.refs_7_
  111.9 2.6 ffn_fwd.3
  114.6 2.6 ffn_fwd.2
  117.8 1.6 collective-permute-start.35
  119.3 9.7 %collective-permute-done.35.far_ref = bf16[256,768]{1,0:T(8,128)(2,1)S(1)} collective-permute-done((bf16[256,768]{1,0:T(8,128)(2,1)S(1)}, bf16[256,768]{1,0:T(8,128)(2,1)S(1)}, u32[]{:S(2)}, u32[]{:S(2)}) %collective-permute-start.35) | collective-permute-done | bytes 393248 | tf_op jit(solution)/shard_map/ppermute | solution.py:908
  129.0 2.0 norm2_both.1
  131.0 1.5 collective-permute-start.37
  132.7 2.2 ffn_bwd.2
  134.9 7.6 %collective-permute-done.37.refs_0_.refs_10_ = bf16[256,768]{1,0:T(8,128)(2,1)S(1)} collective-permute-done((bf16[256,768]{1,0:T(8,128)(2,1)S(1)}, bf16[256,768]{1,0:T(8,128)(2,1)S(1)}, u32[]{:S(2)}, u32[]{:S(2)}) %collective-permute-start.37) | collective-permute-done | bytes 393248 | tf_op jit(solution)/shard_map/ppermute | solution.py:908
  142.5 1.7 collective-permute-done.38.refs_1_.refs_11_
  144.2 2.2 ffn_bwd.3
  148.3 1.6 collective-permute-start.41
  149.8 4.1 %ffn_grads.1 = (bf16[768,768]{1,0:T(8,128)(2,1)S(1)}, bf16[768,768]{1,0:T(8,128)(2,1)S(1)}, f32[8,768]{1,0:T(8,128)S(1)}) custom-call(s32[5]{0:T(128)S(1)} %stack.82.meta.refs_0_, bf16[512,768]{1,0:T(8,128)(2,1)S(1)} %get-tuple-element.224.refs_0_, bf16[512,768]{1,0:T(8,128)(2,1)S(1)} %get-tuple-element.225.refs_1_, ...), custom_call_target="tpu_custom_call" | custom-call | flops 720000000 | bytes 1000 | tf_op jit(solution)/shard_map/ffn_grads/pallas_call | solution.py:266
  154.5 5.0 %collective-permute-done.41.far_ref = bf16[256,768]{1,0:T(8,128)(2,1)S(1)} collective-permute-done((bf16[256,768]{1,0:T(8,128)(2,1)S(1)}, bf16[256,768]{1,0:T(8,128)(2,1)S(1)}, u32[]{:S(2)}, u32[]{:S(2)}) %collective-permute-start.41) | collective-permute-done | bytes 393248 | tf_op jit(solution)/shard_map/ppermute | solution.py:908
  162.0 2.8 %collective-permute-start.43 = (bf16[192,256]{1,0:T(8,128)(2,1)S(1)}, bf16[192,256]{1,0:T(8,128)(2,1)S(1)}, u32[]{:S(2)}, u32[]{:S(2)}) collective-permute-start(bf16[192,256]{1,0:T(8,128)(2,1)S(1)} %get-tuple-element.243), channel_id=1, source_target_pairs={{0,2},{1,3},{2,0},{3,1},{4,6},{5,7},{6,4},{7,5},{8,10},{9,11},{10,... | collective-permute-start | bytes 294920 | tf_op jit(solution)/shard_map/ppermute | solution.py:913
  164.8 1.9 collective-permute-start.44
  166.8 2.8 %collective-permute-done.42.refs_5_ = bf16[192,256]{1,0:T(8,128)(2,1)S(1)} collective-permute-done((bf16[192,256]{1,0:T(8,128)(2,1)S(1)}, bf16[192,256]{1,0:T(8,128)(2,1)S(1)}, u32[]{:S(2)}, u32[]{:S(2)}) %collective-permute-start.42) | collective-permute-done | bytes 98336 | tf_op jit(solution)/shard_map/ppermute | solution.py:913
  169.6 1.6 collective-permute-start.47
  171.2 1.7 collective-permute-done.43.refs_6_
  173.2 8.6 %attn_bwd.4 = (bf16[512,384]{1,0:T(8,128)(2,1)S(1)}, bf16[512,384]{1,0:T(8,128)(2,1)S(1)}, f32[1024,256]{1,0:T(8,128)S(1)}) custom-call(s32[1]{0:T(128)} %constant.102.clone.1.at_ref, bf16[1024,256]{1,0:T(8,128)(2,1)S(1)} %get-tuple-element.240.q_ref, bf16[1024,256]{1,0:T(8,128)(2,1)S(1)} %grad_rows.1.g_ref, bf16[2048,256]{1,0:T(8,128)(2,1)S(1)} %get-tuple-element.256.k_ref, ...), custom_call_target="tpu_custom_call" | custom-call | flops 2400000000 | bytes 1000 | tf_op jit(solution)/shard_map/attn_bwd/pallas_call | solution.py:241
  182.8 2.3 collective-permute-start.50
  185.1 8.6 %attn_bwd.5 = (bf16[512,384]{1,0:T(8,128)(2,1)S(1)}, bf16[512,384]{1,0:T(8,128)(2,1)S(1)}, f32[1024,256]{1,0:T(8,128)S(1)}) custom-call(s32[1]{0:T(128)} %constant.101.clone.1.at_ref, bf16[1024,256]{1,0:T(8,128)(2,1)S(1)} %get-tuple-element.240.q_ref, bf16[1024,256]{1,0:T(8,128)(2,1)S(1)} %grad_rows.1.g_ref, bf16[2048,256]{1,0:T(8,128)(2,1)S(1)} %get-tuple-element.256.k_ref, ...), custom_call_target="tpu_custom_call" | custom-call | flops 2400000000 | bytes 1000 | tf_op jit(solution)/shard_map/attn_bwd/pallas_call | solution.py:241
  194.0 2.4 collective-permute-done.50.refs_1_
  197.1 1.5 collective-permute-start.54
  198.6 8.6 %attn_bwd.6 = (bf16[512,384]{1,0:T(8,128)(2,1)S(1)}, bf16[512,384]{1,0:T(8,128)(2,1)S(1)}, f32[1024,256]{1,0:T(8,128)S(1)}) custom-call(s32[1]{0:T(128)} %constant.102.clone.1.at_ref, bf16[1024,256]{1,0:T(8,128)(2,1)S(1)} %get-tuple-element.240.q_ref, bf16[1024,256]{1,0:T(8,128)(2,1)S(1)} %grad_rows.1.g_ref, bf16[2048,256]{1,0:T(8,128)(2,1)S(1)} %get-tuple-element.254.k_ref, ...), custom_call_target="tpu_custom_call" | custom-call | flops 2400000000 | bytes 1000 | tf_op jit(solution)/shard_map/attn_bwd/pallas_call | solution.py:241
  207.8 1.6 collective-permute-done.51.refs_1_
  209.8 8.6 %attn_bwd.7 = (bf16[512,384]{1,0:T(8,128)(2,1)S(1)}, bf16[512,384]{1,0:T(8,128)(2,1)S(1)}, f32[1024,256]{1,0:T(8,128)S(1)}) custom-call(s32[1]{0:T(128)} %constant.101.clone.1.at_ref, bf16[1024,256]{1,0:T(8,128)(2,1)S(1)} %get-tuple-element.240.q_ref, bf16[1024,256]{1,0:T(8,128)(2,1)S(1)} %grad_rows.1.g_ref, bf16[2048,256]{1,0:T(8,128)(2,1)S(1)} %get-tuple-element.254.k_ref, ...), custom_call_target="tpu_custom_call" | custom-call | flops 3600000000 | bytes 1000 | tf_op jit(solution)/shard_map/attn_bwd/pallas_call | solution.py:241
  218.5 2.1 join_grads.1
  222.4 2.8 %qkv_grads.1 = (f32[208,576]{1,0:T(8,128)S(1)}, f32[192,576]{1,0:T(8,128)S(1)}, bf16[208,576]{1,0:T(8,128)(2,1)S(1)}, bf16[192,576]{1,0:T(8,128)(2,1)}) custom-call(s32[5]{0:T(128)S(1)} %stack.82.meta.refs_0_, bf16[304,768]{1,0:T(8,128)(2,1)S(1)} %pad_maximum_fusion.1.refs_0_, bf16[304,768]{1,0:T(8,128)(2,1)S(1)} %collective-permute-done.refs_1_, ...), custom_call_target="tpu_custom_call" | custom-call | flops 720000000 | bytes 1000 | tf_op jit(solution)/shard_map/qkv_grads/pallas_call | solution.py:266
  227.9 4.3 %collective-permute-done.55 = bf16[256,768]{1,0:T(8,128)(2,1)} collective-permute-done((bf16[256,768]{1,0:T(8,128)(2,1)}, bf16[256,768]{1,0:T(8,128)(2,1)}, u32[]{:S(2)}, u32[]{:S(2)}) %collective-permute-start.55) | collective-permute-done | bytes 393248 | tf_op jit(solution)/shard_map/ppermute | solution.py:913
  235.5 3.3 %collective-permute-done.61 = bf16[208,576]{1,0:T(8,128)(2,1)S(1)} collective-permute-done((bf16[208,576]{1,0:T(8,128)(2,1)S(1)}, bf16[208,576]{1,0:T(8,128)(2,1)S(1)}, u32[]{:S(2)}, u32[]{:S(2)}) %collective-permute-start.61) | collective-permute-done | bytes 239648 | tf_op jit(solution)/shard_map/ppermute | solution.py:908
  239.6 5.2 %collective-permute-done.59 = bf16[256,768]{1,0:T(8,128)(2,1)S(1)} collective-permute-done((bf16[256,768]{1,0:T(8,128)(2,1)S(1)}, bf16[256,768]{1,0:T(8,128)(2,1)S(1)}, u32[]{:S(2)}, u32[]{:S(2)}) %collective-permute-start.59) | collective-permute-done | bytes 393248 | tf_op jit(solution)/shard_map/ppermute | solution.py:913
  245.0 2.0 collective-permute-done.66.other
  247.0 2.2 finish_grads.1
  249.2 1.6 collective-permute-start.68
  252.5 2.4 collective-permute-start.63
  256.7 1.6 collective-permute-start.65
  258.4 1.5 up_grads.1
  259.9 2.0 collective-permute-done.64.refs_2_
  (215 shorter events, 41.5 us)
Async XLA Ops:
  2.7 19.9 %collective-permute-start = (bf16[304,768]{1,0:T(8,128)(2,1)S(1)}, bf16[304,768]{1,0:T(8,128)(2,1)S(1)}, u32[]{:S(2)}, u32[]{:S(2)}) collective-permute-start(bf16[304,768]{1,0:T(8,128)(2,1)S(1)} %pad_maximum_fusion.1.refs_0_), channel_id=1, source_target_pairs={{0,1},{1,2},{2,3},{3,0},{4,5},{5,6},{6,7},{7,4},{8,9},{9,10},{10,1... | collective-permute-start | bytes 1400840 | tf_op jit(solution)/shard_map/ppermute | solution.py:913
  7.9 12.9 %collective-permute-start.1 = (bf16[48,576]{1,0:T(8,128)(2,1)S(1)}, bf16[48,576]{1,0:T(8,128)(2,1)S(1)}, u32[]{:S(2)}, u32[]{:S(2)}) collective-permute-start(bf16[48,576]{1,0:T(8,128)(2,1)S(1)} %get-tuple-element.327), channel_id=1, source_target_pairs={{0,1},{1,2},{2,3},{3,0},{4,5},{5,6},{6,7},{7,4},{8,9},{9,10},{10,1... | collective-permute-start | bytes 165896 | tf_op jit(solution)/shard_map/ppermute | solution.py:913
  9.5 13.1 %collective-permute-start.2 = (bf16[48,576]{1,0:T(8,128)(2,1)S(1)}, bf16[48,576]{1,0:T(8,128)(2,1)S(1)}, u32[]{:S(2)}, u32[]{:S(2)}) collective-permute-start(bf16[48,576]{1,0:T(8,128)(2,1)S(1)} %get-tuple-element.326), channel_id=1, source_target_pairs={{0,2},{1,3},{2,0},{3,1},{4,6},{5,7},{6,4},{7,5},{8,10},{9,11},{10,... | collective-permute-start | bytes 165896 | tf_op jit(solution)/shard_map/ppermute | solution.py:913
  10.6 12.0 %collective-permute-start.3 = (bf16[48,576]{1,0:T(8,128)(2,1)S(1)}, bf16[48,576]{1,0:T(8,128)(2,1)S(1)}, u32[]{:S(2)}, u32[]{:S(2)}) collective-permute-start(bf16[48,576]{1,0:T(8,128)(2,1)S(1)} %get-tuple-element.325), channel_id=1, source_target_pairs={{0,3},{1,0},{2,1},{3,2},{4,7},{5,4},{6,5},{7,6},{8,11},{9,8},{10,9... | collective-permute-start | bytes 165896 | tf_op jit(solution)/shard_map/ppermute | solution.py:913
  22.6 14.4 %collective-permute-start.7 = (bf16[304,768]{1,0:T(8,128)(2,1)S(1)}, bf16[304,768]{1,0:T(8,128)(2,1)S(1)}, u32[]{:S(2)}, u32[]{:S(2)}) collective-permute-start(bf16[304,768]{1,0:T(8,128)(2,1)S(1)} %collective-permute-done.refs_1_), channel_id=1, source_target_pairs={{0,1},{1,2},{2,3},{3,0},{4,5},{5,6},{6,7},{7,4},{8,9},{9,10},{10,1... | collective-permute-start | bytes 1400840 | tf_op jit(solution)/shard_map/ppermute | solution.py:913
  24.5 8.7 %collective-permute-start.5 = (bf16[192,576]{1,0:T(8,128)(2,1)S(1)}, bf16[192,576]{1,0:T(8,128)(2,1)S(1)}, u32[]{:S(2)}, u32[]{:S(2)}) collective-permute-start(bf16[192,576]{1,0:T(8,128)(2,1)S(1)} %constant_dynamic-update-slice_fusion.refs_2_.refs_4_), channel_id=1, source_target_pairs={{0,8},{8,0},{4,12},{12,4},{1,9},{9,1},{5,13},{13,5},{2,10},{10,2},... | collective-permute-start | bytes 663560 | tf_op jit(solution)/shard_map/ppermute | solution.py:908
  26.1 13.4 %collective-permute-start.10 = (bf16[192,192]{1,0:T(8,128)(2,1)S(1)}, bf16[192,192]{1,0:T(8,128)(2,1)S(1)}, u32[]{:S(2)}, u32[]{:S(2)}) collective-permute-start(bf16[192,192]{1,0:T(8,128)(2,1)S(1)} %get-tuple-element.319), channel_id=1, source_target_pairs={{0,4},{4,0},{8,12},{12,8},{1,5},{5,1},{9,13},{13,9},{2,6},{6,2},{1... | collective-permute-start | bytes 221192 | tf_op jit(solution)/shard_map/ppermute | solution.py:904
  26.2 13.3 %collective-permute-start.11 = (bf16[192,192]{1,0:T(8,128)(2,1)S(1)}, bf16[192,192]{1,0:T(8,128)(2,1)S(1)}, u32[]{:S(2)}, u32[]{:S(2)}) collective-permute-start(bf16[192,192]{1,0:T(8,128)(2,1)S(1)} %get-tuple-element.318), channel_id=1, source_target_pairs={{0,8},{8,0},{4,12},{12,4},{1,9},{9,1},{5,13},{13,5},{2,10},{10,2},... | collective-permute-start | bytes 221192 | tf_op jit(solution)/shard_map/ppermute | solution.py:908
  27.7 5.5 %collective-permute-start.4 = (bf16[192,576]{1,0:T(8,128)(2,1)S(1)}, bf16[192,576]{1,0:T(8,128)(2,1)S(1)}, u32[]{:S(2)}, u32[]{:S(2)}) collective-permute-start(bf16[192,576]{1,0:T(8,128)(2,1)S(1)} %constant_dynamic-update-slice_fusion.refs_2_.refs_4_), channel_id=1, source_target_pairs={{0,4},{4,0},{8,12},{12,8},{1,5},{5,1},{9,13},{13,9},{2,6},{6,2},{1... | collective-permute-start | bytes 663560 | tf_op jit(solution)/shard_map/ppermute | solution.py:904
  33.2 3.9 %collective-permute-start.6 = (bf16[192,576]{1,0:T(8,128)(2,1)S(1)}, bf16[192,576]{1,0:T(8,128)(2,1)S(1)}, u32[]{:S(2)}, u32[]{:S(2)}) collective-permute-start(bf16[192,576]{1,0:T(8,128)(2,1)S(1)} %collective-permute-done.5.refs_4_.refs_6_), channel_id=1, source_target_pairs={{0,4},{4,0},{8,12},{12,8},{1,5},{5,1},{9,13},{13,9},{2,6},{6,2},{1... | collective-permute-start | bytes 663560 | tf_op jit(solution)/shard_map/ppermute | solution.py:904
  33.2 6.3 %collective-permute-start.12 = (bf16[192,192]{1,0:T(8,128)(2,1)S(1)}, bf16[192,192]{1,0:T(8,128)(2,1)S(1)}, u32[]{:S(2)}, u32[]{:S(2)}) collective-permute-start(bf16[192,192]{1,0:T(8,128)(2,1)S(1)} %get-tuple-element.317), channel_id=1, source_target_pairs={{0,12},{4,8},{8,4},{12,0},{1,13},{5,9},{9,5},{13,1},{2,14},{6,10},... | collective-permute-start | bytes 221192 | tf_op jit(solution)/shard_map/ppermute | solution.py:995
  37.0 13.5 %collective-permute-start.8 = (bf16[304,768]{1,0:T(8,128)(2,1)S(1)}, bf16[304,768]{1,0:T(8,128)(2,1)S(1)}, u32[]{:S(2)}, u32[]{:S(2)}) collective-permute-start(bf16[304,768]{1,0:T(8,128)(2,1)S(1)} %collective-permute-done.7.refs_2_), channel_id=1, source_target_pairs={{0,1},{1,2},{2,3},{3,0},{4,5},{5,6},{6,7},{7,4},{8,9},{9,10},{10,1... | collective-permute-start | bytes 1400840 | tf_op jit(solution)/shard_map/ppermute | solution.py:913
  38.6 3.3 %collective-permute-start.9 = (bf16[512,384]{1,0:T(8,128)(2,1)S(1)}, bf16[512,384]{1,0:T(8,128)(2,1)S(1)}, u32[]{:S(2)}, u32[]{:S(2)}) collective-permute-start(bf16[512,384]{1,0:T(8,128)(2,1)S(1)} %get-tuple-element.171.refs_3_), channel_id=1, source_target_pairs={{0,4},{4,0},{8,12},{12,8},{1,5},{5,1},{9,13},{13,9},{2,6},{6,2},{1... | collective-permute-start | bytes 1179656 | tf_op jit(solution)/shard_map/ppermute | solution.py:904
  40.3 13.8 %collective-permute-start.14 = (bf16[512,384]{1,0:T(8,128)(2,1)S(1)}, bf16[512,384]{1,0:T(8,128)(2,1)S(1)}, u32[]{:S(2)}, u32[]{:S(2)}) collective-permute-start(bf16[512,384]{1,0:T(8,128)(2,1)S(1)} %get-tuple-element.171.refs_3_), channel_id=1, source_target_pairs={{0,8},{8,0},{4,12},{12,4},{1,9},{9,1},{5,13},{13,5},{2,10},{10,2},... | collective-permute-start | bytes 1179656 | tf_op jit(solution)/shard_map/ppermute | solution.py:908
  52.1 13.4 %collective-permute-start.16 = (bf16[512,384]{1,0:T(8,128)(2,1)S(1)}, bf16[512,384]{1,0:T(8,128)(2,1)S(1)}, u32[]{:S(2)}, u32[]{:S(2)}) collective-permute-start(bf16[512,384]{1,0:T(8,128)(2,1)S(1)} %get-tuple-element.175.refs_4_), channel_id=1, source_target_pairs={{0,8},{8,0},{4,12},{12,4},{1,9},{9,1},{5,13},{13,5},{2,10},{10,2},... | collective-permute-start | bytes 1179656 | tf_op jit(solution)/shard_map/ppermute | solution.py:908
  53.6 11.8 %collective-permute-start.15 = (bf16[208,768]{1,0:T(8,128)(2,1)S(1)}, bf16[208,768]{1,0:T(8,128)(2,1)S(1)}, u32[]{:S(2)}, u32[]{:S(2)}) collective-permute-start(bf16[208,768]{1,0:T(8,128)(2,1)S(1)} %get-tuple-element.193), channel_id=1, source_target_pairs={{0,1},{1,2},{2,3},{3,0},{4,5},{5,6},{6,7},{7,4},{8,9},{9,10},{10,1... | collective-permute-start | bytes 958472 | tf_op jit(solution)/shard_map/ppermute | solution.py:913
  65.5 5.0 %collective-permute-start.17 = (bf16[512,384]{1,0:T(8,128)(2,1)S(1)}, bf16[512,384]{1,0:T(8,128)(2,1)S(1)}, u32[]{:S(2)}, u32[]{:S(2)}) collective-permute-start(bf16[512,384]{1,0:T(8,128)(2,1)S(1)} %collective-permute-done.14.refs_3_), channel_id=1, source_target_pairs={{0,4},{4,0},{8,12},{12,8},{1,5},{5,1},{9,13},{13,9},{2,6},{6,2},{1... | collective-permute-start | bytes 1179656 | tf_op jit(solution)/shard_map/ppermute | solution.py:904
  65.5 6.5 %collective-permute-start.18 = (bf16[512,384]{1,0:T(8,128)(2,1)S(1)}, bf16[512,384]{1,0:T(8,128)(2,1)S(1)}, u32[]{:S(2)}, u32[]{:S(2)}) collective-permute-start(bf16[512,384]{1,0:T(8,128)(2,1)S(1)} %collective-permute-done.16.refs_4_), channel_id=1, source_target_pairs={{0,4},{4,0},{8,12},{12,8},{1,5},{5,1},{9,13},{13,9},{2,6},{6,2},{1... | collective-permute-start | bytes 1179656 | tf_op jit(solution)/shard_map/ppermute | solution.py:904
  66.0 16.7 %collective-permute-start.22 = (bf16[224,768]{1,0:T(8,128)(2,1)S(1)}, bf16[224,768]{1,0:T(8,128)(2,1)S(1)}, u32[]{:S(2)}, u32[]{:S(2)}) collective-permute-start(bf16[224,768]{1,0:T(8,128)(2,1)S(1)} %get-tuple-element.194.refs_4_), channel_id=1, source_target_pairs={{0,8},{8,0},{4,12},{12,4},{1,9},{9,1},{5,13},{13,5},{2,10},{10,2},... | collective-permute-start | bytes 1032200 | tf_op jit(solution)/shard_map/ppermute | solution.py:908
  66.5 16.0 %collective-permute-start.19 = (bf16[208,768]{1,0:T(8,128)(2,1)S(1)}, bf16[208,768]{1,0:T(8,128)(2,1)S(1)}, u32[]{:S(2)}, u32[]{:S(2)}) collective-permute-start(bf16[208,768]{1,0:T(8,128)(2,1)S(1)} %collective-permute-done.15.refs_3_), channel_id=1, source_target_pairs={{0,1},{1,2},{2,3},{3,0},{4,5},{5,6},{6,7},{7,4},{8,9},{9,10},{10,1... | collective-permute-start | bytes 958472 | tf_op jit(solution)/shard_map/ppermute | solution.py:913
  66.5 16.2 %collective-permute-start.20 = (bf16[208,768]{1,0:T(8,128)(2,1)S(1)}, bf16[208,768]{1,0:T(8,128)(2,1)S(1)}, u32[]{:S(2)}, u32[]{:S(2)}) collective-permute-start(bf16[208,768]{1,0:T(8,128)(2,1)S(1)} %get-tuple-element.193), channel_id=1, source_target_pairs={{0,3},{1,0},{2,1},{3,2},{4,7},{5,4},{6,5},{7,6},{8,11},{9,8},{10,9... | collective-permute-start | bytes 958472 | tf_op jit(solution)/shard_map/ppermute | solution.py:913
  70.5 12.2 %collective-permute-start.21 = (bf16[208,768]{1,0:T(8,128)(2,1)S(1)}, bf16[208,768]{1,0:T(8,128)(2,1)S(1)}, u32[]{:S(2)}, u32[]{:S(2)}) collective-permute-start(bf16[208,768]{1,0:T(8,128)(2,1)S(1)} %collective-permute-done.15.refs_3_), channel_id=1, source_target_pairs={{0,16},{16,0},{1,17},{17,1},{2,18},{18,2},{3,19},{19,3},{4,20},{20... | collective-permute-start | bytes 958472 | tf_op jit(solution)/shard_map/ppermute | solution.py:1014
  72.0 25.0 %collective-permute-start.27 = (bf16[224,768]{1,0:T(8,128)(2,1)S(1)}, bf16[224,768]{1,0:T(8,128)(2,1)S(1)}, u32[]{:S(2)}, u32[]{:S(2)}) collective-permute-start(bf16[224,768]{1,0:T(8,128)(2,1)S(1)} %get-tuple-element.194.refs_4_), channel_id=1, source_target_pairs={{0,4},{4,0},{8,12},{12,8},{1,5},{5,1},{9,13},{13,9},{2,6},{6,2},{1... | collective-permute-start | bytes 1032200 | tf_op jit(solution)/shard_map/ppermute | solution.py:904
  82.7 14.4 %collective-permute-start.28 = (bf16[224,768]{1,0:T(8,128)(2,1)S(1)}, bf16[224,768]{1,0:T(8,128)(2,1)S(1)}, u32[]{:S(2)}, u32[]{:S(2)}) collective-permute-start(bf16[224,768]{1,0:T(8,128)(2,1)S(1)} %collective-permute-done.22.refs_6_), channel_id=1, source_target_pairs={{0,4},{4,0},{8,12},{12,8},{1,5},{5,1},{9,13},{13,9},{2,6},{6,2},{1... | collective-permute-start | bytes 1032200 | tf_op jit(solution)/shard_map/ppermute | solution.py:904
  83.1 13.9 %collective-permute-start.26 = (bf16[208,768]{1,0:T(8,128)(2,1)S(1)}, bf16[208,768]{1,0:T(8,128)(2,1)S(1)}, u32[]{:S(2)}, u32[]{:S(2)}) collective-permute-start(bf16[208,768]{1,0:T(8,128)(2,1)S(1)} %collective-permute-done.19.refs_5_), channel_id=1, source_target_pairs={{0,16},{16,0},{1,17},{17,1},{2,18},{18,2},{3,19},{19,3},{4,20},{20... | collective-permute-start | bytes 958472 | tf_op jit(solution)/shard_map/ppermute | solution.py:1014
  84.3 5.6 %collective-permute-start.23 = (bf16[192,256]{1,0:T(8,128)(2,1)S(1)}, bf16[192,256]{1,0:T(8,128)(2,1)S(1)}, u32[]{:S(2)}, u32[]{:S(2)}) collective-permute-start(bf16[192,256]{1,0:T(8,128)(2,1)S(1)} %get-tuple-element.197.refs_1_), channel_id=1, source_target_pairs={{0,3},{1,0},{2,1},{3,2},{4,7},{5,4},{6,5},{7,6},{8,11},{9,8},{10,9... | collective-permute-start | bytes 294920 | tf_op jit(solution)/shard_map/ppermute | solution.py:913
  86.7 8.7 %collective-permute-start.24 = (bf16[192,256]{1,0:T(8,128)(2,1)S(1)}, bf16[192,256]{1,0:T(8,128)(2,1)S(1)}, u32[]{:S(2)}, u32[]{:S(2)}) collective-permute-start(bf16[192,256]{1,0:T(8,128)(2,1)S(1)} %get-tuple-element.198.refs_2_), channel_id=1, source_target_pairs={{0,2},{1,3},{2,0},{3,1},{4,6},{5,7},{6,4},{7,5},{8,10},{9,11},{10,... | collective-permute-start | bytes 294920 | tf_op jit(solution)/shard_map/ppermute | solution.py:913
  89.9 7.1 %collective-permute-start.25 = (bf16[192,256]{1,0:T(8,128)(2,1)S(1)}, bf16[192,256]{1,0:T(8,128)(2,1)S(1)}, u32[]{:S(2)}, u32[]{:S(2)}) collective-permute-start(bf16[192,256]{1,0:T(8,128)(2,1)S(1)} %get-tuple-element.199.refs_3_), channel_id=1, source_target_pairs={{0,1},{1,2},{2,3},{3,0},{4,5},{5,6},{6,7},{7,4},{8,9},{9,10},{10,1... | collective-permute-start | bytes 294920 | tf_op jit(solution)/shard_map/ppermute | solution.py:913
  98.5 11.2 %collective-permute-start.29 = (bf16[256,768]{1,0:T(8,128)(2,1)S(1)}, bf16[256,768]{1,0:T(8,128)(2,1)S(1)}, u32[]{:S(2)}, u32[]{:S(2)}) collective-permute-start(bf16[256,768]{1,0:T(8,128)(2,1)S(1)} %get-tuple-element.207.refs_0_.refs_4_), channel_id=1, source_target_pairs={{0,4},{4,0},{8,12},{12,8},{1,5},{5,1},{9,13},{13,9},{2,6},{6,2},{1... | collective-permute-start | bytes 1179656 | tf_op jit(solution)/shard_map/ppermute | solution.py:904
  98.6 11.5 %collective-permute-start.30 = (bf16[256,768]{1,0:T(8,128)(2,1)S(1)}, bf16[256,768]{1,0:T(8,128)(2,1)S(1)}, u32[]{:S(2)}, u32[]{:S(2)}) collective-permute-start(bf16[256,768]{1,0:T(8,128)(2,1)S(1)} %get-tuple-element.207.refs_0_.refs_4_), channel_id=1, source_target_pairs={{0,8},{8,0},{4,12},{12,4},{1,9},{9,1},{5,13},{13,5},{2,10},{10,2},... | collective-permute-start | bytes 1179656 | tf_op jit(solution)/shard_map/ppermute | solution.py:908
  100.2 9.6 %collective-permute-start.31 = (bf16[208,768]{1,0:T(8,128)(2,1)S(1)}, bf16[208,768]{1,0:T(8,128)(2,1)S(1)}, u32[]{:S(2)}, u32[]{:S(2)}) collective-permute-start(bf16[208,768]{1,0:T(8,128)(2,1)S(1)} %collective-permute-done.20.refs_7_), channel_id=1, source_target_pairs={{0,16},{16,0},{1,17},{17,1},{2,18},{18,2},{3,19},{19,3},{4,20},{20... | collective-permute-start | bytes 958472 | tf_op jit(solution)/shard_map/ppermute | solution.py:1014
  114.4 3.2 %collective-permute-start.34 = (bf16[256,768]{1,0:T(8,128)(2,1)S(1)}, bf16[256,768]{1,0:T(8,128)(2,1)S(1)}, u32[]{:S(2)}, u32[]{:S(2)}) collective-permute-start(bf16[256,768]{1,0:T(8,128)(2,1)S(1)} %get-tuple-element.218), channel_id=1, source_target_pairs={{0,4},{4,0},{8,12},{12,8},{1,5},{5,1},{9,13},{13,9},{2,6},{6,2},{1... | collective-permute-start | bytes 1179656 | tf_op jit(solution)/shard_map/ppermute | solution.py:904
  117.8 11.2 %collective-permute-start.35 = (bf16[256,768]{1,0:T(8,128)(2,1)S(1)}, bf16[256,768]{1,0:T(8,128)(2,1)S(1)}, u32[]{:S(2)}, u32[]{:S(2)}) collective-permute-start(bf16[256,768]{1,0:T(8,128)(2,1)S(1)} %add_convert_fusion.5), channel_id=1, source_target_pairs={{0,8},{8,0},{4,12},{12,4},{1,9},{9,1},{5,13},{13,5},{2,10},{10,2},... | collective-permute-start | bytes 1179656 | tf_op jit(solution)/shard_map/ppermute | solution.py:908
  131.0 11.5 %collective-permute-start.37 = (bf16[256,768]{1,0:T(8,128)(2,1)S(1)}, bf16[256,768]{1,0:T(8,128)(2,1)S(1)}, u32[]{:S(2)}, u32[]{:S(2)}) collective-permute-start(bf16[256,768]{1,0:T(8,128)(2,1)S(1)} %get-tuple-element.221.refs_0_.refs_8_), channel_id=1, source_target_pairs={{0,8},{8,0},{4,12},{12,4},{1,9},{9,1},{5,13},{13,5},{2,10},{10,2},... | collective-permute-start | bytes 1179656 | tf_op jit(solution)/shard_map/ppermute | solution.py:908
  146.6 7.9 %collective-permute-start.39 = (bf16[256,768]{1,0:T(8,128)(2,1)S(1)}, bf16[256,768]{1,0:T(8,128)(2,1)S(1)}, u32[]{:S(2)}, u32[]{:S(2)}) collective-permute-start(bf16[256,768]{1,0:T(8,128)(2,1)S(1)} %get-tuple-element.227), channel_id=1, source_target_pairs={{0,4},{4,0},{8,12},{12,8},{1,5},{5,1},{9,13},{13,9},{2,6},{6,2},{1... | collective-permute-start | bytes 1179656 | tf_op jit(solution)/shard_map/ppermute | solution.py:904
  148.3 11.2 %collective-permute-start.41 = (bf16[256,768]{1,0:T(8,128)(2,1)S(1)}, bf16[256,768]{1,0:T(8,128)(2,1)S(1)}, u32[]{:S(2)}, u32[]{:S(2)}) collective-permute-start(bf16[256,768]{1,0:T(8,128)(2,1)S(1)} %add_convert_fusion.4), channel_id=1, source_target_pairs={{0,8},{8,0},{4,12},{12,4},{1,9},{9,1},{5,13},{13,5},{2,10},{10,2},... | collective-permute-start | bytes 1179656 | tf_op jit(solution)/shard_map/ppermute | solution.py:908
  153.9 28.4 %collective-permute-start.46 = (bf16[768,768]{1,0:T(8,128)(2,1)S(1)}, bf16[768,768]{1,0:T(8,128)(2,1)S(1)}, u32[]{:S(2)}, u32[]{:S(2)}) collective-permute-start(bf16[768,768]{1,0:T(8,128)(2,1)S(1)} %get-tuple-element.259), channel_id=1, source_target_pairs={{0,16},{16,0},{1,17},{17,1},{2,18},{18,2},{3,19},{19,3},{4,20},{20... | collective-permute-start | bytes 3538952 | tf_op jit(solution)/shard_map/ppermute | solution.py:1090
  161.9 7.6 %collective-permute-start.45 = (bf16[416,768]{1,0:T(8,128)(2,1)S(1)}, bf16[416,768]{1,0:T(8,128)(2,1)S(1)}, u32[]{:S(2)}, u32[]{:S(2)}) collective-permute-start(bf16[416,768]{1,0:T(8,128)(2,1)S(1)} %get-tuple-element.251), channel_id=1, source_target_pairs={{0,4},{4,0},{8,12},{12,8},{1,5},{5,1},{9,13},{13,9},{2,6},{6,2},{1... | collective-permute-start | bytes 1916936 | tf_op jit(solution)/shard_map/ppermute | solution.py:904
  162.0 7.5 %collective-permute-start.42 = (bf16[192,256]{1,0:T(8,128)(2,1)S(1)}, bf16[192,256]{1,0:T(8,128)(2,1)S(1)}, u32[]{:S(2)}, u32[]{:S(2)}) collective-permute-start(bf16[192,256]{1,0:T(8,128)(2,1)S(1)} %get-tuple-element.242), channel_id=1, source_target_pairs={{0,1},{1,2},{2,3},{3,0},{4,5},{5,6},{6,7},{7,4},{8,9},{9,10},{10,1... | collective-permute-start | bytes 294920 | tf_op jit(solution)/shard_map/ppermute | solution.py:913
  162.0 10.8 %collective-permute-start.43 = (bf16[192,256]{1,0:T(8,128)(2,1)S(1)}, bf16[192,256]{1,0:T(8,128)(2,1)S(1)}, u32[]{:S(2)}, u32[]{:S(2)}) collective-permute-start(bf16[192,256]{1,0:T(8,128)(2,1)S(1)} %get-tuple-element.243), channel_id=1, source_target_pairs={{0,2},{1,3},{2,0},{3,1},{4,6},{5,7},{6,4},{7,5},{8,10},{9,11},{10,... | collective-permute-start | bytes 294920 | tf_op jit(solution)/shard_map/ppermute | solution.py:913
  164.8 8.0 %collective-permute-start.44 = (bf16[192,256]{1,0:T(8,128)(2,1)S(1)}, bf16[192,256]{1,0:T(8,128)(2,1)S(1)}, u32[]{:S(2)}, u32[]{:S(2)}) collective-permute-start(bf16[192,256]{1,0:T(8,128)(2,1)S(1)} %get-tuple-element.244), channel_id=1, source_target_pairs={{0,3},{1,0},{2,1},{3,2},{4,7},{5,4},{6,5},{7,6},{8,11},{9,8},{10,9... | collective-permute-start | bytes 294920 | tf_op jit(solution)/shard_map/ppermute | solution.py:913
  169.6 12.8 %collective-permute-start.47 = (bf16[224,768]{1,0:T(8,128)(2,1)S(1)}, bf16[224,768]{1,0:T(8,128)(2,1)S(1)}, u32[]{:S(2)}, u32[]{:S(2)}) collective-permute-start(bf16[224,768]{1,0:T(8,128)(2,1)S(1)} %far_message.1), channel_id=1, source_target_pairs={{0,8},{8,0},{4,12},{12,4},{1,9},{9,1},{5,13},{13,5},{2,10},{10,2},... | collective-permute-start | bytes 1032200 | tf_op jit(solution)/shard_map/ppermute | solution.py:908
  181.8 11.9 %collective-permute-start.49 = (bf16[512,384]{1,0:T(8,128)(2,1)S(1)}, bf16[512,384]{1,0:T(8,128)(2,1)S(1)}, u32[]{:S(2)}, u32[]{:S(2)}) collective-permute-start(bf16[512,384]{1,0:T(8,128)(2,1)S(1)} %get-tuple-element.267), channel_id=1, source_target_pairs={{0,4},{4,0},{8,12},{12,8},{1,5},{5,1},{9,13},{13,9},{2,6},{6,2},{1... | collective-permute-start | bytes 1179656 | tf_op jit(solution)/shard_map/ppermute | solution.py:904
  181.9 12.0 %collective-permute-start.48 = (bf16[512,384]{1,0:T(8,128)(2,1)S(1)}, bf16[512,384]{1,0:T(8,128)(2,1)S(1)}, u32[]{:S(2)}, u32[]{:S(2)}) collective-permute-start(bf16[512,384]{1,0:T(8,128)(2,1)S(1)} %get-tuple-element.265), channel_id=1, source_target_pairs={{0,4},{4,0},{8,12},{12,8},{1,5},{5,1},{9,13},{13,9},{2,6},{6,2},{1... | collective-permute-start | bytes 1179656 | tf_op jit(solution)/shard_map/ppermute | solution.py:904
  182.8 13.6 %collective-permute-start.50 = (bf16[272,768]{1,0:T(8,128)(2,1)S(1)}, bf16[272,768]{1,0:T(8,128)(2,1)S(1)}, u32[]{:S(2)}, u32[]{:S(2)}) collective-permute-start(bf16[272,768]{1,0:T(8,128)(2,1)S(1)} %get-tuple-element.269), channel_id=1, source_target_pairs={{0,1},{1,2},{2,3},{3,0},{4,5},{5,6},{6,7},{7,4},{8,9},{9,10},{10,1... | collective-permute-start | bytes 1253384 | tf_op jit(solution)/shard_map/ppermute | solution.py:913
  196.5 12.8 %collective-permute-start.51 = (bf16[272,768]{1,0:T(8,128)(2,1)S(1)}, bf16[272,768]{1,0:T(8,128)(2,1)S(1)}, u32[]{:S(2)}, u32[]{:S(2)}) collective-permute-start(bf16[272,768]{1,0:T(8,128)(2,1)S(1)} %sum_messages.3), channel_id=1, source_target_pairs={{0,1},{1,2},{2,3},{3,0},{4,5},{5,6},{6,7},{7,4},{8,9},{9,10},{10,1... | collective-permute-start | bytes 1253384 | tf_op jit(solution)/shard_map/ppermute | solution.py:913
  197.1 21.4 %collective-permute-start.54 = (bf16[1024,384]{1,0:T(8,128)(2,1)S(1)}, bf16[1024,384]{1,0:T(8,128)(2,1)S(1)}, u32[]{:S(2)}, u32[]{:S(2)}) collective-permute-start(bf16[1024,384]{1,0:T(8,128)(2,1)S(1)} %pad_maximum_fusion), channel_id=1, source_target_pairs={{0,8},{8,0},{4,12},{12,4},{1,9},{9,1},{5,13},{13,5},{2,10},{10,2},... | collective-permute-start | bytes 2359304 | tf_op jit(solution)/shard_map/ppermute | solution.py:908
  207.2 11.2 %collective-permute-start.52 = (bf16[512,384]{1,0:T(8,128)(2,1)S(1)}, bf16[512,384]{1,0:T(8,128)(2,1)S(1)}, u32[]{:S(2)}, u32[]{:S(2)}) collective-permute-start(bf16[512,384]{1,0:T(8,128)(2,1)S(1)} %get-tuple-element.277), channel_id=1, source_target_pairs={{0,4},{4,0},{8,12},{12,8},{1,5},{5,1},{9,13},{13,9},{2,6},{6,2},{1... | collective-permute-start | bytes 1179656 | tf_op jit(solution)/shard_map/ppermute | solution.py:904
  207.3 11.1 %collective-permute-start.53 = (bf16[512,384]{1,0:T(8,128)(2,1)S(1)}, bf16[512,384]{1,0:T(8,128)(2,1)S(1)}, u32[]{:S(2)}, u32[]{:S(2)}) collective-permute-start(bf16[512,384]{1,0:T(8,128)(2,1)S(1)} %get-tuple-element.278), channel_id=1, source_target_pairs={{0,4},{4,0},{8,12},{12,8},{1,5},{5,1},{9,13},{13,9},{2,6},{6,2},{1... | collective-permute-start | bytes 1179656 | tf_op jit(solution)/shard_map/ppermute | solution.py:904
  209.5 12.1 %collective-permute-start.56 = (bf16[272,768]{1,0:T(8,128)(2,1)S(1)}, bf16[272,768]{1,0:T(8,128)(2,1)S(1)}, u32[]{:S(2)}, u32[]{:S(2)}) collective-permute-start(bf16[272,768]{1,0:T(8,128)(2,1)S(1)} %sum_messages.4), channel_id=1, source_target_pairs={{0,1},{1,2},{2,3},{3,0},{4,5},{5,6},{6,7},{7,4},{8,9},{9,10},{10,1... | collective-permute-start | bytes 1253384 | tf_op jit(solution)/shard_map/ppermute | solution.py:913
  220.6 11.6 %collective-permute-start.55 = (bf16[256,768]{1,0:T(8,128)(2,1)}, bf16[256,768]{1,0:T(8,128)(2,1)}, u32[]{:S(2)}, u32[]{:S(2)}) collective-permute-start(bf16[256,768]{1,0:T(8,128)(2,1)} %get-tuple-element.284), channel_id=1, source_target_pairs={{0,1},{1,2},{2,3},{3,0},{4,5},{5,6},{6,7},{7,4},{8,9},{9,10},{10,1... | collective-permute-start | bytes 1179656 | tf_op jit(solution)/shard_map/ppermute | solution.py:913
  225.2 7.0 %collective-permute-start.57 = (bf16[208,576]{1,0:T(8,128)(2,1)S(1)}, bf16[208,576]{1,0:T(8,128)(2,1)S(1)}, u32[]{:S(2)}, u32[]{:S(2)}) collective-permute-start(bf16[208,576]{1,0:T(8,128)(2,1)S(1)} %get-tuple-element.291), channel_id=1, source_target_pairs={{0,4},{4,0},{8,12},{12,8},{1,5},{5,1},{9,13},{13,9},{2,6},{6,2},{1... | collective-permute-start | bytes 718856 | tf_op jit(solution)/shard_map/ppermute | solution.py:904
  225.3 7.0 %collective-permute-start.58 = (bf16[192,576]{1,0:T(8,128)(2,1)}, bf16[192,576]{1,0:T(8,128)(2,1)S(1)}, u32[]{:S(2)}, u32[]{:S(2)}) collective-permute-start(bf16[192,576]{1,0:T(8,128)(2,1)} %get-tuple-element.292), channel_id=1, source_target_pairs={{0,4},{4,0},{8,12},{12,8},{1,5},{5,1},{9,13},{13,9},{2,6},{6,2},{1... | collective-permute-start | bytes 663560 | tf_op jit(solution)/shard_map/ppermute | solution.py:904
  232.4 6.5 %collective-permute-start.61 = (bf16[208,576]{1,0:T(8,128)(2,1)S(1)}, bf16[208,576]{1,0:T(8,128)(2,1)S(1)}, u32[]{:S(2)}, u32[]{:S(2)}) collective-permute-start(bf16[208,576]{1,0:T(8,128)(2,1)S(1)} %pad_maximum_fusion.2), channel_id=1, source_target_pairs={{0,8},{8,0},{4,12},{12,4},{1,9},{9,1},{5,13},{13,5},{2,10},{10,2},... | collective-permute-start | bytes 718856 | tf_op jit(solution)/shard_map/ppermute | solution.py:908
  234.9 10.0 %collective-permute-start.59 = (bf16[256,768]{1,0:T(8,128)(2,1)S(1)}, bf16[256,768]{1,0:T(8,128)(2,1)S(1)}, u32[]{:S(2)}, u32[]{:S(2)}) collective-permute-start(bf16[256,768]{1,0:T(8,128)(2,1)S(1)} %add_convert_fusion.1), channel_id=1, source_target_pairs={{0,1},{1,2},{2,3},{3,0},{4,5},{5,6},{6,7},{7,4},{8,9},{9,10},{10,1... | collective-permute-start | bytes 1179656 | tf_op jit(solution)/shard_map/ppermute | solution.py:913
  234.9 12.0 %collective-permute-start.66 = (bf16[272,768]{1,0:T(8,128)(2,1)S(1)}, bf16[272,768]{1,0:T(8,128)(2,1)S(1)}, u32[]{:S(2)}, u32[]{:S(2)}) collective-permute-start(bf16[272,768]{1,0:T(8,128)(2,1)S(1)} %sum_messages.5.own), channel_id=1, source_target_pairs={{0,16},{16,0},{1,17},{17,1},{2,18},{18,2},{3,19},{19,3},{4,20},{20... | collective-permute-start | bytes 1253384 | tf_op jit(solution)/shard_map/ppermute | solution.py:1142
  239.1 13.3 %collective-permute-start.62 = (bf16[208,576]{1,0:T(8,128)(2,1)S(1)}, bf16[208,576]{1,0:T(8,128)(2,1)S(1)}, u32[]{:S(2)}, u32[]{:S(2)}) collective-permute-start(bf16[208,576]{1,0:T(8,128)(2,1)S(1)} %pad_maximum_fusion.3), channel_id=1, source_target_pairs={{0,16},{16,0},{1,17},{17,1},{2,18},{18,2},{3,19},{19,3},{4,20},{20... | collective-permute-start | bytes 718856 | tf_op jit(solution)/shard_map/ppermute | solution.py:1161
  245.0 18.4 %collective-permute-start.60 = (bf16[256,768]{1,0:T(8,128)(2,1)S(1)}, bf16[256,768]{1,0:T(8,128)(2,1)S(1)}, u32[]{:S(2)}, u32[]{:S(2)}) collective-permute-start(bf16[256,768]{1,0:T(8,128)(2,1)S(1)} %add_convert_fusion), channel_id=1, source_target_pairs={{0,1},{1,2},{2,3},{3,0},{4,5},{5,6},{6,7},{7,4},{8,9},{9,10},{10,1... | collective-permute-start | bytes 1179656 | tf_op jit(solution)/shard_map/ppermute | solution.py:913
  249.2 6.3 %collective-permute-start.67 = (bf16[192,192]{1,0:T(8,128)(2,1)S(1)}, bf16[192,192]{1,0:T(8,128)(2,1)S(1)}, u32[]{:S(2)}, u32[]{:S(2)}) collective-permute-start(bf16[192,192]{1,0:T(8,128)(2,1)S(1)} %get-tuple-element.309), channel_id=1, source_target_pairs={{0,4},{4,0},{8,12},{12,8},{1,5},{5,1},{9,13},{13,9},{2,6},{6,2},{1... | collective-permute-start | bytes 221192 | tf_op jit(solution)/shard_map/ppermute | solution.py:904
  249.2 7.5 %collective-permute-start.68 = (bf16[192,192]{1,0:T(8,128)(2,1)S(1)}, bf16[192,192]{1,0:T(8,128)(2,1)S(1)}, u32[]{:S(2)}, u32[]{:S(2)}) collective-permute-start(bf16[192,192]{1,0:T(8,128)(2,1)S(1)} %get-tuple-element.310), channel_id=1, source_target_pairs={{0,8},{8,0},{4,12},{12,4},{1,9},{9,1},{5,13},{13,5},{2,10},{10,2},... | collective-permute-start | bytes 221192 | tf_op jit(solution)/shard_map/ppermute | solution.py:908
  250.8 7.6 %collective-permute-start.69 = (bf16[192,192]{1,0:T(8,128)(2,1)S(1)}, bf16[192,192]{1,0:T(8,128)(2,1)S(1)}, u32[]{:S(2)}, u32[]{:S(2)}) collective-permute-start(bf16[192,192]{1,0:T(8,128)(2,1)S(1)} %get-tuple-element.311), channel_id=1, source_target_pairs={{0,12},{4,8},{8,4},{12,0},{1,13},{5,9},{9,5},{13,1},{2,14},{6,10},... | collective-permute-start | bytes 221192 | tf_op jit(solution)/shard_map/ppermute | solution.py:1178
  252.5 7.4 %collective-permute-start.63 = (bf16[48,576]{1,0:T(8,128)(2,1)S(1)}, bf16[48,576]{1,0:T(8,128)(2,1)S(1)}, u32[]{:S(2)}, u32[]{:S(2)}) collective-permute-start(bf16[48,576]{1,0:T(8,128)(2,1)S(1)} %get-tuple-element.323), channel_id=1, source_target_pairs={{0,1},{1,2},{2,3},{3,0},{4,5},{5,6},{6,7},{7,4},{8,9},{9,10},{10,1... | collective-permute-start | bytes 165896 | tf_op jit(solution)/shard_map/ppermute | solution.py:913
  255.4 6.4 %collective-permute-start.64 = (bf16[48,576]{1,0:T(8,128)(2,1)S(1)}, bf16[48,576]{1,0:T(8,128)(2,1)S(1)}, u32[]{:S(2)}, u32[]{:S(2)}) collective-permute-start(bf16[48,576]{1,0:T(8,128)(2,1)S(1)} %get-tuple-element.322), channel_id=1, source_target_pairs={{0,2},{1,3},{2,0},{3,1},{4,6},{5,7},{6,4},{7,5},{8,10},{9,11},{10,... | collective-permute-start | bytes 165896 | tf_op jit(solution)/shard_map/ppermute | solution.py:913
  256.7 5.3 %collective-permute-start.65 = (bf16[48,576]{1,0:T(8,128)(2,1)S(1)}, bf16[48,576]{1,0:T(8,128)(2,1)S(1)}, u32[]{:S(2)}, u32[]{:S(2)}) collective-permute-start(bf16[48,576]{1,0:T(8,128)(2,1)S(1)} %get-tuple-element.321), channel_id=1, source_target_pairs={{0,3},{1,0},{2,1},{3,2},{4,7},{5,4},{6,5},{7,6},{8,11},{9,8},{10,9... | collective-permute-start | bytes 165896 | tf_op jit(solution)/shard_map/ppermute | solution.py:913
  (31 other events, 229.4 us)

commit v2 on v0

--- a/solution.py
+++ b/solution.py
@@ -232,7 +232,7 @@
         out[:, width:] = dv[at, :width].astype(out.dtype)
 
 
-def attn_bwd(at, q, g, k, v, dq, heads, us, pieces=2, block=512):
+def attn_bwd(at, q, g, k, v, dq, heads, us, pieces=2, block=1024):
     rows = q.shape[0]
     half = k.shape[0] // 2
     width = heads * HD
@@ -792,7 +792,7 @@
     rows = dq.shape[0]
     wide, width = w.shape
     shapes = [jax.ShapeDtypeStruct((rows // n, wide), BF)] * n
-    shapes += [jax.ShapeDtypeStruct((rows // n, width), BF if k == 1 else F32) for k in range(n)]
+    shapes += [jax.ShapeDtypeStruct((rows // n, width), BF)] * n
     kernel = functools.partial(join_kernel, scale=scale, hw=wide // 3)
     out = small_call(kernel, shapes, "join_grads")(*keep, *near, far, dq, w)
     return out[:n], out[n:]
@@ -1135,7 +1135,7 @@
     got, got_far = core_swap(send), core_swap(send_far)
     ring[0], got, got_far, packed = lax.optimization_barrier((ring[0], got, got_far, packed))
     for step in range(2, cols_n + 1):
-        total = back[step % cols_n] + ring[-1].astype(F32)
+        total = back[step % cols_n].astype(F32) + ring[-1].astype(F32)
         if step < cols_n:
             ring.append(shift_col(total.astype(BF), 1))
     grad_tokens = grad_resid1 + total

time: 273 us -> 269 us (0.985)
  no operation moved by 1% of the time
where the time goes in v2:
time: 269 us; the launch traced here: 264 us
  waiting for transfers between devices  98.5 us (37%)
  Pallas kernels  89 us (33%)
  starting transfers between devices  60.8 us (23%)
  other arithmetic  6.81 us (3%)
  local copies, waits for them, and re-layouts  6.41 us (2%)
    ppermute x24, waiting for transfers between devices, shift_col(): return lax.ppermute(x, 'col', [(i, (i + step) % n) for i in range(n)])  56.5 us
    pallas_call x4, Pallas kernels, attn_bwd(): pl.pallas_call(functools.partial(attn_bwd_kernel, heads=heads, block=bloc...  34.4 us
    ppermute x13, waiting for transfers between devices, cross_swap(): return lax.ppermute(x, 'row', CROSS)  31.7 us
    pallas_call x15, Pallas kernels, meta_call(): pl.pallas_call(kernel, in_specs=[pl.BlockSpec(memory_space=pltpu.SMEM)] +...  29.9 us
    ppermute x24, starting transfers between devices, shift_col(): return lax.ppermute(x, 'col', [(i, (i + step) % n) for i in range(n)])  28.4 us
    pallas_call x2, Pallas kernels, attn_fwd(): pl.pallas_call(functools.partial(attn_fwd_kernel, heads=heads, first=firs...  20.4 us
    ppermute x13, starting transfers between devices, cross_swap(): return lax.ppermute(x, 'row', CROSS)  17.1 us
  transfers between devices with their start and end apart: 70, of which 29 were waited for; matrix products, arithmetic and copies ran while one was open for 3% of the time, Pallas kernels for 31%

profile of v2, /device:TPU:0, one launch (start us, length us, event | category | flops | bytes accessed | tf_op | source)
XLA Modules:
  0.0 264.1 jit_solution(15360766376491111115)
XLA Ops:
  2.7 3.1 %collective-permute-start = (bf16[304,768]{1,0:T(8,128)(2,1)S(1)}, bf16[304,768]{1,0:T(8,128)(2,1)S(1)}, u32[]{:S(2)}, u32[]{:S(2)}) collective-permute-start(bf16[304,768]{1,0:T(8,128)(2,1)S(1)} %pad_maximum_fusion.1.refs_0_), channel_id=1, source_target_pairs={{0,1},{1,2},{2,3},{3,0},{4,5},{5,6},{6,7},{7,4},{8,9},{9,10},{10,1... | collective-permute-start | bytes 1400840 | tf_op jit(solution)/shard_map/ppermute | solution.py:913
  7.9 1.6 collective-permute-start.1
  10.6 2.8 %collective-permute-start.3 = (bf16[48,576]{1,0:T(8,128)(2,1)S(1)}, bf16[48,576]{1,0:T(8,128)(2,1)S(1)}, u32[]{:S(2)}, u32[]{:S(2)}) collective-permute-start(bf16[48,576]{1,0:T(8,128)(2,1)S(1)} %get-tuple-element.323), channel_id=1, source_target_pairs={{0,3},{1,0},{2,1},{3,2},{4,7},{5,4},{6,5},{7,6},{8,11},{9,8},{10,9... | collective-permute-start | bytes 165896 | tf_op jit(solution)/shard_map/ppermute | solution.py:913
  13.8 7.0 %collective-permute-done.1 = bf16[48,576]{1,0:T(8,128)(2,1)S(1)} collective-permute-done((bf16[48,576]{1,0:T(8,128)(2,1)S(1)}, bf16[48,576]{1,0:T(8,128)(2,1)S(1)}, u32[]{:S(2)}, u32[]{:S(2)}) %collective-permute-start.1) | collective-permute-done | bytes 55328 | tf_op jit(solution)/shard_map/ppermute | solution.py:913
  20.8 1.8 collective-permute-done.2
  22.6 1.8 collective-permute-start.7
  24.5 1.6 collective-permute-start.5
  27.9 5.4 %collective-permute-done.5.refs_4_.refs_6_ = bf16[192,576]{1,0:T(8,128)(2,1)S(1)} collective-permute-done((bf16[192,576]{1,0:T(8,128)(2,1)S(1)}, bf16[192,576]{1,0:T(8,128)(2,1)S(1)}, u32[]{:S(2)}, u32[]{:S(2)}) %collective-permute-start.5) | collective-permute-done | bytes 221216 | tf_op jit(solution)/shard_map/ppermute | solution.py:908
  33.2 1.7 collective-permute-start.12
  34.9 2.1 collective-permute-done.7.refs_2_
  37.1 1.5 project_qkv.2
  40.3 1.6 collective-permute-start.14
  41.9 8.6 %collective-permute-done.8.refs_3_ = bf16[304,768]{1,0:T(8,128)(2,1)S(1)} collective-permute-done((bf16[304,768]{1,0:T(8,128)(2,1)S(1)}, bf16[304,768]{1,0:T(8,128)(2,1)S(1)}, u32[]{:S(2)}, u32[]{:S(2)}) %collective-permute-start.8) | collective-permute-done | bytes 466976 | tf_op jit(solution)/shard_map/ppermute | solution.py:913
  50.5 1.5 project_qkv.3
  52.1 1.6 collective-permute-start.16
  54.1 10.0 %attn_fwd_near.1 = (f32[192,1024]{1,0:T(8,128)S(1)}, f32[16,1024]{1,0:T(8,128)S(1)}, bf16[2048,256]{1,0:T(8,128)(2,1)S(1)}, bf16[2048,256]{1,0:T(8,128)(2,1)S(1)}) custom-call(s32[5]{0:T(128)S(1)} %stack.82.meta.refs_0_, bf16[512,256]{1,0:T(8,128)(2,1)S(1)} %get-tuple-element.168.refs_1_, bf16[512,256]{1,0:T(8,128)(2,1)S(1)} %get-tuple-element.173.refs_2_, ...), custom_call_target="tpu_custom_call" | custom-call | flops 2400000000 | bytes 1000 | tf_op jit(solution)/shard_map/attn_fwd_near/pallas_call | solution.py:156
  66.7 1.6 collective-permute-start.20
  68.3 10.5 %attn_fwd_far.1 = (bf16[192,256]{1,0:T(8,128)(2,1)S(1)}, bf16[192,256]{1,0:T(8,128)(2,1)S(1)}, bf16[192,256]{1,0:T(8,128)(2,1)S(1)}, bf16[192,256]{1,0:T(8,128)(...) custom-call(s32[5]{0:T(128)S(1)} %stack.82.meta.refs_0_, ...), custom_call_target="tpu_custom_call" | custom-call | flops 2400000000 | bytes 1000 | tf_op jit(solution)/shard_map/attn_fwd_far/pallas_call | solution.py:156
  79.8 3.3 %collective-permute-start.22 = (bf16[192,256]{1,0:T(8,128)(2,1)S(1)}, bf16[192,256]{1,0:T(8,128)(2,1)S(1)}, u32[]{:S(2)}, u32[]{:S(2)}) collective-permute-start(bf16[192,256]{1,0:T(8,128)(2,1)S(1)} %get-tuple-element.195.refs_1_), channel_id=1, source_target_pairs={{0,3},{1,0},{2,1},{3,2},{4,7},{5,4},{6,5},{7,6},{8,11},{9,8},{10,9... | collective-permute-start | bytes 294920 | tf_op jit(solution)/shard_map/ppermute | solution.py:913
  83.6 2.7 %collective-permute-done.22.refs_1_ = bf16[192,256]{1,0:T(8,128)(2,1)S(1)} collective-permute-done((bf16[192,256]{1,0:T(8,128)(2,1)S(1)}, bf16[192,256]{1,0:T(8,128)(2,1)S(1)}, u32[]{:S(2)}, u32[]{:S(2)}) %collective-permute-start.22) | collective-permute-done | bytes 98336 | tf_op jit(solution)/shard_map/ppermute | solution.py:913
  86.3 5.1 %collective-permute-done.23.refs_2_ = bf16[192,256]{1,0:T(8,128)(2,1)S(1)} collective-permute-done((bf16[192,256]{1,0:T(8,128)(2,1)S(1)}, bf16[192,256]{1,0:T(8,128)(2,1)S(1)}, u32[]{:S(2)}, u32[]{:S(2)}) %collective-permute-start.23) | collective-permute-done | bytes 98336 | tf_op jit(solution)/shard_map/ppermute | solution.py:913
  91.5 1.8 collective-permute-done.24.refs_3_
  93.5 1.5 project_norm1.1
  95.1 1.6 collective-permute-start.29
  96.6 6.1 %collective-permute-done.30.refs_7_ = bf16[208,768]{1,0:T(8,128)(2,1)S(1)} collective-permute-done((bf16[208,768]{1,0:T(8,128)(2,1)S(1)}, bf16[208,768]{1,0:T(8,128)(2,1)S(1)}, u32[]{:S(2)}, u32[]{:S(2)}) %collective-permute-start.30) | collective-permute-done | bytes 319520 | tf_op jit(solution)/shard_map/ppermute | solution.py:913
  104.2 2.5 collective-permute-done.29.refs_0_.refs_6_
  106.6 3.1 %collective-permute-done.31.refs_8_ = bf16[208,768]{1,0:T(8,128)(2,1)S(1)} collective-permute-done((bf16[208,768]{1,0:T(8,128)(2,1)S(1)}, bf16[208,768]{1,0:T(8,128)(2,1)S(1)}, u32[]{:S(2)}, u32[]{:S(2)}) %collective-permute-start.31) | collective-permute-done | bytes 319520 | tf_op jit(solution)/shard_map/ppermute | solution.py:1014
  109.8 1.7 collective-permute-done.33.refs_1_.refs_7_
  111.5 2.6 ffn_fwd.3
  114.3 2.6 ffn_fwd.2
  118.8 9.8 %collective-permute-done.35.far_ref = bf16[256,768]{1,0:T(8,128)(2,1)S(1)} collective-permute-done((bf16[256,768]{1,0:T(8,128)(2,1)S(1)}, bf16[256,768]{1,0:T(8,128)(2,1)S(1)}, u32[]{:S(2)}, u32[]{:S(2)}) %collective-permute-start.35) | collective-permute-done | bytes 393248 | tf_op jit(solution)/shard_map/ppermute | solution.py:908
  128.6 2.0 norm2_both.1
  132.3 2.2 ffn_bwd.2
  134.5 7.6 %collective-permute-done.37.refs_0_.refs_10_ = bf16[256,768]{1,0:T(8,128)(2,1)S(1)} collective-permute-done((bf16[256,768]{1,0:T(8,128)(2,1)S(1)}, bf16[256,768]{1,0:T(8,128)(2,1)S(1)}, u32[]{:S(2)}, u32[]{:S(2)}) %collective-permute-start.37) | collective-permute-done | bytes 393248 | tf_op jit(solution)/shard_map/ppermute | solution.py:908
  142.1 1.7 collective-permute-done.38.refs_1_.refs_11_
  143.9 2.1 ffn_bwd.3
  149.3 4.1 %ffn_grads.1 = (bf16[768,768]{1,0:T(8,128)(2,1)S(1)}, bf16[768,768]{1,0:T(8,128)(2,1)S(1)}, f32[8,768]{1,0:T(8,128)S(1)}) custom-call(s32[5]{0:T(128)S(1)} %stack.82.meta.refs_0_, bf16[512,768]{1,0:T(8,128)(2,1)S(1)} %get-tuple-element.222.refs_0_, bf16[512,768]{1,0:T(8,128)(2,1)S(1)} %get-tuple-element.223.refs_1_, ...), custom_call_target="tpu_custom_call" | custom-call | flops 720000000 | bytes 1000 | tf_op jit(solution)/shard_map/ffn_grads/pallas_call | solution.py:266
  153.4 1.6 collective-permute-start.46
  155.0 4.1 %collective-permute-done.41.far_ref = bf16[256,768]{1,0:T(8,128)(2,1)S(1)} collective-permute-done((bf16[256,768]{1,0:T(8,128)(2,1)S(1)}, bf16[256,768]{1,0:T(8,128)(2,1)S(1)}, u32[]{:S(2)}, u32[]{:S(2)}) %collective-permute-start.41) | collective-permute-done | bytes 393248 | tf_op jit(solution)/shard_map/ppermute | solution.py:908
  161.7 1.7 collective-permute-start.43
  163.3 2.8 %collective-permute-start.44 = (bf16[192,256]{1,0:T(8,128)(2,1)S(1)}, bf16[192,256]{1,0:T(8,128)(2,1)S(1)}, u32[]{:S(2)}, u32[]{:S(2)}) collective-permute-start(bf16[192,256]{1,0:T(8,128)(2,1)S(1)} %get-tuple-element.242), channel_id=1, source_target_pairs={{0,3},{1,0},{2,1},{3,2},{4,7},{5,4},{6,5},{7,6},{8,11},{9,8},{10,9... | collective-permute-start | bytes 294920 | tf_op jit(solution)/shard_map/ppermute | solution.py:913
  166.2 3.0 %collective-permute-done.42.refs_5_ = bf16[192,256]{1,0:T(8,128)(2,1)S(1)} collective-permute-done((bf16[192,256]{1,0:T(8,128)(2,1)S(1)}, bf16[192,256]{1,0:T(8,128)(2,1)S(1)}, u32[]{:S(2)}, u32[]{:S(2)}) %collective-permute-start.42) | collective-permute-done | bytes 98336 | tf_op jit(solution)/shard_map/ppermute | solution.py:913
  170.6 1.8 collective-permute-done.43.refs_6_
  172.8 8.6 %attn_bwd.4 = (bf16[512,384]{1,0:T(8,128)(2,1)S(1)}, bf16[512,384]{1,0:T(8,128)(2,1)S(1)}, f32[1024,256]{1,0:T(8,128)S(1)}) custom-call(s32[1]{0:T(128)} %constant.102.clone.1.at_ref, bf16[1024,256]{1,0:T(8,128)(2,1)S(1)} %get-tuple-element.238.q_ref, bf16[1024,256]{1,0:T(8,128)(2,1)S(1)} %grad_rows.1.g_ref, bf16[2048,256]{1,0:T(8,128)(2,1)S(1)} %get-tuple-element.254.k_ref, ...), custom_call_target="tpu_custom_call" | custom-call | flops 2400000000 | bytes 1000 | tf_op jit(solution)/shard_map/attn_bwd/pallas_call | solution.py:241
  182.4 2.3 collective-permute-start.50
  184.7 8.6 %attn_bwd.5 = (bf16[512,384]{1,0:T(8,128)(2,1)S(1)}, bf16[512,384]{1,0:T(8,128)(2,1)S(1)}, f32[1024,256]{1,0:T(8,128)S(1)}) custom-call(s32[1]{0:T(128)} %constant.101.clone.1.at_ref, bf16[1024,256]{1,0:T(8,128)(2,1)S(1)} %get-tuple-element.238.q_ref, bf16[1024,256]{1,0:T(8,128)(2,1)S(1)} %grad_rows.1.g_ref, bf16[2048,256]{1,0:T(8,128)(2,1)S(1)} %get-tuple-element.254.k_ref, ...), custom_call_target="tpu_custom_call" | custom-call | flops 2400000000 | bytes 1000 | tf_op jit(solution)/shard_map/attn_bwd/pallas_call | solution.py:241
  193.7 2.4 collective-permute-done.50.refs_1_
  198.1 8.6 %attn_bwd.6 = (bf16[512,384]{1,0:T(8,128)(2,1)S(1)}, bf16[512,384]{1,0:T(8,128)(2,1)S(1)}, f32[1024,256]{1,0:T(8,128)S(1)}) custom-call(s32[1]{0:T(128)} %constant.102.clone.1.at_ref, bf16[1024,256]{1,0:T(8,128)(2,1)S(1)} %get-tuple-element.238.q_ref, bf16[1024,256]{1,0:T(8,128)(2,1)S(1)} %grad_rows.1.g_ref, bf16[2048,256]{1,0:T(8,128)(2,1)S(1)} %get-tuple-element.252.k_ref, ...), custom_call_target="tpu_custom_call" | custom-call | flops 2400000000 | bytes 1000 | tf_op jit(solution)/shard_map/attn_bwd/pallas_call | solution.py:241
  207.3 1.7 collective-permute-done.51.refs_1_
  209.4 8.6 %attn_bwd.7 = (bf16[512,384]{1,0:T(8,128)(2,1)S(1)}, bf16[512,384]{1,0:T(8,128)(2,1)S(1)}, f32[1024,256]{1,0:T(8,128)S(1)}) custom-call(s32[1]{0:T(128)} %constant.101.clone.1.at_ref, bf16[1024,256]{1,0:T(8,128)(2,1)S(1)} %get-tuple-element.238.q_ref, bf16[1024,256]{1,0:T(8,128)(2,1)S(1)} %grad_rows.1.g_ref, bf16[2048,256]{1,0:T(8,128)(2,1)S(1)} %get-tuple-element.252.k_ref, ...), custom_call_target="tpu_custom_call" | custom-call | flops 3600000000 | bytes 1000 | tf_op jit(solution)/shard_map/attn_bwd/pallas_call | solution.py:241
  218.1 2.0 join_grads.1
  221.9 2.8 %qkv_grads.1 = (f32[208,576]{1,0:T(8,128)S(1)}, f32[192,576]{1,0:T(8,128)S(1)}, bf16[208,576]{1,0:T(8,128)(2,1)S(1)}, bf16[192,576]{1,0:T(8,128)(2,1)}) custom-call(s32[5]{0:T(128)S(1)} %stack.82.meta.refs_0_, bf16[304,768]{1,0:T(8,128)(2,1)S(1)} %pad_maximum_fusion.1.refs_0_, bf16[304,768]{1,0:T(8,128)(2,1)S(1)} %collective-permute-done.refs_1_, ...), custom_call_target="tpu_custom_call" | custom-call | flops 720000000 | bytes 1000 | tf_op jit(solution)/shard_map/qkv_grads/pallas_call | solution.py:266
  227.4 4.2 %collective-permute-done.55 = bf16[256,768]{1,0:T(8,128)(2,1)} collective-permute-done((bf16[256,768]{1,0:T(8,128)(2,1)}, bf16[256,768]{1,0:T(8,128)(2,1)}, u32[]{:S(2)}, u32[]{:S(2)}) %collective-permute-start.55) | collective-permute-done | bytes 393248 | tf_op jit(solution)/shard_map/ppermute | solution.py:913
  234.3 1.6 collective-permute-start.66
  235.9 2.3 collective-permute-done.61
  238.4 1.6 collective-permute-start.62
  240.0 4.2 %collective-permute-done.59 = bf16[256,768]{1,0:T(8,128)(2,1)S(1)} collective-permute-done((bf16[256,768]{1,0:T(8,128)(2,1)S(1)}, bf16[256,768]{1,0:T(8,128)(2,1)S(1)}, u32[]{:S(2)}, u32[]{:S(2)}) %collective-permute-start.59) | collective-permute-done | bytes 393248 | tf_op jit(solution)/shard_map/ppermute | solution.py:913
  244.4 2.1 collective-permute-done.66.other
  246.5 2.2 finish_grads.1
  252.0 2.4 collective-permute-start.63
  256.1 1.8 collective-permute-start.65
  257.8 1.5 up_grads.1
  259.4 2.0 collective-permute-done.64.refs_2_
  261.4 1.4 spread.1
  (215 shorter events, 43.9 us)
Async XLA Ops:
  2.7 19.9 %collective-permute-start = (bf16[304,768]{1,0:T(8,128)(2,1)S(1)}, bf16[304,768]{1,0:T(8,128)(2,1)S(1)}, u32[]{:S(2)}, u32[]{:S(2)}) collective-permute-start(bf16[304,768]{1,0:T(8,128)(2,1)S(1)} %pad_maximum_fusion.1.refs_0_), channel_id=1, source_target_pairs={{0,1},{1,2},{2,3},{3,0},{4,5},{5,6},{6,7},{7,4},{8,9},{9,10},{10,1... | collective-permute-start | bytes 1400840 | tf_op jit(solution)/shard_map/ppermute | solution.py:913
  7.9 12.9 %collective-permute-start.1 = (bf16[48,576]{1,0:T(8,128)(2,1)S(1)}, bf16[48,576]{1,0:T(8,128)(2,1)S(1)}, u32[]{:S(2)}, u32[]{:S(2)}) collective-permute-start(bf16[48,576]{1,0:T(8,128)(2,1)S(1)} %get-tuple-element.325), channel_id=1, source_target_pairs={{0,1},{1,2},{2,3},{3,0},{4,5},{5,6},{6,7},{7,4},{8,9},{9,10},{10,1... | collective-permute-start | bytes 165896 | tf_op jit(solution)/shard_map/ppermute | solution.py:913
  9.5 13.1 %collective-permute-start.2 = (bf16[48,576]{1,0:T(8,128)(2,1)S(1)}, bf16[48,576]{1,0:T(8,128)(2,1)S(1)}, u32[]{:S(2)}, u32[]{:S(2)}) collective-permute-start(bf16[48,576]{1,0:T(8,128)(2,1)S(1)} %get-tuple-element.324), channel_id=1, source_target_pairs={{0,2},{1,3},{2,0},{3,1},{4,6},{5,7},{6,4},{7,5},{8,10},{9,11},{10,... | collective-permute-start | bytes 165896 | tf_op jit(solution)/shard_map/ppermute | solution.py:913
  10.6 12.0 %collective-permute-start.3 = (bf16[48,576]{1,0:T(8,128)(2,1)S(1)}, bf16[48,576]{1,0:T(8,128)(2,1)S(1)}, u32[]{:S(2)}, u32[]{:S(2)}) collective-permute-start(bf16[48,576]{1,0:T(8,128)(2,1)S(1)} %get-tuple-element.323), channel_id=1, source_target_pairs={{0,3},{1,0},{2,1},{3,2},{4,7},{5,4},{6,5},{7,6},{8,11},{9,8},{10,9... | collective-permute-start | bytes 165896 | tf_op jit(solution)/shard_map/ppermute | solution.py:913
  22.6 14.4 %collective-permute-start.7 = (bf16[304,768]{1,0:T(8,128)(2,1)S(1)}, bf16[304,768]{1,0:T(8,128)(2,1)S(1)}, u32[]{:S(2)}, u32[]{:S(2)}) collective-permute-start(bf16[304,768]{1,0:T(8,128)(2,1)S(1)} %collective-permute-done.refs_1_), channel_id=1, source_target_pairs={{0,1},{1,2},{2,3},{3,0},{4,5},{5,6},{6,7},{7,4},{8,9},{9,10},{10,1... | collective-permute-start | bytes 1400840 | tf_op jit(solution)/shard_map/ppermute | solution.py:913
  24.5 8.7 %collective-permute-start.5 = (bf16[192,576]{1,0:T(8,128)(2,1)S(1)}, bf16[192,576]{1,0:T(8,128)(2,1)S(1)}, u32[]{:S(2)}, u32[]{:S(2)}) collective-permute-start(bf16[192,576]{1,0:T(8,128)(2,1)S(1)} %constant_dynamic-update-slice_fusion.refs_2_.refs_4_), channel_id=1, source_target_pairs={{0,8},{8,0},{4,12},{12,4},{1,9},{9,1},{5,13},{13,5},{2,10},{10,2},... | collective-permute-start | bytes 663560 | tf_op jit(solution)/shard_map/ppermute | solution.py:908
  26.1 13.4 %collective-permute-start.10 = (bf16[192,192]{1,0:T(8,128)(2,1)S(1)}, bf16[192,192]{1,0:T(8,128)(2,1)S(1)}, u32[]{:S(2)}, u32[]{:S(2)}) collective-permute-start(bf16[192,192]{1,0:T(8,128)(2,1)S(1)} %get-tuple-element.317), channel_id=1, source_target_pairs={{0,4},{4,0},{8,12},{12,8},{1,5},{5,1},{9,13},{13,9},{2,6},{6,2},{1... | collective-permute-start | bytes 221192 | tf_op jit(solution)/shard_map/ppermute | solution.py:904
  26.2 13.3 %collective-permute-start.11 = (bf16[192,192]{1,0:T(8,128)(2,1)S(1)}, bf16[192,192]{1,0:T(8,128)(2,1)S(1)}, u32[]{:S(2)}, u32[]{:S(2)}) collective-permute-start(bf16[192,192]{1,0:T(8,128)(2,1)S(1)} %get-tuple-element.316), channel_id=1, source_target_pairs={{0,8},{8,0},{4,12},{12,4},{1,9},{9,1},{5,13},{13,5},{2,10},{10,2},... | collective-permute-start | bytes 221192 | tf_op jit(solution)/shard_map/ppermute | solution.py:908
  27.7 5.5 %collective-permute-start.4 = (bf16[192,576]{1,0:T(8,128)(2,1)S(1)}, bf16[192,576]{1,0:T(8,128)(2,1)S(1)}, u32[]{:S(2)}, u32[]{:S(2)}) collective-permute-start(bf16[192,576]{1,0:T(8,128)(2,1)S(1)} %constant_dynamic-update-slice_fusion.refs_2_.refs_4_), channel_id=1, source_target_pairs={{0,4},{4,0},{8,12},{12,8},{1,5},{5,1},{9,13},{13,9},{2,6},{6,2},{1... | collective-permute-start | bytes 663560 | tf_op jit(solution)/shard_map/ppermute | solution.py:904
  33.2 3.9 %collective-permute-start.6 = (bf16[192,576]{1,0:T(8,128)(2,1)S(1)}, bf16[192,576]{1,0:T(8,128)(2,1)S(1)}, u32[]{:S(2)}, u32[]{:S(2)}) collective-permute-start(bf16[192,576]{1,0:T(8,128)(2,1)S(1)} %collective-permute-done.5.refs_4_.refs_6_), channel_id=1, source_target_pairs={{0,4},{4,0},{8,12},{12,8},{1,5},{5,1},{9,13},{13,9},{2,6},{6,2},{1... | collective-permute-start | bytes 663560 | tf_op jit(solution)/shard_map/ppermute | solution.py:904
  33.2 6.3 %collective-permute-start.12 = (bf16[192,192]{1,0:T(8,128)(2,1)S(1)}, bf16[192,192]{1,0:T(8,128)(2,1)S(1)}, u32[]{:S(2)}, u32[]{:S(2)}) collective-permute-start(bf16[192,192]{1,0:T(8,128)(2,1)S(1)} %get-tuple-element.315), channel_id=1, source_target_pairs={{0,12},{4,8},{8,4},{12,0},{1,13},{5,9},{9,5},{13,1},{2,14},{6,10},... | collective-permute-start | bytes 221192 | tf_op jit(solution)/shard_map/ppermute | solution.py:995
  37.0 13.5 %collective-permute-start.8 = (bf16[304,768]{1,0:T(8,128)(2,1)S(1)}, bf16[304,768]{1,0:T(8,128)(2,1)S(1)}, u32[]{:S(2)}, u32[]{:S(2)}) collective-permute-start(bf16[304,768]{1,0:T(8,128)(2,1)S(1)} %collective-permute-done.7.refs_2_), channel_id=1, source_target_pairs={{0,1},{1,2},{2,3},{3,0},{4,5},{5,6},{6,7},{7,4},{8,9},{9,10},{10,1... | collective-permute-start | bytes 1400840 | tf_op jit(solution)/shard_map/ppermute | solution.py:913
  38.6 3.3 %collective-permute-start.9 = (bf16[512,384]{1,0:T(8,128)(2,1)S(1)}, bf16[512,384]{1,0:T(8,128)(2,1)S(1)}, u32[]{:S(2)}, u32[]{:S(2)}) collective-permute-start(bf16[512,384]{1,0:T(8,128)(2,1)S(1)} %get-tuple-element.170.refs_3_), channel_id=1, source_target_pairs={{0,4},{4,0},{8,12},{12,8},{1,5},{5,1},{9,13},{13,9},{2,6},{6,2},{1... | collective-permute-start | bytes 1179656 | tf_op jit(solution)/shard_map/ppermute | solution.py:904
  40.3 13.8 %collective-permute-start.14 = (bf16[512,384]{1,0:T(8,128)(2,1)S(1)}, bf16[512,384]{1,0:T(8,128)(2,1)S(1)}, u32[]{:S(2)}, u32[]{:S(2)}) collective-permute-start(bf16[512,384]{1,0:T(8,128)(2,1)S(1)} %get-tuple-element.170.refs_3_), channel_id=1, source_target_pairs={{0,8},{8,0},{4,12},{12,4},{1,9},{9,1},{5,13},{13,5},{2,10},{10,2},... | collective-permute-start | bytes 1179656 | tf_op jit(solution)/shard_map/ppermute | solution.py:908
  52.1 13.4 %collective-permute-start.16 = (bf16[512,384]{1,0:T(8,128)(2,1)S(1)}, bf16[512,384]{1,0:T(8,128)(2,1)S(1)}, u32[]{:S(2)}, u32[]{:S(2)}) collective-permute-start(bf16[512,384]{1,0:T(8,128)(2,1)S(1)} %get-tuple-element.174.refs_4_), channel_id=1, source_target_pairs={{0,8},{8,0},{4,12},{12,4},{1,9},{9,1},{5,13},{13,5},{2,10},{10,2},... | collective-permute-start | bytes 1179656 | tf_op jit(solution)/shard_map/ppermute | solution.py:908
  53.6 11.8 %collective-permute-start.15 = (bf16[208,768]{1,0:T(8,128)(2,1)S(1)}, bf16[208,768]{1,0:T(8,128)(2,1)S(1)}, u32[]{:S(2)}, u32[]{:S(2)}) collective-permute-start(bf16[208,768]{1,0:T(8,128)(2,1)S(1)} %get-tuple-element.179), channel_id=1, source_target_pairs={{0,1},{1,2},{2,3},{3,0},{4,5},{5,6},{6,7},{7,4},{8,9},{9,10},{10,1... | collective-permute-start | bytes 958472 | tf_op jit(solution)/shard_map/ppermute | solution.py:913
  65.5 2.8 %collective-permute-start.17 = (bf16[512,384]{1,0:T(8,128)(2,1)S(1)}, bf16[512,384]{1,0:T(8,128)(2,1)S(1)}, u32[]{:S(2)}, u32[]{:S(2)}) collective-permute-start(bf16[512,384]{1,0:T(8,128)(2,1)S(1)} %collective-permute-done.14.refs_3_), channel_id=1, source_target_pairs={{0,4},{4,0},{8,12},{12,8},{1,5},{5,1},{9,13},{13,9},{2,6},{6,2},{1... | collective-permute-start | bytes 1179656 | tf_op jit(solution)/shard_map/ppermute | solution.py:904
  65.5 2.8 %collective-permute-start.18 = (bf16[512,384]{1,0:T(8,128)(2,1)S(1)}, bf16[512,384]{1,0:T(8,128)(2,1)S(1)}, u32[]{:S(2)}, u32[]{:S(2)}) collective-permute-start(bf16[512,384]{1,0:T(8,128)(2,1)S(1)} %collective-permute-done.16.refs_4_), channel_id=1, source_target_pairs={{0,4},{4,0},{8,12},{12,8},{1,5},{5,1},{9,13},{13,9},{2,6},{6,2},{1... | collective-permute-start | bytes 1179656 | tf_op jit(solution)/shard_map/ppermute | solution.py:904
  66.0 12.8 %collective-permute-start.21 = (bf16[224,768]{1,0:T(8,128)(2,1)S(1)}, bf16[224,768]{1,0:T(8,128)(2,1)S(1)}, u32[]{:S(2)}, u32[]{:S(2)}) collective-permute-start(bf16[224,768]{1,0:T(8,128)(2,1)S(1)} %get-tuple-element.192.refs_4_), channel_id=1, source_target_pairs={{0,8},{8,0},{4,12},{12,4},{1,9},{9,1},{5,13},{13,5},{2,10},{10,2},... | collective-permute-start | bytes 1032200 | tf_op jit(solution)/shard_map/ppermute | solution.py:908
  66.5 12.2 %collective-permute-start.19 = (bf16[208,768]{1,0:T(8,128)(2,1)S(1)}, bf16[208,768]{1,0:T(8,128)(2,1)S(1)}, u32[]{:S(2)}, u32[]{:S(2)}) collective-permute-start(bf16[208,768]{1,0:T(8,128)(2,1)S(1)} %collective-permute-done.15.refs_3_), channel_id=1, source_target_pairs={{0,1},{1,2},{2,3},{3,0},{4,5},{5,6},{6,7},{7,4},{8,9},{9,10},{10,1... | collective-permute-start | bytes 958472 | tf_op jit(solution)/shard_map/ppermute | solution.py:913
  66.7 12.1 %collective-permute-start.20 = (bf16[208,768]{1,0:T(8,128)(2,1)S(1)}, bf16[208,768]{1,0:T(8,128)(2,1)S(1)}, u32[]{:S(2)}, u32[]{:S(2)}) collective-permute-start(bf16[208,768]{1,0:T(8,128)(2,1)S(1)} %collective-permute-done.15.refs_3_), channel_id=1, source_target_pairs={{0,16},{16,0},{1,17},{17,1},{2,18},{18,2},{3,19},{19,3},{4,20},{20... | collective-permute-start | bytes 958472 | tf_op jit(solution)/shard_map/ppermute | solution.py:1014
  78.8 14.5 %collective-permute-start.25 = (bf16[208,768]{1,0:T(8,128)(2,1)S(1)}, bf16[208,768]{1,0:T(8,128)(2,1)S(1)}, u32[]{:S(2)}, u32[]{:S(2)}) collective-permute-start(bf16[208,768]{1,0:T(8,128)(2,1)S(1)} %collective-permute-done.19.refs_5_), channel_id=1, source_target_pairs={{0,16},{16,0},{1,17},{17,1},{2,18},{18,2},{3,19},{19,3},{4,20},{20... | collective-permute-start | bytes 958472 | tf_op jit(solution)/shard_map/ppermute | solution.py:1014
  79.8 6.5 %collective-permute-start.22 = (bf16[192,256]{1,0:T(8,128)(2,1)S(1)}, bf16[192,256]{1,0:T(8,128)(2,1)S(1)}, u32[]{:S(2)}, u32[]{:S(2)}) collective-permute-start(bf16[192,256]{1,0:T(8,128)(2,1)S(1)} %get-tuple-element.195.refs_1_), channel_id=1, source_target_pairs={{0,3},{1,0},{2,1},{3,2},{4,7},{5,4},{6,5},{7,6},{8,11},{9,8},{10,9... | collective-permute-start | bytes 294920 | tf_op jit(solution)/shard_map/ppermute | solution.py:913
  83.1 10.4 %collective-permute-start.26 = (bf16[224,768]{1,0:T(8,128)(2,1)S(1)}, bf16[224,768]{1,0:T(8,128)(2,1)S(1)}, u32[]{:S(2)}, u32[]{:S(2)}) collective-permute-start(bf16[224,768]{1,0:T(8,128)(2,1)S(1)} %get-tuple-element.192.refs_4_), channel_id=1, source_target_pairs={{0,4},{4,0},{8,12},{12,8},{1,5},{5,1},{9,13},{13,9},{2,6},{6,2},{1... | collective-permute-start | bytes 1032200 | tf_op jit(solution)/shard_map/ppermute | solution.py:904
  83.1 10.4 %collective-permute-start.27 = (bf16[224,768]{1,0:T(8,128)(2,1)S(1)}, bf16[224,768]{1,0:T(8,128)(2,1)S(1)}, u32[]{:S(2)}, u32[]{:S(2)}) collective-permute-start(bf16[224,768]{1,0:T(8,128)(2,1)S(1)} %collective-permute-done.21.refs_6_), channel_id=1, source_target_pairs={{0,4},{4,0},{8,12},{12,8},{1,5},{5,1},{9,13},{13,9},{2,6},{6,2},{1... | collective-permute-start | bytes 1032200 | tf_op jit(solution)/shard_map/ppermute | solution.py:904
  83.6 7.9 %collective-permute-start.23 = (bf16[192,256]{1,0:T(8,128)(2,1)S(1)}, bf16[192,256]{1,0:T(8,128)(2,1)S(1)}, u32[]{:S(2)}, u32[]{:S(2)}) collective-permute-start(bf16[192,256]{1,0:T(8,128)(2,1)S(1)} %get-tuple-element.196.refs_2_), channel_id=1, source_target_pairs={{0,2},{1,3},{2,0},{3,1},{4,6},{5,7},{6,4},{7,5},{8,10},{9,11},{10,... | collective-permute-start | bytes 294920 | tf_op jit(solution)/shard_map/ppermute | solution.py:913
  86.3 7.0 %collective-permute-start.24 = (bf16[192,256]{1,0:T(8,128)(2,1)S(1)}, bf16[192,256]{1,0:T(8,128)(2,1)S(1)}, u32[]{:S(2)}, u32[]{:S(2)}) collective-permute-start(bf16[192,256]{1,0:T(8,128)(2,1)S(1)} %get-tuple-element.197.refs_3_), channel_id=1, source_target_pairs={{0,1},{1,2},{2,3},{3,0},{4,5},{5,6},{6,7},{7,4},{8,9},{9,10},{10,1... | collective-permute-start | bytes 294920 | tf_op jit(solution)/shard_map/ppermute | solution.py:913
  93.3 9.5 %collective-permute-start.30 = (bf16[208,768]{1,0:T(8,128)(2,1)S(1)}, bf16[208,768]{1,0:T(8,128)(2,1)S(1)}, u32[]{:S(2)}, u32[]{:S(2)}) collective-permute-start(bf16[208,768]{1,0:T(8,128)(2,1)S(1)} %collective-permute-done.19.refs_5_), channel_id=1, source_target_pairs={{0,1},{1,2},{2,3},{3,0},{4,5},{5,6},{6,7},{7,4},{8,9},{9,10},{10,1... | collective-permute-start | bytes 958472 | tf_op jit(solution)/shard_map/ppermute | solution.py:913
  95.0 9.1 %collective-permute-start.28 = (bf16[256,768]{1,0:T(8,128)(2,1)S(1)}, bf16[256,768]{1,0:T(8,128)(2,1)S(1)}, u32[]{:S(2)}, u32[]{:S(2)}) collective-permute-start(bf16[256,768]{1,0:T(8,128)(2,1)S(1)} %get-tuple-element.205.refs_0_.refs_4_), channel_id=1, source_target_pairs={{0,4},{4,0},{8,12},{12,8},{1,5},{5,1},{9,13},{13,9},{2,6},{6,2},{1... | collective-permute-start | bytes 1179656 | tf_op jit(solution)/shard_map/ppermute | solution.py:904
  95.1 11.5 %collective-permute-start.29 = (bf16[256,768]{1,0:T(8,128)(2,1)S(1)}, bf16[256,768]{1,0:T(8,128)(2,1)S(1)}, u32[]{:S(2)}, u32[]{:S(2)}) collective-permute-start(bf16[256,768]{1,0:T(8,128)(2,1)S(1)} %get-tuple-element.205.refs_0_.refs_4_), channel_id=1, source_target_pairs={{0,8},{8,0},{4,12},{12,4},{1,9},{9,1},{5,13},{13,5},{2,10},{10,2},... | collective-permute-start | bytes 1179656 | tf_op jit(solution)/shard_map/ppermute | solution.py:908
  102.8 7.0 %collective-permute-start.31 = (bf16[208,768]{1,0:T(8,128)(2,1)S(1)}, bf16[208,768]{1,0:T(8,128)(2,1)S(1)}, u32[]{:S(2)}, u32[]{:S(2)}) collective-permute-start(bf16[208,768]{1,0:T(8,128)(2,1)S(1)} %collective-permute-done.30.refs_7_), channel_id=1, source_target_pairs={{0,16},{16,0},{1,17},{17,1},{2,18},{18,2},{3,19},{19,3},{4,20},{20... | collective-permute-start | bytes 958472 | tf_op jit(solution)/shard_map/ppermute | solution.py:1014
  114.1 3.2 %collective-permute-start.34 = (bf16[256,768]{1,0:T(8,128)(2,1)S(1)}, bf16[256,768]{1,0:T(8,128)(2,1)S(1)}, u32[]{:S(2)}, u32[]{:S(2)}) collective-permute-start(bf16[256,768]{1,0:T(8,128)(2,1)S(1)} %get-tuple-element.216), channel_id=1, source_target_pairs={{0,4},{4,0},{8,12},{12,8},{1,5},{5,1},{9,13},{13,9},{2,6},{6,2},{1... | collective-permute-start | bytes 1179656 | tf_op jit(solution)/shard_map/ppermute | solution.py:904
  117.4 11.2 %collective-permute-start.35 = (bf16[256,768]{1,0:T(8,128)(2,1)S(1)}, bf16[256,768]{1,0:T(8,128)(2,1)S(1)}, u32[]{:S(2)}, u32[]{:S(2)}) collective-permute-start(bf16[256,768]{1,0:T(8,128)(2,1)S(1)} %add_convert_fusion.5), channel_id=1, source_target_pairs={{0,8},{8,0},{4,12},{12,4},{1,9},{9,1},{5,13},{13,5},{2,10},{10,2},... | collective-permute-start | bytes 1179656 | tf_op jit(solution)/shard_map/ppermute | solution.py:908
  130.6 11.5 %collective-permute-start.37 = (bf16[256,768]{1,0:T(8,128)(2,1)S(1)}, bf16[256,768]{1,0:T(8,128)(2,1)S(1)}, u32[]{:S(2)}, u32[]{:S(2)}) collective-permute-start(bf16[256,768]{1,0:T(8,128)(2,1)S(1)} %get-tuple-element.219.refs_0_.refs_8_), channel_id=1, source_target_pairs={{0,8},{8,0},{4,12},{12,4},{1,9},{9,1},{5,13},{13,5},{2,10},{10,2},... | collective-permute-start | bytes 1179656 | tf_op jit(solution)/shard_map/ppermute | solution.py:908
  146.2 8.8 %collective-permute-start.39 = (bf16[256,768]{1,0:T(8,128)(2,1)S(1)}, bf16[256,768]{1,0:T(8,128)(2,1)S(1)}, u32[]{:S(2)}, u32[]{:S(2)}) collective-permute-start(bf16[256,768]{1,0:T(8,128)(2,1)S(1)} %get-tuple-element.225), channel_id=1, source_target_pairs={{0,4},{4,0},{8,12},{12,8},{1,5},{5,1},{9,13},{13,9},{2,6},{6,2},{1... | collective-permute-start | bytes 1179656 | tf_op jit(solution)/shard_map/ppermute | solution.py:904
  147.9 11.2 %collective-permute-start.41 = (bf16[256,768]{1,0:T(8,128)(2,1)S(1)}, bf16[256,768]{1,0:T(8,128)(2,1)S(1)}, u32[]{:S(2)}, u32[]{:S(2)}) collective-permute-start(bf16[256,768]{1,0:T(8,128)(2,1)S(1)} %add_convert_fusion.4), channel_id=1, source_target_pairs={{0,8},{8,0},{4,12},{12,4},{1,9},{9,1},{5,13},{13,5},{2,10},{10,2},... | collective-permute-start | bytes 1179656 | tf_op jit(solution)/shard_map/ppermute | solution.py:908
  153.4 28.6 %collective-permute-start.46 = (bf16[768,768]{1,0:T(8,128)(2,1)S(1)}, bf16[768,768]{1,0:T(8,128)(2,1)S(1)}, u32[]{:S(2)}, u32[]{:S(2)}) collective-permute-start(bf16[768,768]{1,0:T(8,128)(2,1)S(1)} %get-tuple-element.257), channel_id=1, source_target_pairs={{0,16},{16,0},{1,17},{17,1},{2,18},{18,2},{3,19},{19,3},{4,20},{20... | collective-permute-start | bytes 3538952 | tf_op jit(solution)/shard_map/ppermute | solution.py:1091
  161.5 7.6 %collective-permute-start.45 = (bf16[416,768]{1,0:T(8,128)(2,1)S(1)}, bf16[416,768]{1,0:T(8,128)(2,1)S(1)}, u32[]{:S(2)}, u32[]{:S(2)}) collective-permute-start(bf16[416,768]{1,0:T(8,128)(2,1)S(1)} %get-tuple-element.249), channel_id=1, source_target_pairs={{0,4},{4,0},{8,12},{12,8},{1,5},{5,1},{9,13},{13,9},{2,6},{6,2},{1... | collective-permute-start | bytes 1916936 | tf_op jit(solution)/shard_map/ppermute | solution.py:904
  161.6 7.5 %collective-permute-start.42 = (bf16[192,256]{1,0:T(8,128)(2,1)S(1)}, bf16[192,256]{1,0:T(8,128)(2,1)S(1)}, u32[]{:S(2)}, u32[]{:S(2)}) collective-permute-start(bf16[192,256]{1,0:T(8,128)(2,1)S(1)} %get-tuple-element.240), channel_id=1, source_target_pairs={{0,1},{1,2},{2,3},{3,0},{4,5},{5,6},{6,7},{7,4},{8,9},{9,10},{10,1... | collective-permute-start | bytes 294920 | tf_op jit(solution)/shard_map/ppermute | solution.py:913
  161.7 10.8 %collective-permute-start.43 = (bf16[192,256]{1,0:T(8,128)(2,1)S(1)}, bf16[192,256]{1,0:T(8,128)(2,1)S(1)}, u32[]{:S(2)}, u32[]{:S(2)}) collective-permute-start(bf16[192,256]{1,0:T(8,128)(2,1)S(1)} %get-tuple-element.241), channel_id=1, source_target_pairs={{0,2},{1,3},{2,0},{3,1},{4,6},{5,7},{6,4},{7,5},{8,10},{9,11},{10,... | collective-permute-start | bytes 294920 | tf_op jit(solution)/shard_map/ppermute | solution.py:913
  163.3 9.1 %collective-permute-start.44 = (bf16[192,256]{1,0:T(8,128)(2,1)S(1)}, bf16[192,256]{1,0:T(8,128)(2,1)S(1)}, u32[]{:S(2)}, u32[]{:S(2)}) collective-permute-start(bf16[192,256]{1,0:T(8,128)(2,1)S(1)} %get-tuple-element.242), channel_id=1, source_target_pairs={{0,3},{1,0},{2,1},{3,2},{4,7},{5,4},{6,5},{7,6},{8,11},{9,8},{10,9... | collective-permute-start | bytes 294920 | tf_op jit(solution)/shard_map/ppermute | solution.py:913
  169.2 12.8 %collective-permute-start.47 = (bf16[224,768]{1,0:T(8,128)(2,1)S(1)}, bf16[224,768]{1,0:T(8,128)(2,1)S(1)}, u32[]{:S(2)}, u32[]{:S(2)}) collective-permute-start(bf16[224,768]{1,0:T(8,128)(2,1)S(1)} %far_message.1), channel_id=1, source_target_pairs={{0,8},{8,0},{4,12},{12,4},{1,9},{9,1},{5,13},{13,5},{2,10},{10,2},... | collective-permute-start | bytes 1032200 | tf_op jit(solution)/shard_map/ppermute | solution.py:908
  181.4 11.9 %collective-permute-start.49 = (bf16[512,384]{1,0:T(8,128)(2,1)S(1)}, bf16[512,384]{1,0:T(8,128)(2,1)S(1)}, u32[]{:S(2)}, u32[]{:S(2)}) collective-permute-start(bf16[512,384]{1,0:T(8,128)(2,1)S(1)} %get-tuple-element.265), channel_id=1, source_target_pairs={{0,4},{4,0},{8,12},{12,8},{1,5},{5,1},{9,13},{13,9},{2,6},{6,2},{1... | collective-permute-start | bytes 1179656 | tf_op jit(solution)/shard_map/ppermute | solution.py:904
  181.5 12.0 %collective-permute-start.48 = (bf16[512,384]{1,0:T(8,128)(2,1)S(1)}, bf16[512,384]{1,0:T(8,128)(2,1)S(1)}, u32[]{:S(2)}, u32[]{:S(2)}) collective-permute-start(bf16[512,384]{1,0:T(8,128)(2,1)S(1)} %get-tuple-element.263), channel_id=1, source_target_pairs={{0,4},{4,0},{8,12},{12,8},{1,5},{5,1},{9,13},{13,9},{2,6},{6,2},{1... | collective-permute-start | bytes 1179656 | tf_op jit(solution)/shard_map/ppermute | solution.py:904
  182.4 13.6 %collective-permute-start.50 = (bf16[272,768]{1,0:T(8,128)(2,1)S(1)}, bf16[272,768]{1,0:T(8,128)(2,1)S(1)}, u32[]{:S(2)}, u32[]{:S(2)}) collective-permute-start(bf16[272,768]{1,0:T(8,128)(2,1)S(1)} %get-tuple-element.267), channel_id=1, source_target_pairs={{0,1},{1,2},{2,3},{3,0},{4,5},{5,6},{6,7},{7,4},{8,9},{9,10},{10,1... | collective-permute-start | bytes 1253384 | tf_op jit(solution)/shard_map/ppermute | solution.py:913
  196.1 12.8 %collective-permute-start.51 = (bf16[272,768]{1,0:T(8,128)(2,1)S(1)}, bf16[272,768]{1,0:T(8,128)(2,1)S(1)}, u32[]{:S(2)}, u32[]{:S(2)}) collective-permute-start(bf16[272,768]{1,0:T(8,128)(2,1)S(1)} %sum_messages.3), channel_id=1, source_target_pairs={{0,1},{1,2},{2,3},{3,0},{4,5},{5,6},{6,7},{7,4},{8,9},{9,10},{10,1... | collective-permute-start | bytes 1253384 | tf_op jit(solution)/shard_map/ppermute | solution.py:913
  196.7 21.3 %collective-permute-start.54 = (bf16[1024,384]{1,0:T(8,128)(2,1)S(1)}, bf16[1024,384]{1,0:T(8,128)(2,1)S(1)}, u32[]{:S(2)}, u32[]{:S(2)}) collective-permute-start(bf16[1024,384]{1,0:T(8,128)(2,1)S(1)} %pad_maximum_fusion), channel_id=1, source_target_pairs={{0,8},{8,0},{4,12},{12,4},{1,9},{9,1},{5,13},{13,5},{2,10},{10,2},... | collective-permute-start | bytes 2359304 | tf_op jit(solution)/shard_map/ppermute | solution.py:908
  206.7 11.3 %collective-permute-start.52 = (bf16[512,384]{1,0:T(8,128)(2,1)S(1)}, bf16[512,384]{1,0:T(8,128)(2,1)S(1)}, u32[]{:S(2)}, u32[]{:S(2)}) collective-permute-start(bf16[512,384]{1,0:T(8,128)(2,1)S(1)} %get-tuple-element.275), channel_id=1, source_target_pairs={{0,4},{4,0},{8,12},{12,8},{1,5},{5,1},{9,13},{13,9},{2,6},{6,2},{1... | collective-permute-start | bytes 1179656 | tf_op jit(solution)/shard_map/ppermute | solution.py:904
  206.8 11.3 %collective-permute-start.53 = (bf16[512,384]{1,0:T(8,128)(2,1)S(1)}, bf16[512,384]{1,0:T(8,128)(2,1)S(1)}, u32[]{:S(2)}, u32[]{:S(2)}) collective-permute-start(bf16[512,384]{1,0:T(8,128)(2,1)S(1)} %get-tuple-element.276), channel_id=1, source_target_pairs={{0,4},{4,0},{8,12},{12,8},{1,5},{5,1},{9,13},{13,9},{2,6},{6,2},{1... | collective-permute-start | bytes 1179656 | tf_op jit(solution)/shard_map/ppermute | solution.py:904
  209.1 12.0 %collective-permute-start.56 = (bf16[272,768]{1,0:T(8,128)(2,1)S(1)}, bf16[272,768]{1,0:T(8,128)(2,1)S(1)}, u32[]{:S(2)}, u32[]{:S(2)}) collective-permute-start(bf16[272,768]{1,0:T(8,128)(2,1)S(1)} %sum_messages.4), channel_id=1, source_target_pairs={{0,1},{1,2},{2,3},{3,0},{4,5},{5,6},{6,7},{7,4},{8,9},{9,10},{10,1... | collective-permute-start | bytes 1253384 | tf_op jit(solution)/shard_map/ppermute | solution.py:913
  220.1 11.5 %collective-permute-start.55 = (bf16[256,768]{1,0:T(8,128)(2,1)}, bf16[256,768]{1,0:T(8,128)(2,1)}, u32[]{:S(2)}, u32[]{:S(2)}) collective-permute-start(bf16[256,768]{1,0:T(8,128)(2,1)} %get-tuple-element.282), channel_id=1, source_target_pairs={{0,1},{1,2},{2,3},{3,0},{4,5},{5,6},{6,7},{7,4},{8,9},{9,10},{10,1... | collective-permute-start | bytes 1179656 | tf_op jit(solution)/shard_map/ppermute | solution.py:913
  224.7 6.9 %collective-permute-start.57 = (bf16[208,576]{1,0:T(8,128)(2,1)S(1)}, bf16[208,576]{1,0:T(8,128)(2,1)S(1)}, u32[]{:S(2)}, u32[]{:S(2)}) collective-permute-start(bf16[208,576]{1,0:T(8,128)(2,1)S(1)} %get-tuple-element.289), channel_id=1, source_target_pairs={{0,4},{4,0},{8,12},{12,8},{1,5},{5,1},{9,13},{13,9},{2,6},{6,2},{1... | collective-permute-start | bytes 718856 | tf_op jit(solution)/shard_map/ppermute | solution.py:904
  224.7 6.9 %collective-permute-start.58 = (bf16[192,576]{1,0:T(8,128)(2,1)}, bf16[192,576]{1,0:T(8,128)(2,1)S(1)}, u32[]{:S(2)}, u32[]{:S(2)}) collective-permute-start(bf16[192,576]{1,0:T(8,128)(2,1)} %get-tuple-element.290), channel_id=1, source_target_pairs={{0,4},{4,0},{8,12},{12,8},{1,5},{5,1},{9,13},{13,9},{2,6},{6,2},{1... | collective-permute-start | bytes 663560 | tf_op jit(solution)/shard_map/ppermute | solution.py:904
  231.8 6.5 %collective-permute-start.61 = (bf16[208,576]{1,0:T(8,128)(2,1)S(1)}, bf16[208,576]{1,0:T(8,128)(2,1)S(1)}, u32[]{:S(2)}, u32[]{:S(2)}) collective-permute-start(bf16[208,576]{1,0:T(8,128)(2,1)S(1)} %pad_maximum_fusion.2), channel_id=1, source_target_pairs={{0,8},{8,0},{4,12},{12,4},{1,9},{9,1},{5,13},{13,5},{2,10},{10,2},... | collective-permute-start | bytes 718856 | tf_op jit(solution)/shard_map/ppermute | solution.py:908
  234.2 10.0 %collective-permute-start.59 = (bf16[256,768]{1,0:T(8,128)(2,1)S(1)}, bf16[256,768]{1,0:T(8,128)(2,1)S(1)}, u32[]{:S(2)}, u32[]{:S(2)}) collective-permute-start(bf16[256,768]{1,0:T(8,128)(2,1)S(1)} %add_convert_fusion.1), channel_id=1, source_target_pairs={{0,1},{1,2},{2,3},{3,0},{4,5},{5,6},{6,7},{7,4},{8,9},{9,10},{10,1... | collective-permute-start | bytes 1179656 | tf_op jit(solution)/shard_map/ppermute | solution.py:913
  234.3 12.2 %collective-permute-start.66 = (bf16[272,768]{1,0:T(8,128)(2,1)S(1)}, bf16[272,768]{1,0:T(8,128)(2,1)S(1)}, u32[]{:S(2)}, u32[]{:S(2)}) collective-permute-start(bf16[272,768]{1,0:T(8,128)(2,1)S(1)} %sum_messages.5.own), channel_id=1, source_target_pairs={{0,16},{16,0},{1,17},{17,1},{2,18},{18,2},{3,19},{19,3},{4,20},{20... | collective-permute-start | bytes 1253384 | tf_op jit(solution)/shard_map/ppermute | solution.py:1143
  238.4 13.4 %collective-permute-start.62 = (bf16[208,576]{1,0:T(8,128)(2,1)S(1)}, bf16[208,576]{1,0:T(8,128)(2,1)S(1)}, u32[]{:S(2)}, u32[]{:S(2)}) collective-permute-start(bf16[208,576]{1,0:T(8,128)(2,1)S(1)} %pad_maximum_fusion.3), channel_id=1, source_target_pairs={{0,16},{16,0},{1,17},{17,1},{2,18},{18,2},{3,19},{19,3},{4,20},{20... | collective-permute-start | bytes 718856 | tf_op jit(solution)/shard_map/ppermute | solution.py:1162
  244.3 18.5 %collective-permute-start.60 = (bf16[256,768]{1,0:T(8,128)(2,1)S(1)}, bf16[256,768]{1,0:T(8,128)(2,1)S(1)}, u32[]{:S(2)}, u32[]{:S(2)}) collective-permute-start(bf16[256,768]{1,0:T(8,128)(2,1)S(1)} %add_convert_fusion), channel_id=1, source_target_pairs={{0,1},{1,2},{2,3},{3,0},{4,5},{5,6},{6,7},{7,4},{8,9},{9,10},{10,1... | collective-permute-start | bytes 1179656 | tf_op jit(solution)/shard_map/ppermute | solution.py:913
  248.7 6.3 %collective-permute-start.67 = (bf16[192,192]{1,0:T(8,128)(2,1)S(1)}, bf16[192,192]{1,0:T(8,128)(2,1)S(1)}, u32[]{:S(2)}, u32[]{:S(2)}) collective-permute-start(bf16[192,192]{1,0:T(8,128)(2,1)S(1)} %get-tuple-element.307), channel_id=1, source_target_pairs={{0,4},{4,0},{8,12},{12,8},{1,5},{5,1},{9,13},{13,9},{2,6},{6,2},{1... | collective-permute-start | bytes 221192 | tf_op jit(solution)/shard_map/ppermute | solution.py:904
  248.7 7.4 %collective-permute-start.68 = (bf16[192,192]{1,0:T(8,128)(2,1)S(1)}, bf16[192,192]{1,0:T(8,128)(2,1)S(1)}, u32[]{:S(2)}, u32[]{:S(2)}) collective-permute-start(bf16[192,192]{1,0:T(8,128)(2,1)S(1)} %get-tuple-element.308), channel_id=1, source_target_pairs={{0,8},{8,0},{4,12},{12,4},{1,9},{9,1},{5,13},{13,5},{2,10},{10,2},... | collective-permute-start | bytes 221192 | tf_op jit(solution)/shard_map/ppermute | solution.py:908
  250.1 7.8 %collective-permute-start.69 = (bf16[192,192]{1,0:T(8,128)(2,1)S(1)}, bf16[192,192]{1,0:T(8,128)(2,1)S(1)}, u32[]{:S(2)}, u32[]{:S(2)}) collective-permute-start(bf16[192,192]{1,0:T(8,128)(2,1)S(1)} %get-tuple-element.309), channel_id=1, source_target_pairs={{0,12},{4,8},{8,4},{12,0},{1,13},{5,9},{9,5},{13,1},{2,14},{6,10},... | collective-permute-start | bytes 221192 | tf_op jit(solution)/shard_map/ppermute | solution.py:1179
  252.0 7.4 %collective-permute-start.63 = (bf16[48,576]{1,0:T(8,128)(2,1)S(1)}, bf16[48,576]{1,0:T(8,128)(2,1)S(1)}, u32[]{:S(2)}, u32[]{:S(2)}) collective-permute-start(bf16[48,576]{1,0:T(8,128)(2,1)S(1)} %get-tuple-element.321), channel_id=1, source_target_pairs={{0,1},{1,2},{2,3},{3,0},{4,5},{5,6},{6,7},{7,4},{8,9},{9,10},{10,1... | collective-permute-start | bytes 165896 | tf_op jit(solution)/shard_map/ppermute | solution.py:913
  254.9 6.4 %collective-permute-start.64 = (bf16[48,576]{1,0:T(8,128)(2,1)S(1)}, bf16[48,576]{1,0:T(8,128)(2,1)S(1)}, u32[]{:S(2)}, u32[]{:S(2)}) collective-permute-start(bf16[48,576]{1,0:T(8,128)(2,1)S(1)} %get-tuple-element.320), channel_id=1, source_target_pairs={{0,2},{1,3},{2,0},{3,1},{4,6},{5,7},{6,4},{7,5},{8,10},{9,11},{10,... | collective-permute-start | bytes 165896 | tf_op jit(solution)/shard_map/ppermute | solution.py:913
  256.1 5.3 %collective-permute-start.65 = (bf16[48,576]{1,0:T(8,128)(2,1)S(1)}, bf16[48,576]{1,0:T(8,128)(2,1)S(1)}, u32[]{:S(2)}, u32[]{:S(2)}) collective-permute-start(bf16[48,576]{1,0:T(8,128)(2,1)S(1)} %get-tuple-element.319), channel_id=1, source_target_pairs={{0,3},{1,0},{2,1},{3,2},{4,7},{5,4},{6,5},{7,6},{8,11},{9,8},{10,9... | collective-permute-start | bytes 165896 | tf_op jit(solution)/shard_map/ppermute | solution.py:913
  (31 other events, 229.4 us)

commit v3 on v2

--- a/solution.py
+++ b/solution.py
@@ -448,7 +448,7 @@
     slope = cdf + x * (math.sqrt(0.5 / math.pi) * jnp.exp(-0.5 * x * x))
     slope_ref[...] = slope.astype(BF)
     out = nn(act, jnp.concatenate(weight_rows(meta, packs, units, True), axis=0))
-    keep_ref[...] = out[:rows]
+    keep_ref[...] = out[:rows].astype(BF)
     send_ref[...] = out[rows:].astype(BF)
 
 
@@ -458,7 +458,7 @@
         functools.partial(ffn_fwd_kernel, n=len(packs), units=units),
         [meta, h0, h1, *packs],
         [
-            jax.ShapeDtypeStruct((rows, width), F32),
+            jax.ShapeDtypeStruct((rows, width), BF),
             jax.ShapeDtypeStruct((rows, width), BF),
             jax.ShapeDtypeStruct((2 * rows, wide), BF),
             jax.ShapeDtypeStruct((2 * rows, wide), BF),
@@ -478,7 +478,7 @@
     pre = (nt(g, down) * slope_ref[...].astype(F32)).astype(BF)
     pre_ref[...] = pre
     out = nn(pre, jnp.concatenate(weight_rows(meta, packs, units, False), axis=0))
-    keep_ref[...] = out[:rows]
+    keep_ref[...] = out[:rows].astype(BF)
     send_ref[...] = out[rows:].astype(BF)
 
 
@@ -488,7 +488,7 @@
         functools.partial(ffn_bwd_kernel, n=len(packs), units=units),
         [meta, g0, g1, *packs, slope],
         [
-            jax.ShapeDtypeStruct((rows, width), F32),
+            jax.ShapeDtypeStruct((rows, width), BF),
             jax.ShapeDtypeStruct((rows, width), BF),
             jax.ShapeDtypeStruct(slope.shape, BF),
         ],
@@ -539,7 +539,7 @@
 def norm2_kernel(
     meta, hid_ref, keep_ref, near_ref, far_ref, cot_ref, vec_ref, out_ref, grad_ref, low_ref, sum_ref
 ):
-    branch = keep_ref[...] + near_ref[...].astype(F32) + far_ref[...].astype(F32) + vec_ref[3:4, :]
+    branch = keep_ref[...].astype(F32) + near_ref[...].astype(F32) + far_ref[...].astype(F32) + vec_ref[3:4, :]
     gain = vec_ref[4:5, :]
     normed, normal, inv = norm_forward(hid_ref[...] + branch, gain, vec_ref[5:6, :])
     row = lax.broadcasted_iota(jnp.int32, (out_ref.shape[0], 1), 0)
@@ -570,7 +570,7 @@
 def norm1_back_kernel(
     keep_ref, near_ref, far_ref, add_ref, normal_ref, inv_ref, vec_ref, w_ref, out_ref, low_ref, sum_ref, *mixed
 ):
-    grad = keep_ref[...] + near_ref[...].astype(F32) + far_ref[...].astype(F32) + add_ref[...]
+    grad = keep_ref[...].astype(F32) + near_ref[...].astype(F32) + far_ref[...].astype(F32) + add_ref[...]
     normal = normal_ref[...]
     resid = norm_backward(grad, normal, inv_ref[:, 0:1], vec_ref[1:2, :])
     out_ref[...] = resid
@@ -1065,7 +1065,7 @@
     h_diag = core_swap(h_far)
     keep0, send0, act0, slope0 = ffn_fwd(meta, h_own, h_near, packs, units, units * cols_n)
     keep1, send1, act1, slope1 = ffn_fwd(meta, h_far, h_diag, packs, units, units * cols_n)
-    far = (keep1 + core_swap(send1).astype(F32)).astype(BF)
+    far = (keep1.astype(F32) + core_swap(send1).astype(F32)).astype(BF)
     got_far = cross_swap(far)
     got_near = core_swap(send0)
     output, grad_resid2, grad_branch, sums2 = norm2(
@@ -1077,7 +1077,7 @@
     g_far = after(g_far, send0)
     g_diag = core_swap(g_far)
     keep1, send1, pre1 = ffn_bwd(meta, g_far, g_diag, packs, slope1, units)
-    far = (keep1 + core_swap(send1).astype(F32)).astype(BF)
+    far = (keep1.astype(F32) + core_swap(send1).astype(F32)).astype(BF)
     got_far = cross_swap(far)
     got_near = core_swap(send0)
     g_one, g_two, g_up_bias = ffn_grads(

time: 269 us -> 269 us (level)
  no operation moved by 1% of the time
where the time goes in v3:
time: 269 us; the launch traced here: 264 us
  waiting for transfers between devices  98.6 us (37%)
  Pallas kernels  89 us (33%)
  starting transfers between devices  60.7 us (23%)
  other arithmetic  6.84 us (3%)
  local copies, waits for them, and re-layouts  6.41 us (2%)
    ppermute x24, waiting for transfers between devices, shift_col(): return lax.ppermute(x, 'col', [(i, (i + step) % n) for i in range(n)])  56.5 us
    pallas_call x4, Pallas kernels, attn_bwd(): pl.pallas_call(functools.partial(attn_bwd_kernel, heads=heads, block=bloc...  34.4 us
    ppermute x13, waiting for transfers between devices, cross_swap(): return lax.ppermute(x, 'row', CROSS)  31.8 us
    pallas_call x15, Pallas kernels, meta_call(): pl.pallas_call(kernel, in_specs=[pl.BlockSpec(memory_space=pltpu.SMEM)] +...  29.9 us
    ppermute x24, starting transfers between devices, shift_col(): return lax.ppermute(x, 'col', [(i, (i + step) % n) for i in range(n)])  28.3 us
    pallas_call x2, Pallas kernels, attn_fwd(): pl.pallas_call(functools.partial(attn_fwd_kernel, heads=heads, first=firs...  20.4 us
    ppermute x13, starting transfers between devices, cross_swap(): return lax.ppermute(x, 'row', CROSS)  17 us
  transfers between devices with their start and end apart: 70, of which 29 were waited for; matrix products, arithmetic and copies ran while one was open for 3% of the time, Pallas kernels for 31%

profile of v3, /device:TPU:0, one launch (start us, length us, event | category | flops | bytes accessed | tf_op | source)
XLA Modules:
  0.0 264.1 jit_solution(18090916472521020819)
XLA Ops:
  2.7 3.1 %collective-permute-start = (bf16[304,768]{1,0:T(8,128)(2,1)S(1)}, bf16[304,768]{1,0:T(8,128)(2,1)S(1)}, u32[]{:S(2)}, u32[]{:S(2)}) collective-permute-start(bf16[304,768]{1,0:T(8,128)(2,1)S(1)} %pad_maximum_fusion.1.refs_0_), channel_id=1, source_target_pairs={{0,1},{1,2},{2,3},{3,0},{4,5},{5,6},{6,7},{7,4},{8,9},{9,10},{10,1... | collective-permute-start | bytes 1400840 | tf_op jit(solution)/shard_map/ppermute | solution.py:913
  7.9 1.6 collective-permute-start.1
  10.6 2.8 %collective-permute-start.3 = (bf16[48,576]{1,0:T(8,128)(2,1)S(1)}, bf16[48,576]{1,0:T(8,128)(2,1)S(1)}, u32[]{:S(2)}, u32[]{:S(2)}) collective-permute-start(bf16[48,576]{1,0:T(8,128)(2,1)S(1)} %get-tuple-element.323), channel_id=1, source_target_pairs={{0,3},{1,0},{2,1},{3,2},{4,7},{5,4},{6,5},{7,6},{8,11},{9,8},{10,9... | collective-permute-start | bytes 165896 | tf_op jit(solution)/shard_map/ppermute | solution.py:913
  13.8 7.0 %collective-permute-done.1 = bf16[48,576]{1,0:T(8,128)(2,1)S(1)} collective-permute-done((bf16[48,576]{1,0:T(8,128)(2,1)S(1)}, bf16[48,576]{1,0:T(8,128)(2,1)S(1)}, u32[]{:S(2)}, u32[]{:S(2)}) %collective-permute-start.1) | collective-permute-done | bytes 55328 | tf_op jit(solution)/shard_map/ppermute | solution.py:913
  20.8 1.8 collective-permute-done.2
  22.6 1.8 collective-permute-start.7
  24.5 1.6 collective-permute-start.5
  27.9 5.4 %collective-permute-done.5.refs_4_.refs_6_ = bf16[192,576]{1,0:T(8,128)(2,1)S(1)} collective-permute-done((bf16[192,576]{1,0:T(8,128)(2,1)S(1)}, bf16[192,576]{1,0:T(8,128)(2,1)S(1)}, u32[]{:S(2)}, u32[]{:S(2)}) %collective-permute-start.5) | collective-permute-done | bytes 221216 | tf_op jit(solution)/shard_map/ppermute | solution.py:908
  33.2 1.7 collective-permute-start.12
  34.9 2.1 collective-permute-done.7.refs_2_
  37.1 1.5 project_qkv.2
  40.3 1.6 collective-permute-start.14
  41.9 8.6 %collective-permute-done.8.refs_3_ = bf16[304,768]{1,0:T(8,128)(2,1)S(1)} collective-permute-done((bf16[304,768]{1,0:T(8,128)(2,1)S(1)}, bf16[304,768]{1,0:T(8,128)(2,1)S(1)}, u32[]{:S(2)}, u32[]{:S(2)}) %collective-permute-start.8) | collective-permute-done | bytes 466976 | tf_op jit(solution)/shard_map/ppermute | solution.py:913
  50.5 1.5 project_qkv.3
  52.1 1.6 collective-permute-start.16
  54.1 10.0 %attn_fwd_near.1 = (f32[192,1024]{1,0:T(8,128)S(1)}, f32[16,1024]{1,0:T(8,128)S(1)}, bf16[2048,256]{1,0:T(8,128)(2,1)S(1)}, bf16[2048,256]{1,0:T(8,128)(2,1)S(1)}) custom-call(s32[5]{0:T(128)S(1)} %stack.82.meta.refs_0_, bf16[512,256]{1,0:T(8,128)(2,1)S(1)} %get-tuple-element.168.refs_1_, bf16[512,256]{1,0:T(8,128)(2,1)S(1)} %get-tuple-element.173.refs_2_, ...), custom_call_target="tpu_custom_call" | custom-call | flops 2400000000 | bytes 1000 | tf_op jit(solution)/shard_map/attn_fwd_near/pallas_call | solution.py:156
  66.7 1.6 collective-permute-start.20
  68.3 10.5 %attn_fwd_far.1 = (bf16[192,256]{1,0:T(8,128)(2,1)S(1)}, bf16[192,256]{1,0:T(8,128)(2,1)S(1)}, bf16[192,256]{1,0:T(8,128)(2,1)S(1)}, bf16[192,256]{1,0:T(8,128)(...) custom-call(s32[5]{0:T(128)S(1)} %stack.82.meta.refs_0_, ...), custom_call_target="tpu_custom_call" | custom-call | flops 2400000000 | bytes 1000 | tf_op jit(solution)/shard_map/attn_fwd_far/pallas_call | solution.py:156
  79.8 3.3 %collective-permute-start.22 = (bf16[192,256]{1,0:T(8,128)(2,1)S(1)}, bf16[192,256]{1,0:T(8,128)(2,1)S(1)}, u32[]{:S(2)}, u32[]{:S(2)}) collective-permute-start(bf16[192,256]{1,0:T(8,128)(2,1)S(1)} %get-tuple-element.195.refs_1_), channel_id=1, source_target_pairs={{0,3},{1,0},{2,1},{3,2},{4,7},{5,4},{6,5},{7,6},{8,11},{9,8},{10,9... | collective-permute-start | bytes 294920 | tf_op jit(solution)/shard_map/ppermute | solution.py:913
  83.6 2.7 %collective-permute-done.22.refs_1_ = bf16[192,256]{1,0:T(8,128)(2,1)S(1)} collective-permute-done((bf16[192,256]{1,0:T(8,128)(2,1)S(1)}, bf16[192,256]{1,0:T(8,128)(2,1)S(1)}, u32[]{:S(2)}, u32[]{:S(2)}) %collective-permute-start.22) | collective-permute-done | bytes 98336 | tf_op jit(solution)/shard_map/ppermute | solution.py:913
  86.3 5.1 %collective-permute-done.23.refs_2_ = bf16[192,256]{1,0:T(8,128)(2,1)S(1)} collective-permute-done((bf16[192,256]{1,0:T(8,128)(2,1)S(1)}, bf16[192,256]{1,0:T(8,128)(2,1)S(1)}, u32[]{:S(2)}, u32[]{:S(2)}) %collective-permute-start.23) | collective-permute-done | bytes 98336 | tf_op jit(solution)/shard_map/ppermute | solution.py:913
  91.5 1.8 collective-permute-done.24.refs_3_
  93.5 1.5 project_norm1.1
  95.1 1.6 collective-permute-start.29
  96.6 6.1 %collective-permute-done.30.refs_7_ = bf16[208,768]{1,0:T(8,128)(2,1)S(1)} collective-permute-done((bf16[208,768]{1,0:T(8,128)(2,1)S(1)}, bf16[208,768]{1,0:T(8,128)(2,1)S(1)}, u32[]{:S(2)}, u32[]{:S(2)}) %collective-permute-start.30) | collective-permute-done | bytes 319520 | tf_op jit(solution)/shard_map/ppermute | solution.py:913
  104.2 2.5 collective-permute-done.29.refs_0_.refs_6_
  106.6 3.1 %collective-permute-done.31.refs_8_ = bf16[208,768]{1,0:T(8,128)(2,1)S(1)} collective-permute-done((bf16[208,768]{1,0:T(8,128)(2,1)S(1)}, bf16[208,768]{1,0:T(8,128)(2,1)S(1)}, u32[]{:S(2)}, u32[]{:S(2)}) %collective-permute-start.31) | collective-permute-done | bytes 319520 | tf_op jit(solution)/shard_map/ppermute | solution.py:1014
  109.8 1.7 collective-permute-done.33.refs_1_.refs_7_
  111.5 2.6 ffn_fwd.3
  114.3 2.6 ffn_fwd.2
  118.8 9.8 %collective-permute-done.35.far_ref = bf16[256,768]{1,0:T(8,128)(2,1)S(1)} collective-permute-done((bf16[256,768]{1,0:T(8,128)(2,1)S(1)}, bf16[256,768]{1,0:T(8,128)(2,1)S(1)}, u32[]{:S(2)}, u32[]{:S(2)}) %collective-permute-start.35) | collective-permute-done | bytes 393248 | tf_op jit(solution)/shard_map/ppermute | solution.py:908
  128.6 2.0 norm2_both.1
  132.3 2.2 ffn_bwd.2
  134.5 7.6 %collective-permute-done.37.refs_0_.refs_10_ = bf16[256,768]{1,0:T(8,128)(2,1)S(1)} collective-permute-done((bf16[256,768]{1,0:T(8,128)(2,1)S(1)}, bf16[256,768]{1,0:T(8,128)(2,1)S(1)}, u32[]{:S(2)}, u32[]{:S(2)}) %collective-permute-start.37) | collective-permute-done | bytes 393248 | tf_op jit(solution)/shard_map/ppermute | solution.py:908
  142.2 1.7 collective-permute-done.38.refs_1_.refs_11_
  143.9 2.1 ffn_bwd.3
  149.3 4.1 %ffn_grads.1 = (bf16[768,768]{1,0:T(8,128)(2,1)S(1)}, bf16[768,768]{1,0:T(8,128)(2,1)S(1)}, f32[8,768]{1,0:T(8,128)S(1)}) custom-call(s32[5]{0:T(128)S(1)} %stack.82.meta.refs_0_, bf16[512,768]{1,0:T(8,128)(2,1)S(1)} %get-tuple-element.222.refs_0_, bf16[512,768]{1,0:T(8,128)(2,1)S(1)} %get-tuple-element.223.refs_1_, ...), custom_call_target="tpu_custom_call" | custom-call | flops 720000000 | bytes 1000 | tf_op jit(solution)/shard_map/ffn_grads/pallas_call | solution.py:266
  153.4 1.6 collective-permute-start.46
  155.0 4.1 %collective-permute-done.41.far_ref = bf16[256,768]{1,0:T(8,128)(2,1)S(1)} collective-permute-done((bf16[256,768]{1,0:T(8,128)(2,1)S(1)}, bf16[256,768]{1,0:T(8,128)(2,1)S(1)}, u32[]{:S(2)}, u32[]{:S(2)}) %collective-permute-start.41) | collective-permute-done | bytes 393248 | tf_op jit(solution)/shard_map/ppermute | solution.py:908
  161.7 1.7 collective-permute-start.43
  163.4 2.8 %collective-permute-start.44 = (bf16[192,256]{1,0:T(8,128)(2,1)S(1)}, bf16[192,256]{1,0:T(8,128)(2,1)S(1)}, u32[]{:S(2)}, u32[]{:S(2)}) collective-permute-start(bf16[192,256]{1,0:T(8,128)(2,1)S(1)} %get-tuple-element.242), channel_id=1, source_target_pairs={{0,3},{1,0},{2,1},{3,2},{4,7},{5,4},{6,5},{7,6},{8,11},{9,8},{10,9... | collective-permute-start | bytes 294920 | tf_op jit(solution)/shard_map/ppermute | solution.py:913
  166.2 3.0 %collective-permute-done.42.refs_5_ = bf16[192,256]{1,0:T(8,128)(2,1)S(1)} collective-permute-done((bf16[192,256]{1,0:T(8,128)(2,1)S(1)}, bf16[192,256]{1,0:T(8,128)(2,1)S(1)}, u32[]{:S(2)}, u32[]{:S(2)}) %collective-permute-start.42) | collective-permute-done | bytes 98336 | tf_op jit(solution)/shard_map/ppermute | solution.py:913
  170.7 1.8 collective-permute-done.43.refs_6_
  172.8 8.6 %attn_bwd.4 = (bf16[512,384]{1,0:T(8,128)(2,1)S(1)}, bf16[512,384]{1,0:T(8,128)(2,1)S(1)}, f32[1024,256]{1,0:T(8,128)S(1)}) custom-call(s32[1]{0:T(128)} %constant.102.clone.1.at_ref, bf16[1024,256]{1,0:T(8,128)(2,1)S(1)} %get-tuple-element.238.q_ref, bf16[1024,256]{1,0:T(8,128)(2,1)S(1)} %grad_rows.1.g_ref, bf16[2048,256]{1,0:T(8,128)(2,1)S(1)} %get-tuple-element.254.k_ref, ...), custom_call_target="tpu_custom_call" | custom-call | flops 2400000000 | bytes 1000 | tf_op jit(solution)/shard_map/attn_bwd/pallas_call | solution.py:241
  182.4 2.3 collective-permute-start.50
  184.8 8.6 %attn_bwd.5 = (bf16[512,384]{1,0:T(8,128)(2,1)S(1)}, bf16[512,384]{1,0:T(8,128)(2,1)S(1)}, f32[1024,256]{1,0:T(8,128)S(1)}) custom-call(s32[1]{0:T(128)} %constant.101.clone.1.at_ref, bf16[1024,256]{1,0:T(8,128)(2,1)S(1)} %get-tuple-element.238.q_ref, bf16[1024,256]{1,0:T(8,128)(2,1)S(1)} %grad_rows.1.g_ref, bf16[2048,256]{1,0:T(8,128)(2,1)S(1)} %get-tuple-element.254.k_ref, ...), custom_call_target="tpu_custom_call" | custom-call | flops 2400000000 | bytes 1000 | tf_op jit(solution)/shard_map/attn_bwd/pallas_call | solution.py:241
  193.7 2.4 collective-permute-done.50.refs_1_
  198.1 8.6 %attn_bwd.6 = (bf16[512,384]{1,0:T(8,128)(2,1)S(1)}, bf16[512,384]{1,0:T(8,128)(2,1)S(1)}, f32[1024,256]{1,0:T(8,128)S(1)}) custom-call(s32[1]{0:T(128)} %constant.102.clone.1.at_ref, bf16[1024,256]{1,0:T(8,128)(2,1)S(1)} %get-tuple-element.238.q_ref, bf16[1024,256]{1,0:T(8,128)(2,1)S(1)} %grad_rows.1.g_ref, bf16[2048,256]{1,0:T(8,128)(2,1)S(1)} %get-tuple-element.252.k_ref, ...), custom_call_target="tpu_custom_call" | custom-call | flops 2400000000 | bytes 1000 | tf_op jit(solution)/shard_map/attn_bwd/pallas_call | solution.py:241
  207.3 1.7 collective-permute-done.51.refs_1_
  209.5 8.6 %attn_bwd.7 = (bf16[512,384]{1,0:T(8,128)(2,1)S(1)}, bf16[512,384]{1,0:T(8,128)(2,1)S(1)}, f32[1024,256]{1,0:T(8,128)S(1)}) custom-call(s32[1]{0:T(128)} %constant.101.clone.1.at_ref, bf16[1024,256]{1,0:T(8,128)(2,1)S(1)} %get-tuple-element.238.q_ref, bf16[1024,256]{1,0:T(8,128)(2,1)S(1)} %grad_rows.1.g_ref, bf16[2048,256]{1,0:T(8,128)(2,1)S(1)} %get-tuple-element.252.k_ref, ...), custom_call_target="tpu_custom_call" | custom-call | flops 3600000000 | bytes 1000 | tf_op jit(solution)/shard_map/attn_bwd/pallas_call | solution.py:241
  218.1 2.0 join_grads.1
  221.9 2.8 %qkv_grads.1 = (f32[208,576]{1,0:T(8,128)S(1)}, f32[192,576]{1,0:T(8,128)S(1)}, bf16[208,576]{1,0:T(8,128)(2,1)S(1)}, bf16[192,576]{1,0:T(8,128)(2,1)}) custom-call(s32[5]{0:T(128)S(1)} %stack.82.meta.refs_0_, bf16[304,768]{1,0:T(8,128)(2,1)S(1)} %pad_maximum_fusion.1.refs_0_, bf16[304,768]{1,0:T(8,128)(2,1)S(1)} %collective-permute-done.refs_1_, ...), custom_call_target="tpu_custom_call" | custom-call | flops 720000000 | bytes 1000 | tf_op jit(solution)/shard_map/qkv_grads/pallas_call | solution.py:266
  227.4 4.2 %collective-permute-done.55 = bf16[256,768]{1,0:T(8,128)(2,1)} collective-permute-done((bf16[256,768]{1,0:T(8,128)(2,1)}, bf16[256,768]{1,0:T(8,128)(2,1)}, u32[]{:S(2)}, u32[]{:S(2)}) %collective-permute-start.55) | collective-permute-done | bytes 393248 | tf_op jit(solution)/shard_map/ppermute | solution.py:913
  234.4 1.6 collective-permute-start.66
  235.9 2.3 collective-permute-done.61
  238.5 1.6 collective-permute-start.62
  240.0 4.2 %collective-permute-done.59 = bf16[256,768]{1,0:T(8,128)(2,1)S(1)} collective-permute-done((bf16[256,768]{1,0:T(8,128)(2,1)S(1)}, bf16[256,768]{1,0:T(8,128)(2,1)S(1)}, u32[]{:S(2)}, u32[]{:S(2)}) %collective-permute-start.59) | collective-permute-done | bytes 393248 | tf_op jit(solution)/shard_map/ppermute | solution.py:913
  244.4 2.1 collective-permute-done.66.other
  246.5 2.2 finish_grads.1
  252.1 2.4 collective-permute-start.63
  256.1 1.8 collective-permute-start.65
  257.9 1.5 up_grads.1
  259.4 2.0 collective-permute-done.64.refs_2_
  261.4 1.4 spread.1
  (215 shorter events, 43.8 us)
Async XLA Ops:
  2.7 19.9 %collective-permute-start = (bf16[304,768]{1,0:T(8,128)(2,1)S(1)}, bf16[304,768]{1,0:T(8,128)(2,1)S(1)}, u32[]{:S(2)}, u32[]{:S(2)}) collective-permute-start(bf16[304,768]{1,0:T(8,128)(2,1)S(1)} %pad_maximum_fusion.1.refs_0_), channel_id=1, source_target_pairs={{0,1},{1,2},{2,3},{3,0},{4,5},{5,6},{6,7},{7,4},{8,9},{9,10},{10,1... | collective-permute-start | bytes 1400840 | tf_op jit(solution)/shard_map/ppermute | solution.py:913
  7.9 12.9 %collective-permute-start.1 = (bf16[48,576]{1,0:T(8,128)(2,1)S(1)}, bf16[48,576]{1,0:T(8,128)(2,1)S(1)}, u32[]{:S(2)}, u32[]{:S(2)}) collective-permute-start(bf16[48,576]{1,0:T(8,128)(2,1)S(1)} %get-tuple-element.325), channel_id=1, source_target_pairs={{0,1},{1,2},{2,3},{3,0},{4,5},{5,6},{6,7},{7,4},{8,9},{9,10},{10,1... | collective-permute-start | bytes 165896 | tf_op jit(solution)/shard_map/ppermute | solution.py:913
  9.5 13.1 %collective-permute-start.2 = (bf16[48,576]{1,0:T(8,128)(2,1)S(1)}, bf16[48,576]{1,0:T(8,128)(2,1)S(1)}, u32[]{:S(2)}, u32[]{:S(2)}) collective-permute-start(bf16[48,576]{1,0:T(8,128)(2,1)S(1)} %get-tuple-element.324), channel_id=1, source_target_pairs={{0,2},{1,3},{2,0},{3,1},{4,6},{5,7},{6,4},{7,5},{8,10},{9,11},{10,... | collective-permute-start | bytes 165896 | tf_op jit(solution)/shard_map/ppermute | solution.py:913
  10.6 12.0 %collective-permute-start.3 = (bf16[48,576]{1,0:T(8,128)(2,1)S(1)}, bf16[48,576]{1,0:T(8,128)(2,1)S(1)}, u32[]{:S(2)}, u32[]{:S(2)}) collective-permute-start(bf16[48,576]{1,0:T(8,128)(2,1)S(1)} %get-tuple-element.323), channel_id=1, source_target_pairs={{0,3},{1,0},{2,1},{3,2},{4,7},{5,4},{6,5},{7,6},{8,11},{9,8},{10,9... | collective-permute-start | bytes 165896 | tf_op jit(solution)/shard_map/ppermute | solution.py:913
  22.6 14.4 %collective-permute-start.7 = (bf16[304,768]{1,0:T(8,128)(2,1)S(1)}, bf16[304,768]{1,0:T(8,128)(2,1)S(1)}, u32[]{:S(2)}, u32[]{:S(2)}) collective-permute-start(bf16[304,768]{1,0:T(8,128)(2,1)S(1)} %collective-permute-done.refs_1_), channel_id=1, source_target_pairs={{0,1},{1,2},{2,3},{3,0},{4,5},{5,6},{6,7},{7,4},{8,9},{9,10},{10,1... | collective-permute-start | bytes 1400840 | tf_op jit(solution)/shard_map/ppermute | solution.py:913
  24.5 8.7 %collective-permute-start.5 = (bf16[192,576]{1,0:T(8,128)(2,1)S(1)}, bf16[192,576]{1,0:T(8,128)(2,1)S(1)}, u32[]{:S(2)}, u32[]{:S(2)}) collective-permute-start(bf16[192,576]{1,0:T(8,128)(2,1)S(1)} %constant_dynamic-update-slice_fusion.refs_2_.refs_4_), channel_id=1, source_target_pairs={{0,8},{8,0},{4,12},{12,4},{1,9},{9,1},{5,13},{13,5},{2,10},{10,2},... | collective-permute-start | bytes 663560 | tf_op jit(solution)/shard_map/ppermute | solution.py:908
  26.1 13.4 %collective-permute-start.10 = (bf16[192,192]{1,0:T(8,128)(2,1)S(1)}, bf16[192,192]{1,0:T(8,128)(2,1)S(1)}, u32[]{:S(2)}, u32[]{:S(2)}) collective-permute-start(bf16[192,192]{1,0:T(8,128)(2,1)S(1)} %get-tuple-element.317), channel_id=1, source_target_pairs={{0,4},{4,0},{8,12},{12,8},{1,5},{5,1},{9,13},{13,9},{2,6},{6,2},{1... | collective-permute-start | bytes 221192 | tf_op jit(solution)/shard_map/ppermute | solution.py:904
  26.2 13.3 %collective-permute-start.11 = (bf16[192,192]{1,0:T(8,128)(2,1)S(1)}, bf16[192,192]{1,0:T(8,128)(2,1)S(1)}, u32[]{:S(2)}, u32[]{:S(2)}) collective-permute-start(bf16[192,192]{1,0:T(8,128)(2,1)S(1)} %get-tuple-element.316), channel_id=1, source_target_pairs={{0,8},{8,0},{4,12},{12,4},{1,9},{9,1},{5,13},{13,5},{2,10},{10,2},... | collective-permute-start | bytes 221192 | tf_op jit(solution)/shard_map/ppermute | solution.py:908
  27.7 5.5 %collective-permute-start.4 = (bf16[192,576]{1,0:T(8,128)(2,1)S(1)}, bf16[192,576]{1,0:T(8,128)(2,1)S(1)}, u32[]{:S(2)}, u32[]{:S(2)}) collective-permute-start(bf16[192,576]{1,0:T(8,128)(2,1)S(1)} %constant_dynamic-update-slice_fusion.refs_2_.refs_4_), channel_id=1, source_target_pairs={{0,4},{4,0},{8,12},{12,8},{1,5},{5,1},{9,13},{13,9},{2,6},{6,2},{1... | collective-permute-start | bytes 663560 | tf_op jit(solution)/shard_map/ppermute | solution.py:904
  33.2 3.9 %collective-permute-start.6 = (bf16[192,576]{1,0:T(8,128)(2,1)S(1)}, bf16[192,576]{1,0:T(8,128)(2,1)S(1)}, u32[]{:S(2)}, u32[]{:S(2)}) collective-permute-start(bf16[192,576]{1,0:T(8,128)(2,1)S(1)} %collective-permute-done.5.refs_4_.refs_6_), channel_id=1, source_target_pairs={{0,4},{4,0},{8,12},{12,8},{1,5},{5,1},{9,13},{13,9},{2,6},{6,2},{1... | collective-permute-start | bytes 663560 | tf_op jit(solution)/shard_map/ppermute | solution.py:904
  33.2 6.3 %collective-permute-start.12 = (bf16[192,192]{1,0:T(8,128)(2,1)S(1)}, bf16[192,192]{1,0:T(8,128)(2,1)S(1)}, u32[]{:S(2)}, u32[]{:S(2)}) collective-permute-start(bf16[192,192]{1,0:T(8,128)(2,1)S(1)} %get-tuple-element.315), channel_id=1, source_target_pairs={{0,12},{4,8},{8,4},{12,0},{1,13},{5,9},{9,5},{13,1},{2,14},{6,10},... | collective-permute-start | bytes 221192 | tf_op jit(solution)/shard_map/ppermute | solution.py:995
  37.0 13.5 %collective-permute-start.8 = (bf16[304,768]{1,0:T(8,128)(2,1)S(1)}, bf16[304,768]{1,0:T(8,128)(2,1)S(1)}, u32[]{:S(2)}, u32[]{:S(2)}) collective-permute-start(bf16[304,768]{1,0:T(8,128)(2,1)S(1)} %collective-permute-done.7.refs_2_), channel_id=1, source_target_pairs={{0,1},{1,2},{2,3},{3,0},{4,5},{5,6},{6,7},{7,4},{8,9},{9,10},{10,1... | collective-permute-start | bytes 1400840 | tf_op jit(solution)/shard_map/ppermute | solution.py:913
  38.6 3.3 %collective-permute-start.9 = (bf16[512,384]{1,0:T(8,128)(2,1)S(1)}, bf16[512,384]{1,0:T(8,128)(2,1)S(1)}, u32[]{:S(2)}, u32[]{:S(2)}) collective-permute-start(bf16[512,384]{1,0:T(8,128)(2,1)S(1)} %get-tuple-element.170.refs_3_), channel_id=1, source_target_pairs={{0,4},{4,0},{8,12},{12,8},{1,5},{5,1},{9,13},{13,9},{2,6},{6,2},{1... | collective-permute-start | bytes 1179656 | tf_op jit(solution)/shard_map/ppermute | solution.py:904
  40.3 13.8 %collective-permute-start.14 = (bf16[512,384]{1,0:T(8,128)(2,1)S(1)}, bf16[512,384]{1,0:T(8,128)(2,1)S(1)}, u32[]{:S(2)}, u32[]{:S(2)}) collective-permute-start(bf16[512,384]{1,0:T(8,128)(2,1)S(1)} %get-tuple-element.170.refs_3_), channel_id=1, source_target_pairs={{0,8},{8,0},{4,12},{12,4},{1,9},{9,1},{5,13},{13,5},{2,10},{10,2},... | collective-permute-start | bytes 1179656 | tf_op jit(solution)/shard_map/ppermute | solution.py:908
  52.1 13.4 %collective-permute-start.16 = (bf16[512,384]{1,0:T(8,128)(2,1)S(1)}, bf16[512,384]{1,0:T(8,128)(2,1)S(1)}, u32[]{:S(2)}, u32[]{:S(2)}) collective-permute-start(bf16[512,384]{1,0:T(8,128)(2,1)S(1)} %get-tuple-element.174.refs_4_), channel_id=1, source_target_pairs={{0,8},{8,0},{4,12},{12,4},{1,9},{9,1},{5,13},{13,5},{2,10},{10,2},... | collective-permute-start | bytes 1179656 | tf_op jit(solution)/shard_map/ppermute | solution.py:908
  53.6 11.8 %collective-permute-start.15 = (bf16[208,768]{1,0:T(8,128)(2,1)S(1)}, bf16[208,768]{1,0:T(8,128)(2,1)S(1)}, u32[]{:S(2)}, u32[]{:S(2)}) collective-permute-start(bf16[208,768]{1,0:T(8,128)(2,1)S(1)} %get-tuple-element.179), channel_id=1, source_target_pairs={{0,1},{1,2},{2,3},{3,0},{4,5},{5,6},{6,7},{7,4},{8,9},{9,10},{10,1... | collective-permute-start | bytes 958472 | tf_op jit(solution)/shard_map/ppermute | solution.py:913
  65.5 2.8 %collective-permute-start.17 = (bf16[512,384]{1,0:T(8,128)(2,1)S(1)}, bf16[512,384]{1,0:T(8,128)(2,1)S(1)}, u32[]{:S(2)}, u32[]{:S(2)}) collective-permute-start(bf16[512,384]{1,0:T(8,128)(2,1)S(1)} %collective-permute-done.14.refs_3_), channel_id=1, source_target_pairs={{0,4},{4,0},{8,12},{12,8},{1,5},{5,1},{9,13},{13,9},{2,6},{6,2},{1... | collective-permute-start | bytes 1179656 | tf_op jit(solution)/shard_map/ppermute | solution.py:904
  65.5 2.8 %collective-permute-start.18 = (bf16[512,384]{1,0:T(8,128)(2,1)S(1)}, bf16[512,384]{1,0:T(8,128)(2,1)S(1)}, u32[]{:S(2)}, u32[]{:S(2)}) collective-permute-start(bf16[512,384]{1,0:T(8,128)(2,1)S(1)} %collective-permute-done.16.refs_4_), channel_id=1, source_target_pairs={{0,4},{4,0},{8,12},{12,8},{1,5},{5,1},{9,13},{13,9},{2,6},{6,2},{1... | collective-permute-start | bytes 1179656 | tf_op jit(solution)/shard_map/ppermute | solution.py:904
  66.0 12.8 %collective-permute-start.21 = (bf16[224,768]{1,0:T(8,128)(2,1)S(1)}, bf16[224,768]{1,0:T(8,128)(2,1)S(1)}, u32[]{:S(2)}, u32[]{:S(2)}) collective-permute-start(bf16[224,768]{1,0:T(8,128)(2,1)S(1)} %get-tuple-element.192.refs_4_), channel_id=1, source_target_pairs={{0,8},{8,0},{4,12},{12,4},{1,9},{9,1},{5,13},{13,5},{2,10},{10,2},... | collective-permute-start | bytes 1032200 | tf_op jit(solution)/shard_map/ppermute | solution.py:908
  66.5 12.2 %collective-permute-start.19 = (bf16[208,768]{1,0:T(8,128)(2,1)S(1)}, bf16[208,768]{1,0:T(8,128)(2,1)S(1)}, u32[]{:S(2)}, u32[]{:S(2)}) collective-permute-start(bf16[208,768]{1,0:T(8,128)(2,1)S(1)} %collective-permute-done.15.refs_3_), channel_id=1, source_target_pairs={{0,1},{1,2},{2,3},{3,0},{4,5},{5,6},{6,7},{7,4},{8,9},{9,10},{10,1... | collective-permute-start | bytes 958472 | tf_op jit(solution)/shard_map/ppermute | solution.py:913
  66.7 12.1 %collective-permute-start.20 = (bf16[208,768]{1,0:T(8,128)(2,1)S(1)}, bf16[208,768]{1,0:T(8,128)(2,1)S(1)}, u32[]{:S(2)}, u32[]{:S(2)}) collective-permute-start(bf16[208,768]{1,0:T(8,128)(2,1)S(1)} %collective-permute-done.15.refs_3_), channel_id=1, source_target_pairs={{0,16},{16,0},{1,17},{17,1},{2,18},{18,2},{3,19},{19,3},{4,20},{20... | collective-permute-start | bytes 958472 | tf_op jit(solution)/shard_map/ppermute | solution.py:1014
  78.8 14.5 %collective-permute-start.25 = (bf16[208,768]{1,0:T(8,128)(2,1)S(1)}, bf16[208,768]{1,0:T(8,128)(2,1)S(1)}, u32[]{:S(2)}, u32[]{:S(2)}) collective-permute-start(bf16[208,768]{1,0:T(8,128)(2,1)S(1)} %collective-permute-done.19.refs_5_), channel_id=1, source_target_pairs={{0,16},{16,0},{1,17},{17,1},{2,18},{18,2},{3,19},{19,3},{4,20},{20... | collective-permute-start | bytes 958472 | tf_op jit(solution)/shard_map/ppermute | solution.py:1014
  79.8 6.5 %collective-permute-start.22 = (bf16[192,256]{1,0:T(8,128)(2,1)S(1)}, bf16[192,256]{1,0:T(8,128)(2,1)S(1)}, u32[]{:S(2)}, u32[]{:S(2)}) collective-permute-start(bf16[192,256]{1,0:T(8,128)(2,1)S(1)} %get-tuple-element.195.refs_1_), channel_id=1, source_target_pairs={{0,3},{1,0},{2,1},{3,2},{4,7},{5,4},{6,5},{7,6},{8,11},{9,8},{10,9... | collective-permute-start | bytes 294920 | tf_op jit(solution)/shard_map/ppermute | solution.py:913
  83.1 10.4 %collective-permute-start.26 = (bf16[224,768]{1,0:T(8,128)(2,1)S(1)}, bf16[224,768]{1,0:T(8,128)(2,1)S(1)}, u32[]{:S(2)}, u32[]{:S(2)}) collective-permute-start(bf16[224,768]{1,0:T(8,128)(2,1)S(1)} %get-tuple-element.192.refs_4_), channel_id=1, source_target_pairs={{0,4},{4,0},{8,12},{12,8},{1,5},{5,1},{9,13},{13,9},{2,6},{6,2},{1... | collective-permute-start | bytes 1032200 | tf_op jit(solution)/shard_map/ppermute | solution.py:904
  83.1 10.4 %collective-permute-start.27 = (bf16[224,768]{1,0:T(8,128)(2,1)S(1)}, bf16[224,768]{1,0:T(8,128)(2,1)S(1)}, u32[]{:S(2)}, u32[]{:S(2)}) collective-permute-start(bf16[224,768]{1,0:T(8,128)(2,1)S(1)} %collective-permute-done.21.refs_6_), channel_id=1, source_target_pairs={{0,4},{4,0},{8,12},{12,8},{1,5},{5,1},{9,13},{13,9},{2,6},{6,2},{1... | collective-permute-start | bytes 1032200 | tf_op jit(solution)/shard_map/ppermute | solution.py:904
  83.6 7.9 %collective-permute-start.23 = (bf16[192,256]{1,0:T(8,128)(2,1)S(1)}, bf16[192,256]{1,0:T(8,128)(2,1)S(1)}, u32[]{:S(2)}, u32[]{:S(2)}) collective-permute-start(bf16[192,256]{1,0:T(8,128)(2,1)S(1)} %get-tuple-element.196.refs_2_), channel_id=1, source_target_pairs={{0,2},{1,3},{2,0},{3,1},{4,6},{5,7},{6,4},{7,5},{8,10},{9,11},{10,... | collective-permute-start | bytes 294920 | tf_op jit(solution)/shard_map/ppermute | solution.py:913
  86.3 7.0 %collective-permute-start.24 = (bf16[192,256]{1,0:T(8,128)(2,1)S(1)}, bf16[192,256]{1,0:T(8,128)(2,1)S(1)}, u32[]{:S(2)}, u32[]{:S(2)}) collective-permute-start(bf16[192,256]{1,0:T(8,128)(2,1)S(1)} %get-tuple-element.197.refs_3_), channel_id=1, source_target_pairs={{0,1},{1,2},{2,3},{3,0},{4,5},{5,6},{6,7},{7,4},{8,9},{9,10},{10,1... | collective-permute-start | bytes 294920 | tf_op jit(solution)/shard_map/ppermute | solution.py:913
  93.3 9.5 %collective-permute-start.30 = (bf16[208,768]{1,0:T(8,128)(2,1)S(1)}, bf16[208,768]{1,0:T(8,128)(2,1)S(1)}, u32[]{:S(2)}, u32[]{:S(2)}) collective-permute-start(bf16[208,768]{1,0:T(8,128)(2,1)S(1)} %collective-permute-done.19.refs_5_), channel_id=1, source_target_pairs={{0,1},{1,2},{2,3},{3,0},{4,5},{5,6},{6,7},{7,4},{8,9},{9,10},{10,1... | collective-permute-start | bytes 958472 | tf_op jit(solution)/shard_map/ppermute | solution.py:913
  95.0 9.1 %collective-permute-start.28 = (bf16[256,768]{1,0:T(8,128)(2,1)S(1)}, bf16[256,768]{1,0:T(8,128)(2,1)S(1)}, u32[]{:S(2)}, u32[]{:S(2)}) collective-permute-start(bf16[256,768]{1,0:T(8,128)(2,1)S(1)} %get-tuple-element.205.refs_0_.refs_4_), channel_id=1, source_target_pairs={{0,4},{4,0},{8,12},{12,8},{1,5},{5,1},{9,13},{13,9},{2,6},{6,2},{1... | collective-permute-start | bytes 1179656 | tf_op jit(solution)/shard_map/ppermute | solution.py:904
  95.1 11.5 %collective-permute-start.29 = (bf16[256,768]{1,0:T(8,128)(2,1)S(1)}, bf16[256,768]{1,0:T(8,128)(2,1)S(1)}, u32[]{:S(2)}, u32[]{:S(2)}) collective-permute-start(bf16[256,768]{1,0:T(8,128)(2,1)S(1)} %get-tuple-element.205.refs_0_.refs_4_), channel_id=1, source_target_pairs={{0,8},{8,0},{4,12},{12,4},{1,9},{9,1},{5,13},{13,5},{2,10},{10,2},... | collective-permute-start | bytes 1179656 | tf_op jit(solution)/shard_map/ppermute | solution.py:908
  102.8 7.0 %collective-permute-start.31 = (bf16[208,768]{1,0:T(8,128)(2,1)S(1)}, bf16[208,768]{1,0:T(8,128)(2,1)S(1)}, u32[]{:S(2)}, u32[]{:S(2)}) collective-permute-start(bf16[208,768]{1,0:T(8,128)(2,1)S(1)} %collective-permute-done.30.refs_7_), channel_id=1, source_target_pairs={{0,16},{16,0},{1,17},{17,1},{2,18},{18,2},{3,19},{19,3},{4,20},{20... | collective-permute-start | bytes 958472 | tf_op jit(solution)/shard_map/ppermute | solution.py:1014
  114.1 3.2 %collective-permute-start.34 = (bf16[256,768]{1,0:T(8,128)(2,1)S(1)}, bf16[256,768]{1,0:T(8,128)(2,1)S(1)}, u32[]{:S(2)}, u32[]{:S(2)}) collective-permute-start(bf16[256,768]{1,0:T(8,128)(2,1)S(1)} %get-tuple-element.216), channel_id=1, source_target_pairs={{0,4},{4,0},{8,12},{12,8},{1,5},{5,1},{9,13},{13,9},{2,6},{6,2},{1... | collective-permute-start | bytes 1179656 | tf_op jit(solution)/shard_map/ppermute | solution.py:904
  117.4 11.2 %collective-permute-start.35 = (bf16[256,768]{1,0:T(8,128)(2,1)S(1)}, bf16[256,768]{1,0:T(8,128)(2,1)S(1)}, u32[]{:S(2)}, u32[]{:S(2)}) collective-permute-start(bf16[256,768]{1,0:T(8,128)(2,1)S(1)} %add_convert_fusion.5), channel_id=1, source_target_pairs={{0,8},{8,0},{4,12},{12,4},{1,9},{9,1},{5,13},{13,5},{2,10},{10,2},... | collective-permute-start | bytes 1179656 | tf_op jit(solution)/shard_map/ppermute | solution.py:908
  130.6 11.5 %collective-permute-start.37 = (bf16[256,768]{1,0:T(8,128)(2,1)S(1)}, bf16[256,768]{1,0:T(8,128)(2,1)S(1)}, u32[]{:S(2)}, u32[]{:S(2)}) collective-permute-start(bf16[256,768]{1,0:T(8,128)(2,1)S(1)} %get-tuple-element.219.refs_0_.refs_8_), channel_id=1, source_target_pairs={{0,8},{8,0},{4,12},{12,4},{1,9},{9,1},{5,13},{13,5},{2,10},{10,2},... | collective-permute-start | bytes 1179656 | tf_op jit(solution)/shard_map/ppermute | solution.py:908
  146.2 8.8 %collective-permute-start.39 = (bf16[256,768]{1,0:T(8,128)(2,1)S(1)}, bf16[256,768]{1,0:T(8,128)(2,1)S(1)}, u32[]{:S(2)}, u32[]{:S(2)}) collective-permute-start(bf16[256,768]{1,0:T(8,128)(2,1)S(1)} %get-tuple-element.225), channel_id=1, source_target_pairs={{0,4},{4,0},{8,12},{12,8},{1,5},{5,1},{9,13},{13,9},{2,6},{6,2},{1... | collective-permute-start | bytes 1179656 | tf_op jit(solution)/shard_map/ppermute | solution.py:904
  147.9 11.2 %collective-permute-start.41 = (bf16[256,768]{1,0:T(8,128)(2,1)S(1)}, bf16[256,768]{1,0:T(8,128)(2,1)S(1)}, u32[]{:S(2)}, u32[]{:S(2)}) collective-permute-start(bf16[256,768]{1,0:T(8,128)(2,1)S(1)} %add_convert_fusion.4), channel_id=1, source_target_pairs={{0,8},{8,0},{4,12},{12,4},{1,9},{9,1},{5,13},{13,5},{2,10},{10,2},... | collective-permute-start | bytes 1179656 | tf_op jit(solution)/shard_map/ppermute | solution.py:908
  153.4 28.6 %collective-permute-start.46 = (bf16[768,768]{1,0:T(8,128)(2,1)S(1)}, bf16[768,768]{1,0:T(8,128)(2,1)S(1)}, u32[]{:S(2)}, u32[]{:S(2)}) collective-permute-start(bf16[768,768]{1,0:T(8,128)(2,1)S(1)} %get-tuple-element.257), channel_id=1, source_target_pairs={{0,16},{16,0},{1,17},{17,1},{2,18},{18,2},{3,19},{19,3},{4,20},{20... | collective-permute-start | bytes 3538952 | tf_op jit(solution)/shard_map/ppermute | solution.py:1091
  161.6 7.6 %collective-permute-start.45 = (bf16[416,768]{1,0:T(8,128)(2,1)S(1)}, bf16[416,768]{1,0:T(8,128)(2,1)S(1)}, u32[]{:S(2)}, u32[]{:S(2)}) collective-permute-start(bf16[416,768]{1,0:T(8,128)(2,1)S(1)} %get-tuple-element.249), channel_id=1, source_target_pairs={{0,4},{4,0},{8,12},{12,8},{1,5},{5,1},{9,13},{13,9},{2,6},{6,2},{1... | collective-permute-start | bytes 1916936 | tf_op jit(solution)/shard_map/ppermute | solution.py:904
  161.6 7.5 %collective-permute-start.42 = (bf16[192,256]{1,0:T(8,128)(2,1)S(1)}, bf16[192,256]{1,0:T(8,128)(2,1)S(1)}, u32[]{:S(2)}, u32[]{:S(2)}) collective-permute-start(bf16[192,256]{1,0:T(8,128)(2,1)S(1)} %get-tuple-element.240), channel_id=1, source_target_pairs={{0,1},{1,2},{2,3},{3,0},{4,5},{5,6},{6,7},{7,4},{8,9},{9,10},{10,1... | collective-permute-start | bytes 294920 | tf_op jit(solution)/shard_map/ppermute | solution.py:913
  161.7 10.8 %collective-permute-start.43 = (bf16[192,256]{1,0:T(8,128)(2,1)S(1)}, bf16[192,256]{1,0:T(8,128)(2,1)S(1)}, u32[]{:S(2)}, u32[]{:S(2)}) collective-permute-start(bf16[192,256]{1,0:T(8,128)(2,1)S(1)} %get-tuple-element.241), channel_id=1, source_target_pairs={{0,2},{1,3},{2,0},{3,1},{4,6},{5,7},{6,4},{7,5},{8,10},{9,11},{10,... | collective-permute-start | bytes 294920 | tf_op jit(solution)/shard_map/ppermute | solution.py:913
  163.4 9.1 %collective-permute-start.44 = (bf16[192,256]{1,0:T(8,128)(2,1)S(1)}, bf16[192,256]{1,0:T(8,128)(2,1)S(1)}, u32[]{:S(2)}, u32[]{:S(2)}) collective-permute-start(bf16[192,256]{1,0:T(8,128)(2,1)S(1)} %get-tuple-element.242), channel_id=1, source_target_pairs={{0,3},{1,0},{2,1},{3,2},{4,7},{5,4},{6,5},{7,6},{8,11},{9,8},{10,9... | collective-permute-start | bytes 294920 | tf_op jit(solution)/shard_map/ppermute | solution.py:913
  169.3 12.8 %collective-permute-start.47 = (bf16[224,768]{1,0:T(8,128)(2,1)S(1)}, bf16[224,768]{1,0:T(8,128)(2,1)S(1)}, u32[]{:S(2)}, u32[]{:S(2)}) collective-permute-start(bf16[224,768]{1,0:T(8,128)(2,1)S(1)} %far_message.1), channel_id=1, source_target_pairs={{0,8},{8,0},{4,12},{12,4},{1,9},{9,1},{5,13},{13,5},{2,10},{10,2},... | collective-permute-start | bytes 1032200 | tf_op jit(solution)/shard_map/ppermute | solution.py:908
  181.5 11.9 %collective-permute-start.49 = (bf16[512,384]{1,0:T(8,128)(2,1)S(1)}, bf16[512,384]{1,0:T(8,128)(2,1)S(1)}, u32[]{:S(2)}, u32[]{:S(2)}) collective-permute-start(bf16[512,384]{1,0:T(8,128)(2,1)S(1)} %get-tuple-element.265), channel_id=1, source_target_pairs={{0,4},{4,0},{8,12},{12,8},{1,5},{5,1},{9,13},{13,9},{2,6},{6,2},{1... | collective-permute-start | bytes 1179656 | tf_op jit(solution)/shard_map/ppermute | solution.py:904
  181.5 11.9 %collective-permute-start.48 = (bf16[512,384]{1,0:T(8,128)(2,1)S(1)}, bf16[512,384]{1,0:T(8,128)(2,1)S(1)}, u32[]{:S(2)}, u32[]{:S(2)}) collective-permute-start(bf16[512,384]{1,0:T(8,128)(2,1)S(1)} %get-tuple-element.263), channel_id=1, source_target_pairs={{0,4},{4,0},{8,12},{12,8},{1,5},{5,1},{9,13},{13,9},{2,6},{6,2},{1... | collective-permute-start | bytes 1179656 | tf_op jit(solution)/shard_map/ppermute | solution.py:904
  182.4 13.6 %collective-permute-start.50 = (bf16[272,768]{1,0:T(8,128)(2,1)S(1)}, bf16[272,768]{1,0:T(8,128)(2,1)S(1)}, u32[]{:S(2)}, u32[]{:S(2)}) collective-permute-start(bf16[272,768]{1,0:T(8,128)(2,1)S(1)} %get-tuple-element.267), channel_id=1, source_target_pairs={{0,1},{1,2},{2,3},{3,0},{4,5},{5,6},{6,7},{7,4},{8,9},{9,10},{10,1... | collective-permute-start | bytes 1253384 | tf_op jit(solution)/shard_map/ppermute | solution.py:913
  196.2 12.8 %collective-permute-start.51 = (bf16[272,768]{1,0:T(8,128)(2,1)S(1)}, bf16[272,768]{1,0:T(8,128)(2,1)S(1)}, u32[]{:S(2)}, u32[]{:S(2)}) collective-permute-start(bf16[272,768]{1,0:T(8,128)(2,1)S(1)} %sum_messages.3), channel_id=1, source_target_pairs={{0,1},{1,2},{2,3},{3,0},{4,5},{5,6},{6,7},{7,4},{8,9},{9,10},{10,1... | collective-permute-start | bytes 1253384 | tf_op jit(solution)/shard_map/ppermute | solution.py:913
  196.8 21.4 %collective-permute-start.54 = (bf16[1024,384]{1,0:T(8,128)(2,1)S(1)}, bf16[1024,384]{1,0:T(8,128)(2,1)S(1)}, u32[]{:S(2)}, u32[]{:S(2)}) collective-permute-start(bf16[1024,384]{1,0:T(8,128)(2,1)S(1)} %pad_maximum_fusion), channel_id=1, source_target_pairs={{0,8},{8,0},{4,12},{12,4},{1,9},{9,1},{5,13},{13,5},{2,10},{10,2},... | collective-permute-start | bytes 2359304 | tf_op jit(solution)/shard_map/ppermute | solution.py:908
  206.7 11.4 %collective-permute-start.52 = (bf16[512,384]{1,0:T(8,128)(2,1)S(1)}, bf16[512,384]{1,0:T(8,128)(2,1)S(1)}, u32[]{:S(2)}, u32[]{:S(2)}) collective-permute-start(bf16[512,384]{1,0:T(8,128)(2,1)S(1)} %get-tuple-element.275), channel_id=1, source_target_pairs={{0,4},{4,0},{8,12},{12,8},{1,5},{5,1},{9,13},{13,9},{2,6},{6,2},{1... | collective-permute-start | bytes 1179656 | tf_op jit(solution)/shard_map/ppermute | solution.py:904
  206.8 11.3 %collective-permute-start.53 = (bf16[512,384]{1,0:T(8,128)(2,1)S(1)}, bf16[512,384]{1,0:T(8,128)(2,1)S(1)}, u32[]{:S(2)}, u32[]{:S(2)}) collective-permute-start(bf16[512,384]{1,0:T(8,128)(2,1)S(1)} %get-tuple-element.276), channel_id=1, source_target_pairs={{0,4},{4,0},{8,12},{12,8},{1,5},{5,1},{9,13},{13,9},{2,6},{6,2},{1... | collective-permute-start | bytes 1179656 | tf_op jit(solution)/shard_map/ppermute | solution.py:904
  209.1 12.0 %collective-permute-start.56 = (bf16[272,768]{1,0:T(8,128)(2,1)S(1)}, bf16[272,768]{1,0:T(8,128)(2,1)S(1)}, u32[]{:S(2)}, u32[]{:S(2)}) collective-permute-start(bf16[272,768]{1,0:T(8,128)(2,1)S(1)} %sum_messages.4), channel_id=1, source_target_pairs={{0,1},{1,2},{2,3},{3,0},{4,5},{5,6},{6,7},{7,4},{8,9},{9,10},{10,1... | collective-permute-start | bytes 1253384 | tf_op jit(solution)/shard_map/ppermute | solution.py:913
  220.2 11.5 %collective-permute-start.55 = (bf16[256,768]{1,0:T(8,128)(2,1)}, bf16[256,768]{1,0:T(8,128)(2,1)}, u32[]{:S(2)}, u32[]{:S(2)}) collective-permute-start(bf16[256,768]{1,0:T(8,128)(2,1)} %get-tuple-element.282), channel_id=1, source_target_pairs={{0,1},{1,2},{2,3},{3,0},{4,5},{5,6},{6,7},{7,4},{8,9},{9,10},{10,1... | collective-permute-start | bytes 1179656 | tf_op jit(solution)/shard_map/ppermute | solution.py:913
  224.7 6.9 %collective-permute-start.57 = (bf16[208,576]{1,0:T(8,128)(2,1)S(1)}, bf16[208,576]{1,0:T(8,128)(2,1)S(1)}, u32[]{:S(2)}, u32[]{:S(2)}) collective-permute-start(bf16[208,576]{1,0:T(8,128)(2,1)S(1)} %get-tuple-element.289), channel_id=1, source_target_pairs={{0,4},{4,0},{8,12},{12,8},{1,5},{5,1},{9,13},{13,9},{2,6},{6,2},{1... | collective-permute-start | bytes 718856 | tf_op jit(solution)/shard_map/ppermute | solution.py:904
  224.8 6.9 %collective-permute-start.58 = (bf16[192,576]{1,0:T(8,128)(2,1)}, bf16[192,576]{1,0:T(8,128)(2,1)S(1)}, u32[]{:S(2)}, u32[]{:S(2)}) collective-permute-start(bf16[192,576]{1,0:T(8,128)(2,1)} %get-tuple-element.290), channel_id=1, source_target_pairs={{0,4},{4,0},{8,12},{12,8},{1,5},{5,1},{9,13},{13,9},{2,6},{6,2},{1... | collective-permute-start | bytes 663560 | tf_op jit(solution)/shard_map/ppermute | solution.py:904
  231.8 6.5 %collective-permute-start.61 = (bf16[208,576]{1,0:T(8,128)(2,1)S(1)}, bf16[208,576]{1,0:T(8,128)(2,1)S(1)}, u32[]{:S(2)}, u32[]{:S(2)}) collective-permute-start(bf16[208,576]{1,0:T(8,128)(2,1)S(1)} %pad_maximum_fusion.2), channel_id=1, source_target_pairs={{0,8},{8,0},{4,12},{12,4},{1,9},{9,1},{5,13},{13,5},{2,10},{10,2},... | collective-permute-start | bytes 718856 | tf_op jit(solution)/shard_map/ppermute | solution.py:908
  234.3 10.0 %collective-permute-start.59 = (bf16[256,768]{1,0:T(8,128)(2,1)S(1)}, bf16[256,768]{1,0:T(8,128)(2,1)S(1)}, u32[]{:S(2)}, u32[]{:S(2)}) collective-permute-start(bf16[256,768]{1,0:T(8,128)(2,1)S(1)} %add_convert_fusion.1), channel_id=1, source_target_pairs={{0,1},{1,2},{2,3},{3,0},{4,5},{5,6},{6,7},{7,4},{8,9},{9,10},{10,1... | collective-permute-start | bytes 1179656 | tf_op jit(solution)/shard_map/ppermute | solution.py:913
  234.4 12.2 %collective-permute-start.66 = (bf16[272,768]{1,0:T(8,128)(2,1)S(1)}, bf16[272,768]{1,0:T(8,128)(2,1)S(1)}, u32[]{:S(2)}, u32[]{:S(2)}) collective-permute-start(bf16[272,768]{1,0:T(8,128)(2,1)S(1)} %sum_messages.5.own), channel_id=1, source_target_pairs={{0,16},{16,0},{1,17},{17,1},{2,18},{18,2},{3,19},{19,3},{4,20},{20... | collective-permute-start | bytes 1253384 | tf_op jit(solution)/shard_map/ppermute | solution.py:1143
  238.5 13.4 %collective-permute-start.62 = (bf16[208,576]{1,0:T(8,128)(2,1)S(1)}, bf16[208,576]{1,0:T(8,128)(2,1)S(1)}, u32[]{:S(2)}, u32[]{:S(2)}) collective-permute-start(bf16[208,576]{1,0:T(8,128)(2,1)S(1)} %pad_maximum_fusion.3), channel_id=1, source_target_pairs={{0,16},{16,0},{1,17},{17,1},{2,18},{18,2},{3,19},{19,3},{4,20},{20... | collective-permute-start | bytes 718856 | tf_op jit(solution)/shard_map/ppermute | solution.py:1162
  244.4 18.5 %collective-permute-start.60 = (bf16[256,768]{1,0:T(8,128)(2,1)S(1)}, bf16[256,768]{1,0:T(8,128)(2,1)S(1)}, u32[]{:S(2)}, u32[]{:S(2)}) collective-permute-start(bf16[256,768]{1,0:T(8,128)(2,1)S(1)} %add_convert_fusion), channel_id=1, source_target_pairs={{0,1},{1,2},{2,3},{3,0},{4,5},{5,6},{6,7},{7,4},{8,9},{9,10},{10,1... | collective-permute-start | bytes 1179656 | tf_op jit(solution)/shard_map/ppermute | solution.py:913
  248.7 6.3 %collective-permute-start.67 = (bf16[192,192]{1,0:T(8,128)(2,1)S(1)}, bf16[192,192]{1,0:T(8,128)(2,1)S(1)}, u32[]{:S(2)}, u32[]{:S(2)}) collective-permute-start(bf16[192,192]{1,0:T(8,128)(2,1)S(1)} %get-tuple-element.307), channel_id=1, source_target_pairs={{0,4},{4,0},{8,12},{12,8},{1,5},{5,1},{9,13},{13,9},{2,6},{6,2},{1... | collective-permute-start | bytes 221192 | tf_op jit(solution)/shard_map/ppermute | solution.py:904
  248.7 7.4 %collective-permute-start.68 = (bf16[192,192]{1,0:T(8,128)(2,1)S(1)}, bf16[192,192]{1,0:T(8,128)(2,1)S(1)}, u32[]{:S(2)}, u32[]{:S(2)}) collective-permute-start(bf16[192,192]{1,0:T(8,128)(2,1)S(1)} %get-tuple-element.308), channel_id=1, source_target_pairs={{0,8},{8,0},{4,12},{12,4},{1,9},{9,1},{5,13},{13,5},{2,10},{10,2},... | collective-permute-start | bytes 221192 | tf_op jit(solution)/shard_map/ppermute | solution.py:908
  250.1 7.8 %collective-permute-start.69 = (bf16[192,192]{1,0:T(8,128)(2,1)S(1)}, bf16[192,192]{1,0:T(8,128)(2,1)S(1)}, u32[]{:S(2)}, u32[]{:S(2)}) collective-permute-start(bf16[192,192]{1,0:T(8,128)(2,1)S(1)} %get-tuple-element.309), channel_id=1, source_target_pairs={{0,12},{4,8},{8,4},{12,0},{1,13},{5,9},{9,5},{13,1},{2,14},{6,10},... | collective-permute-start | bytes 221192 | tf_op jit(solution)/shard_map/ppermute | solution.py:1179
  252.1 7.4 %collective-permute-start.63 = (bf16[48,576]{1,0:T(8,128)(2,1)S(1)}, bf16[48,576]{1,0:T(8,128)(2,1)S(1)}, u32[]{:S(2)}, u32[]{:S(2)}) collective-permute-start(bf16[48,576]{1,0:T(8,128)(2,1)S(1)} %get-tuple-element.321), channel_id=1, source_target_pairs={{0,1},{1,2},{2,3},{3,0},{4,5},{5,6},{6,7},{7,4},{8,9},{9,10},{10,1... | collective-permute-start | bytes 165896 | tf_op jit(solution)/shard_map/ppermute | solution.py:913
  255.0 6.4 %collective-permute-start.64 = (bf16[48,576]{1,0:T(8,128)(2,1)S(1)}, bf16[48,576]{1,0:T(8,128)(2,1)S(1)}, u32[]{:S(2)}, u32[]{:S(2)}) collective-permute-start(bf16[48,576]{1,0:T(8,128)(2,1)S(1)} %get-tuple-element.320), channel_id=1, source_target_pairs={{0,2},{1,3},{2,0},{3,1},{4,6},{5,7},{6,4},{7,5},{8,10},{9,11},{10,... | collective-permute-start | bytes 165896 | tf_op jit(solution)/shard_map/ppermute | solution.py:913
  256.1 5.3 %collective-permute-start.65 = (bf16[48,576]{1,0:T(8,128)(2,1)S(1)}, bf16[48,576]{1,0:T(8,128)(2,1)S(1)}, u32[]{:S(2)}, u32[]{:S(2)}) collective-permute-start(bf16[48,576]{1,0:T(8,128)(2,1)S(1)} %get-tuple-element.319), channel_id=1, source_target_pairs={{0,3},{1,0},{2,1},{3,2},{4,7},{5,4},{6,5},{7,6},{8,11},{9,8},{10,9... | collective-permute-start | bytes 165896 | tf_op jit(solution)/shard_map/ppermute | solution.py:913
  (31 other events, 229.3 us)
